TPU v7x, 512 devices: a whole 4x8x8 slice. The times are simulated.
512 devices in a mesh: grp: 8 (over z), ep: 64 (over y, x, core).
Axes of the slice: x: 4, y: 8, z: 8, core: 2. Of those that a mesh axis runs over, the one named last changes fastest.
Arguments:
- tokens: bfloat16 [65536, 512], P(('grp', 'ep')), may hold values from -6 to 6
- teacher: bfloat16 [65536, 7168], P(('grp', 'ep')), may hold values from -6 to 6
- expert_ids: int32 [65536, 4], P(('grp', 'ep')), may hold values from 0 to 63, all different within a row; in each aligned block of 128 rows (0 to 127, 128 to 255, ...) at most 12 rows name the same one
- route_weights: float32 [65536, 4], P(('grp', 'ep')), may hold values from 0.1 to 1
- w_gate: bfloat16 [64, 512, 1024], P('ep', 'grp'), may hold values from -0.25 to 0.25
- w_up: bfloat16 [64, 512, 1024], P('ep', 'grp'), may hold values from -0.25 to 0.25
- w_down: bfloat16 [64, 1024, 512], P('ep', 'grp'), may hold values from -0.1875 to 0.1875
- critic_teacher: bfloat16 [7168, 512], P('ep'), may hold values from -0.0625 to 0.0625
- critic_student: bfloat16 [512, 512], P('ep'), may hold values from -0.25 to 0.25
- critic_head: float32 [512], replicated, may hold values from -0.25 to 0.25
Outputs:
- grad_gate: float32 [64, 512, 1024], P('ep', 'grp')
- grad_up: float32 [64, 512, 1024], P('ep', 'grp')
- grad_down: float32 [64, 1024, 512], P('ep', 'grp')
- scores: float32 [65536], P(('grp', 'ep'))
Inputs may be any that keep to these rules, and one draw needn't show every extreme that they name: `expert_ids`: each row names 4 different experts. Among the 128 rows of one device no expert is named more than 12 times, and in every draw some expert is named exactly 12 times by the rows of some device.
All inputs are finite; a program needn't handle non-finite values.
Results may differ from a plain program's by a relative error of at most 0.013.
Values may be sent and summed in bfloat16 or wider, within the bound.
No kernel may reach another device: no remote copies, remote signals or barrier semaphores. Data moves between devices by JAX's collectives and lax.ppermute only.
A program may use at most 64 MiB of HBM per device.

v0:
```python
import jax
import jax.numpy as jnp
from jax import lax
from jax.sharding import PartitionSpec as P

TOP = 4


def gelu_tanh(value):
    inner = 0.7978845608 * (value + 0.044715 * value * value * value)
    return 0.5 * value * (1.0 + jnp.tanh(inner))


def gelu_slope(value):
    inner = 0.7978845608 * (value + 0.044715 * value * value * value)
    tangent = jnp.tanh(inner)
    return 0.5 * (1.0 + tangent) + 0.5 * value * (1.0 - tangent * tangent) * 0.7978845608 * (
        1.0 + 3.0 * 0.044715 * value * value
    )


def slot_ranks(ids, experts, capacity):
    flat = ids.reshape(-1)
    onehot = (flat[:, None] == jnp.arange(experts, dtype=jnp.int32)[None, :]).astype(jnp.int32)
    before = jnp.cumsum(onehot, axis=0) - onehot
    return flat * capacity + jnp.sum(before * onehot, axis=1)


def contract_rows(left, right):
    return lax.dot_general(
        left, right, (((0,), (0,)), ((), ())), preferred_element_type=jnp.float32
    )


def contract_cols(left, right):
    return lax.dot_general(
        left, right, (((1,), (1,)), ((), ())), preferred_element_type=jnp.float32
    )


def gate_up_parts(routed, dhidden, gate, up, sig):
    dgate = (dhidden * up * sig * (1.0 + gate * (1.0 - sig))).astype(jnp.bfloat16)
    dup = (dhidden * gate * sig).astype(jnp.bfloat16)
    return (contract_rows(routed, dgate), contract_rows(routed, dup))


def body(
    tokens,
    teacher,
    expert_ids,
    route_weights,
    w_gate,
    w_up,
    w_down,
    critic_teacher,
    critic_student,
    critic_head,
):
    experts = lax.axis_size("ep")
    tok_dev, width = tokens.shape
    capacity = 3 * tok_dev * TOP // (2 * experts)
    slots = slot_ranks(expert_ids, experts, capacity)
    spread = jnp.repeat(tokens, TOP, axis=0)
    outbound = jnp.zeros((experts * capacity, width), jnp.bfloat16).at[slots].set(spread)
    routed = lax.all_to_all(
        outbound.reshape(experts, capacity, width), "ep", split_axis=0, concat_axis=0, tiled=True
    ).reshape(experts * capacity, width)
    full_gate, full_up, full_down = (
        lax.all_gather(w_gate, "grp", axis=1, tiled=True),
        lax.all_gather(w_up, "grp", axis=1, tiled=True),
        lax.all_gather(w_down, "grp", axis=1, tiled=True),
    )
    gate = jnp.dot(routed, full_gate[0], preferred_element_type=jnp.float32)
    up = jnp.dot(routed, full_up[0], preferred_element_type=jnp.float32)
    sig = jax.nn.sigmoid(gate)
    hidden = (gate * sig * up).astype(jnp.bfloat16)
    expert_out = jnp.dot(hidden, full_down[0], preferred_element_type=jnp.float32).astype(
        jnp.bfloat16
    )
    returned = lax.all_to_all(
        expert_out.reshape(experts, capacity, width), "ep", split_axis=0, concat_axis=0, tiled=True
    ).reshape(experts * capacity, width)
    picked = returned[slots].reshape(tok_dev, TOP, width)
    student = jnp.sum(picked.astype(jnp.float32) * route_weights[:, :, None], axis=1).astype(
        jnp.bfloat16
    )
    teacher_rows, student_rows = (
        lax.all_gather(critic_teacher, "ep", axis=0, tiled=True),
        lax.all_gather(critic_student, "ep", axis=0, tiled=True),
    )
    pre = jnp.dot(teacher, teacher_rows, preferred_element_type=jnp.float32) + jnp.dot(
        student, student_rows, preferred_element_type=jnp.float32
    )
    score = jnp.sum(gelu_tanh(pre) * critic_head[None, :], axis=1)
    dscore = -jax.nn.sigmoid(-score)
    dpre = (dscore[:, None] * critic_head[None, :] * gelu_slope(pre)).astype(jnp.bfloat16)
    dstudent = contract_cols(dpre, student_rows)
    dassign = (
        (route_weights[:, :, None] * dstudent[:, None, :])
        .astype(jnp.bfloat16)
        .reshape(tok_dev * TOP, width)
    )
    grad_out = jnp.zeros((experts * capacity, width), jnp.bfloat16).at[slots].set(dassign)
    droute = lax.all_to_all(
        grad_out.reshape(experts, capacity, width), "ep", split_axis=0, concat_axis=0, tiled=True
    ).reshape(experts * capacity, width)
    dhidden = contract_cols(droute, full_down[0])
    part_down = contract_rows(hidden, droute)
    part_gate, part_up = gate_up_parts(routed, dhidden, gate, up, sig)
    sum_gate, sum_up, sum_down = (
        lax.psum_scatter(
            part_gate[None].astype(jnp.bfloat16), "grp", scatter_dimension=1, tiled=True
        ).astype(jnp.float32),
        lax.psum_scatter(
            part_up[None].astype(jnp.bfloat16), "grp", scatter_dimension=1, tiled=True
        ).astype(jnp.float32),
        lax.psum_scatter(
            part_down[None].astype(jnp.bfloat16), "grp", scatter_dimension=1, tiled=True
        ).astype(jnp.float32),
    )
    return (sum_gate, sum_up, sum_down, score)


def solution(mesh):
    in_specs = (
        P(("grp", "ep"), None),
        P(("grp", "ep"), None),
        P(("grp", "ep"), None),
        P(("grp", "ep"), None),
        P("ep", "grp", None),
        P("ep", "grp", None),
        P("ep", "grp", None),
        P("ep", None),
        P("ep", None),
        P(),
    )
    out_specs = (P("ep", "grp", None), P("ep", "grp", None), P("ep", "grp", None), P(("grp", "ep")))
    return jax.shard_map(body, mesh=mesh, in_specs=in_specs, out_specs=out_specs, check_vma=False)
```

profile of v0, /device:TPU:2, one launch (start us, length us, event | category | flops | bytes accessed | tf_op | source)
XLA Modules:
  0.0 426.6 jit_solution(13402551651392025176)
XLA Ops:
  14.7 3.3 scatter_custom_fusion
  19.3 39.3 %all_to_all.15 = bf16[64,12,512]{2,1,0:T(8,128)(2,1)} all-to-all(bf16[64,12,512]{2,1,0:T(8,128)(2,1)S(1)} %reshape.96), channel_id=1, replica_groups=mesh['grp'=8,'ep'=64] {'ep'}, dimensions={0} | all-to-all | bytes 1572864 | tf_op jit(solution)/shard_map/all_to_all | solution.py:65
  59.9 3.9 fusion.12
  63.9 34.7 %all-gather.9.cloned.1.call-done = bf16[1,512,1024]{2,1,0:T(8,128)(2,1)} async-done(((bf16[1,64,1024]{2,1,0:T(8,128)(2,1)}), bf16[1,512,1024]{2,1,0:T(8,128)(2,1)}) %all-gather.9.cloned.1.call-update) | async-done | bytes 1048592 | tf_op jit(solution)/shard_map/all_gather | solution.py:70
  98.5 5.5 %multiply_convert_fusion.2 = (bf16[768,1024]{1,0:T(8,128)(2,1)}, f32[768,1024]{1,0:T(8,128)}) fusion(f32[768,1024]{1,0:T(8,128)} %fusion.12, bf16[768,512]{1,0:T(8,128)(2,1)S(1)} %reshape.97, bf16[1,512,1024]{2,1,0:T(8,128)(2,1)} %all-gather.9.cloned.1.call-done), kind=kOutput, calls=%fused_computation.5 | convolution fusion | flops 810024960 | bytes 9699328 | tf_op jit(solution)/shard_map/dot_general | solution.py:74
  104.0 36.6 %all-gather.11.cloned.1.call-done = bf16[1,1024,512]{2,1,0:T(8,128)(2,1)} async-done(((bf16[1,128,512]{2,1,0:T(8,128)(2,1)}), bf16[1,1024,512]{2,1,0:T(8,128)(2,1)}) %all-gather.11.cloned.1.call-update) | async-done | bytes 1048592 | tf_op jit(solution)/shard_map/all_gather | solution.py:71
  140.6 2.7 convolution_convert_fusion.1
  144.5 10.4 %all-to-all-start.1 = ((bf16[64,12,512]{2,1,0:T(8,128)(2,1)}), bf16[64,12,512]{2,1,0:T(8,128)(2,1)}, u32[]{:S(2)}, u32[]{:S(2)}) async-start(bf16[64,12,512]{2,1,0:T(8,128)(2,1)} %reshape.98), calls=%async_computation.1 | async-start | bytes 2097152 | tf_op jit(solution)/shard_map/all_to_all | solution.py:80
  155.2 76.5 %all_gather.19 = bf16[512,512]{1,0:T(8,128)(2,1)} all-gather(bf16[8,512]{1,0:T(8,128)(2,1)S(1)} %copy-done.4), channel_id=1, replica_groups=mesh['grp'=8,'ep'=64] {'ep'}, dimensions={0}, use_global_device_ids=true | all-gather | bytes 532480 | tf_op jit(solution)/shard_map/all_gather | solution.py:89
  233.0 2.6 gather_fusion
  235.6 2.3 reshape.102
  237.9 1.9 multiply_reduce_fusion
  240.0 4.2 fusion.47
  246.2 2.6 mul.168
  248.8 3.4 scatter_custom_fusion.1
  253.3 38.0 %all_to_all.16 = bf16[64,12,512]{2,1,0:T(8,128)(2,1)} all-to-all(bf16[64,12,512]{2,1,0:T(8,128)(2,1)} %reshape.100), channel_id=1, replica_groups=mesh['grp'=8,'ep'=64] {'ep'}, dimensions={0} | all-to-all | bytes 1572864 | tf_op jit(solution)/shard_map/all_to_all | solution.py:104
  292.6 3.4 fusion.4
  296.3 2.4 fusion.7
  298.7 1.6 copy-done.2
  300.3 4.6 %fusion.5 = bf16[1,512,1024]{2,1,0:T(8,128)(2,1)} fusion(bf16[768,512]{1,0:T(8,128)(2,1)S(1)} %reshape.97, f32[768,1024]{1,0:T(8,128)S(1)} %copy-done.1, f32[768,1024]{1,0:T(8,128)S(1)} %fusion.7, f32[768,1024]{1,0:T(8,128)} %get-tuple-element.5), kind=kOutput, calls=%fused_computation.14 | convolution fusion | flops 813694976 | bytes 11272192 | tf_op jit(solution)/shard_map/dot_general | solution.py:30
  305.0 5.0 %fusion.6 = bf16[1,512,1024]{2,1,0:T(8,128)(2,1)} fusion(bf16[768,512]{1,0:T(8,128)(2,1)S(1)} %reshape.97, f32[768,1024]{1,0:T(8,128)} %copy-done.2, f32[768,1024]{1,0:T(8,128)} %fusion.12), kind=kOutput, calls=%fused_computation.15 | convolution fusion | flops 810549248 | bytes 8126464 | tf_op jit(solution)/shard_map/dot_general | solution.py:30
  310.0 21.5 %reduce-scatter.8.cloned.1.call-done = bf16[1,128,512]{2,1,0:T(8,128)(2,1)} async-done(((bf16[1,1024,512]{2,1,0:T(8,128)(2,1)}), bf16[1,128,512]{2,1,0:T(8,128)(2,1)}) %reduce-scatter.8.cloned.1.call-update) | async-done | bytes 131088 | tf_op jit(solution)/shard_map/reduce_scatter | solution.py:117
  333.1 41.6 %reduce-scatter.4.cloned.1.call-done = bf16[1,64,1024]{2,1,0:T(8,128)(2,1)} async-done(((bf16[1,512,1024]{2,1,0:T(8,128)(2,1)}), bf16[1,64,1024]{2,1,0:T(8,128)(2,1)}) %reduce-scatter.4.cloned.1.call-update) | async-done | bytes 131088 | tf_op jit(solution)/shard_map/reduce_scatter | solution.py:111
  376.3 41.8 %reduce-scatter.6.cloned.1.call-done = bf16[1,64,1024]{2,1,0:T(8,128)(2,1)} async-done(((bf16[1,512,1024]{2,1,0:T(8,128)(2,1)}), bf16[1,64,1024]{2,1,0:T(8,128)(2,1)}) %reduce-scatter.6.cloned.1.call-update) | async-done | bytes 131088 | tf_op jit(solution)/shard_map/reduce_scatter | solution.py:114
  (63 shorter events, 22.4 us)
Async XLA Ops:
  7.2 232.8 %copy-start = (bf16[128,7168]{1,0:T(8,128)(2,1)S(1)}, bf16[128,7168]{1,0:T(8,128)(2,1)}, u32[]{:S(2)}) copy-start(bf16[128,7168]{1,0:T(8,128)(2,1)} %param.11) | copy-start | bytes 5505028
  7.2 52.8 %all-gather.7.cloned.1.call-start = ((), (), s32[]{:S(2)}) async-start(), calls=%async_computation.7 | async-start | bytes 1179648 | tf_op jit(solution)/shard_map/all_gather | solution.py:69
  7.9 90.6 %all-gather.9.cloned.1.call-start = ((), (), s32[]{:S(2)}) async-start(), calls=%async_computation.8 | async-start | bytes 1179648 | tf_op jit(solution)/shard_map/all_gather | solution.py:70
  8.7 131.9 %all-gather.11.cloned.1.call-start = ((), (), s32[]{:S(2)}) async-start(), calls=%async_computation.9 | async-start | bytes 1179648 | tf_op jit(solution)/shard_map/all_gather | solution.py:71
  9.4 230.5 %all-gather.5.cloned.1.call-start = ((), (), s32[]{:S(2)}) async-start(), calls=%async_computation.6 | async-start | bytes 7454720 | tf_op jit(solution)/shard_map/all_gather | solution.py:88
  143.3 11.7 %copy-start.5 = (f32[128,4]{0,1:T(4,128)S(1)}, f32[128,4]{0,1:T(4,128)}, u32[]{:S(2)}) copy-start(f32[128,4]{0,1:T(4,128)} %param.13) | copy-start | bytes 6148
  143.3 11.9 %copy-start.4 = (bf16[8,512]{1,0:T(8,128)(2,1)S(1)}, bf16[8,512]{1,0:T(8,128)(2,1)}, u32[]{:S(2)}) copy-start(bf16[8,512]{1,0:T(8,128)(2,1)} %param.18) | copy-start | bytes 24580
  144.5 87.2 %all-to-all-start.1 = ((bf16[64,12,512]{2,1,0:T(8,128)(2,1)}), bf16[64,12,512]{2,1,0:T(8,128)(2,1)}, u32[]{:S(2)}, u32[]{:S(2)}) async-start(bf16[64,12,512]{2,1,0:T(8,128)(2,1)} %reshape.98), calls=%async_computation.1 | async-start | bytes 2097152 | tf_op jit(solution)/shard_map/all_to_all | solution.py:80
  154.9 176.6 %reduce-scatter.8.cloned.1.call-start = ((), (), s32[]{:S(2)}) async-start(), calls=%async_computation.12 | async-start | bytes 1179648 | tf_op jit(solution)/shard_map/reduce_scatter | solution.py:117
  239.9 4.3 %copy-start.3 = (bf16[512,512]{1,0:T(8,128)(2,1)S(1)}, bf16[512,512]{1,0:T(8,128)(2,1)}, u32[]{:S(2)}) copy-start(bf16[512,512]{1,0:T(8,128)(2,1)} %all_gather.19) | copy-start | bytes 1572868
  239.9 4.3 %copy-start.6 = (f32[512]{0:T(512)S(1)}, f32[512]{0:T(512)}, u32[]{:S(2)}) copy-start(f32[512]{0:T(512)} %param.19) | copy-start | bytes 6148
  244.6 7.5 %copy-start.7 = (f32[128]{0:T(128)}, f32[128]{0:T(128)S(1)}, u32[]{:S(2)}) copy-start(f32[128]{0:T(128)S(1)} %get-tuple-element.6) | copy-start | bytes 1540
  296.0 78.7 %reduce-scatter.4.cloned.1.call-start = ((), (), s32[]{:S(2)}) async-start(), calls=%async_computation.10 | async-start | bytes 1179648 | tf_op jit(solution)/shard_map/reduce_scatter | solution.py:111
  296.3 4.1 copy-start.1
  298.7 1.7 copy-start.2
  304.9 113.2 %reduce-scatter.6.cloned.1.call-start = ((), (), s32[]{:S(2)}) async-start(), calls=%async_computation.11 | async-start | bytes 1179648 | tf_op jit(solution)/shard_map/reduce_scatter | solution.py:114
Sparse Core Ops, SparseCore 0:
  10.1 46.6 all-gather.6
  58.8 39.6 all-gather.8
  100.6 39.9 all-gather.10
  143.8 86.6 all-gather.4
  296.1 35.2 reduce-scatter.7
  334.1 40.5 reduce-scatter.3
  377.5 40.5 reduce-scatter.5
where the time goes:
time: 427 us
  waiting for transfers between devices  179 us (42%)
  blocking collectives  154 us (36%)
  matrix products  32.4 us (8%)
  local copies, waits for them, and re-layouts  24 us (6%)
  between operations  14.4 us (3%)
  other arithmetic  12.3 us (3%)
  starting transfers between devices  10.9 us (3%)
    all_gather x1, blocking collectives, body(): lax.all_gather(critic_student, 'ep', axis=0, tiled=True)  76.5 us
    reduce_scatter x1, waiting for transfers between devices, body(): lax.psum_scatter(part_up[None].astype(jnp.bfloat16), 'grp', scatter_dimen...  41.8 us
    reduce_scatter x1, waiting for transfers between devices, body(): lax.psum_scatter(part_gate[None].astype(jnp.bfloat16), 'grp', scatter_dim...  41.6 us
    all_to_all x1, blocking collectives, body(): lax.all_to_all(outbound.reshape(experts, capacity, width), 'ep', split_ax...  39.3 us
    all_to_all x1, blocking collectives, body(): lax.all_to_all(grad_out.reshape(experts, capacity, width), 'ep', split_ax...  38 us
    all_gather x1, waiting for transfers between devices, body(): lax.all_gather(w_down, 'grp', axis=1, tiled=True)  36.6 us
    all_gather x1, waiting for transfers between devices, body(): lax.all_gather(w_up, 'grp', axis=1, tiled=True)  34.7 us
    reduce_scatter x1, waiting for transfers between devices, body(): lax.psum_scatter(part_down[None].astype(jnp.bfloat16), 'grp', scatter_dim...  21.5 us
  transfers between devices with their start and end apart: 8, of which 5 were waited for; matrix products, arithmetic and copies ran while one was open for 11% of the time, Pallas kernels for 0%

commit v1 on v0

v1 whole, which is shorter than its diff:
```python
import jax
import jax.numpy as jnp
from jax import lax
from jax.sharding import Mesh
from jax.sharding import PartitionSpec as P

TOP = 4
EP = ("yx", "c")
BF = jnp.bfloat16
F32 = jnp.float32


def gelu_tanh(value):
    inner = 0.7978845608 * (value + 0.044715 * value * value * value)
    return 0.5 * value * (1.0 + jnp.tanh(inner))


def gelu_slope(value):
    inner = 0.7978845608 * (value + 0.044715 * value * value * value)
    tangent = jnp.tanh(inner)
    return 0.5 * (1.0 + tangent) + 0.5 * value * (1.0 - tangent * tangent) * 0.7978845608 * (
        1.0 + 3.0 * 0.044715 * value * value
    )


def dot(left, right, dims=((1,), (0,))):
    return lax.dot_general(left, right, (dims, ((), ())), preferred_element_type=F32)


def split(value):
    high = value.astype(BF)
    return high, (value - high.astype(F32)).astype(BF)


def shift(value, axis, step):
    count = lax.axis_size(axis)
    return lax.ppermute(value, axis, [(i, (i + step) % count) for i in range(count)])


def swap(value):
    return shift(value, "c", 1)


def both(core, own, other):
    first = core == 0
    return jnp.stack([jnp.where(first, own, other), jnp.where(first, other, own)])


def ring_gather(block):
    count = lax.axis_size("grp")
    here = lax.axis_index("grp")
    full = jnp.zeros((count,) + block.shape, block.dtype)

    def put(full, piece, at):
        return lax.dynamic_update_slice(full, piece[None], (at % count, 0, 0))

    full = put(full, block, here)
    up = down = block
    for step in range(1, count // 2 + 1):
        up = shift(up, "grp", 1)
        full = put(full, up, here - step + count)
        if 2 * step < count:
            down = shift(down, "grp", -1)
            full = put(full, down, here + step)
    return full


def body(
    tokens,
    teacher,
    expert_ids,
    route_weights,
    w_gate,
    w_up,
    w_down,
    critic_teacher,
    critic_student,
    critic_head,
):
    core = lax.axis_index("c")
    chips = lax.axis_size("yx")
    experts = 2 * chips
    tok_dev, width = tokens.shape
    capacity = 3 * tok_dev * TOP // (2 * experts)
    slots = experts * capacity
    hidden_all = w_gate.shape[2]
    half = hidden_all // 2
    rows_in = w_gate.shape[1]

    teacher_rows = lax.all_gather(critic_teacher, EP, axis=0, tiled=True)
    pack = jnp.concatenate(
        [w_gate[0, :, :half], w_gate[0, :, half:], w_up[0, :, :half], w_up[0, :, half:], w_down[0]]
    )
    full = ring_gather(pack)

    meta = jnp.concatenate([expert_ids.T.astype(F32), route_weights.T])
    tok2 = both(core, tokens, swap(tokens)).reshape(2 * tok_dev, width)
    meta2 = both(core, meta, swap(meta))
    ids = meta2[:, :TOP].astype(jnp.int32)
    weights = meta2[:, TOP:]
    member = ids[:, :, None, :] == jnp.arange(experts, dtype=jnp.int32)[None, None, :, None]
    count = jnp.sum(member.astype(F32), axis=1).astype(BF)
    order = jnp.arange(tok_dev)
    earlier = (order[:, None] < order[None, :]).astype(BF)
    before = lax.dot_general(count, earlier, (((2,), (0,)), ((), ())), preferred_element_type=F32)
    rank = jnp.sum(jnp.where(member, before[:, None], 0.0), axis=2).astype(jnp.int32)
    source = jnp.arange(2, dtype=jnp.int32)[:, None, None]
    place = (ids // 2) * (2 * capacity) + source * capacity + rank
    place = jnp.where(ids % 2 == core, place, -1)
    place = place.transpose(1, 0, 2).reshape(TOP, 2 * tok_dev)
    weights = weights.transpose(1, 0, 2).reshape(TOP, 2 * tok_dev)
    hits = place[:, None, :] == jnp.arange(slots, dtype=jnp.int32)[None, :, None]
    pick = jnp.sum(hits.astype(F32), axis=0).astype(BF)
    scaled = jnp.sum(jnp.where(hits, weights[:, None, :], 0.0), axis=0)
    row_weight = jnp.sum(scaled, axis=1)
    scaled_high, scaled_low = split(scaled)

    outbound = dot(pick, tok2).astype(BF).reshape(chips, 2 * capacity, width)
    rows_st = critic_student.shape[0]
    outbound = jnp.concatenate(
        [outbound, jnp.broadcast_to(critic_student[None], (chips, rows_st, width))], axis=1
    )
    inbound = lax.all_to_all(outbound, "yx", split_axis=0, concat_axis=0, tiled=True)
    routed = inbound[:, : 2 * capacity].reshape(slots, width)
    student_half = inbound[:, 2 * capacity :]
    student_rows = (
        both(core, student_half, swap(student_half)).transpose(1, 0, 2, 3).reshape(width, -1)
    )

    gate_w = jnp.concatenate(
        [full[:, :rows_in].reshape(width, half), full[:, rows_in : 2 * rows_in].reshape(width, half)],
        axis=1,
    )
    up_w = jnp.concatenate(
        [
            full[:, 2 * rows_in : 3 * rows_in].reshape(width, half),
            full[:, 3 * rows_in : 4 * rows_in].reshape(width, half),
        ],
        axis=1,
    )
    down_w = full[:, 4 * rows_in :].reshape(hidden_all, width)
    gate = dot(routed, gate_w)
    up = dot(routed, up_w)
    sig = jax.nn.sigmoid(gate)
    hidden = (gate * sig * up).astype(BF)
    expert_out = dot(hidden, down_w).astype(BF)
    returned = lax.all_to_all(
        expert_out.reshape(chips, 2 * capacity, width), "yx", split_axis=0, concat_axis=0, tiled=True
    ).reshape(slots, width)

    partial = dot(scaled_high, returned, ((0,), (0,))) + dot(scaled_low, returned, ((0,), (0,)))
    partial = partial.reshape(2, tok_dev, width)
    mine = lax.dynamic_index_in_dim(partial, core, 0, keepdims=False)
    theirs = lax.dynamic_index_in_dim(partial, 1 - core, 0, keepdims=False)
    student = (mine + swap(theirs)).astype(BF)
    pre = dot(teacher, teacher_rows) + dot(student, student_rows)
    score = jnp.sum(gelu_tanh(pre) * critic_head[None, :], axis=1)
    dscore = -jax.nn.sigmoid(-score)
    dpre = (dscore[:, None] * critic_head[None, :] * gelu_slope(pre)).astype(BF)
    dpre2 = both(core, dpre, swap(dpre)).reshape(2 * tok_dev, -1)
    dstudent = dot(dpre2, student_rows, ((1,), (1,)))
    ds_high, ds_low = split(dstudent)
    grad_rows = dot(pick, ds_high) + dot(pick, ds_low)
    grad_out = (grad_rows * row_weight[:, None]).astype(BF)
    droute = lax.all_to_all(
        grad_out.reshape(chips, 2 * capacity, width), "yx", split_axis=0, concat_axis=0, tiled=True
    ).reshape(slots, width)

    dhidden = dot(droute, down_w, ((1,), (1,)))
    part_down = dot(hidden, droute, ((0,), (0,))).astype(BF)
    dgate = (dhidden * up * sig * (1.0 + gate * (1.0 - sig))).astype(BF)
    dup = (dhidden * gate * sig).astype(BF)
    part_gate = dot(routed, dgate, ((0,), (0,))).astype(BF)
    part_up = dot(routed, dup, ((0,), (0,))).astype(BF)
    groups = lax.axis_size("grp")

    def by_group(value):
        return value.reshape(groups, -1, width)

    parts = jnp.concatenate(
        [
            by_group(part_gate[:, :half]),
            by_group(part_gate[:, half:]),
            by_group(part_up[:, :half]),
            by_group(part_up[:, half:]),
            by_group(part_down),
        ],
        axis=1,
    )
    total = lax.psum_scatter(
        parts.reshape(-1, width), "grp", scatter_dimension=0, tiled=True
    ).astype(F32)
    grad_gate = jnp.concatenate([total[:rows_in], total[rows_in : 2 * rows_in]], axis=1)[None]
    grad_up = jnp.concatenate(
        [total[2 * rows_in : 3 * rows_in], total[3 * rows_in : 4 * rows_in]], axis=1
    )[None]
    return (grad_gate, grad_up, total[4 * rows_in :][None], score)


def solution(mesh):
    groups, members = mesh.devices.shape
    fine = Mesh(mesh.devices.reshape(groups, members // 2, 2), ("grp",) + EP)
    rows = P(("grp",) + EP, None)
    weights = P(EP, "grp", None)
    critic = P(EP, None)
    in_specs = (rows, rows, rows, rows, weights, weights, weights, critic, critic, P())
    out_specs = (weights, weights, weights, P(("grp",) + EP))
    return jax.shard_map(body, mesh=fine, in_specs=in_specs, out_specs=out_specs, check_vma=False)
```

time: 427 us -> 242 us (0.57)
  blocking collectives: 154 us -> 28.3 us
  waiting for transfers between devices: 179 us -> 78.8 us
  starting transfers between devices: 10.9 us -> 60 us
  matrix products: 32.4 us -> 18.8 us
  local copies, waits for them, and re-layouts: 24 us -> 31 us
    all_gather x1 -> x0, blocking collectives: 76.5 us -> none  [body(): lax.all_gather(critic_student, 'ep', axis=0, tiled=True)]
    all_gather x4 -> x1, waiting for transfers between devices: 71.3 us -> 0.02 us  [body(): teacher_rows = lax.all_gather(critic_teacher, EP, axis=0, tiled=True)]
    reduce_scatter x3 -> x1, waiting for transfers between devices: 105 us -> 42.1 us  [body(): lax.psum_scatter(parts.reshape(-1, width), 'grp', scatter_dimension=0, ti...]
    all_to_all x2 -> x1, blocking collectives: 77.3 us -> 28.3 us  [body(): lax.all_to_all(grad_out.reshape(chips, 2 * capacity, width), 'yx', split_...]
    ppermute x0 -> x12, starting transfers between devices: none -> 39.9 us  [shift(): lax.ppermute(value, axis, [(i, (i + step) % count) for i in range(count)])]
    ppermute x0 -> x12, waiting for transfers between devices: none -> 23.8 us  [shift(): lax.ppermute(value, axis, [(i, (i + step) % count) for i in range(count)])]
    dot_general x10 -> x16, matrix products: 32.4 us -> 18.8 us  [the longest x15 18.7 us: dot(): lax.dot_general(left, right, (dims, ((), ())), preferred_element_type=F32)]
    all_to_all x1 -> x2, waiting for transfers between devices: 0.01 us -> 12.3 us  [the longest x1 12.3 us: body(): lax.all_to_all(expert_out.reshape(chips, 2 * capacity, width), 'yx', spli...]
  transfers between devices with their start and end apart: 8 -> 16, of which waited for: 5 -> 7; matrix products, arithmetic and copies ran while one was open for 11% -> 17% of each run, Pallas kernels for 0% -> 0%
where the time goes in v1:
time: 242 us; the launch traced here: 241 us
  waiting for transfers between devices  78.8 us (33%)
  starting transfers between devices  60 us (25%)
  local copies, waits for them, and re-layouts  31 us (13%)
  blocking collectives  28.3 us (12%)
  matrix products  18.8 us (8%)
  between operations  14.6 us (6%)
  other arithmetic  9.32 us (4%)
    reduce_scatter x1, waiting for transfers between devices, body(): lax.psum_scatter(parts.reshape(-1, width), 'grp', scatter_dimension=0, ti...  42.1 us
    ppermute x12, starting transfers between devices, shift(): lax.ppermute(value, axis, [(i, (i + step) % count) for i in range(count)])  39.9 us
    all_to_all x1, blocking collectives, body(): lax.all_to_all(grad_out.reshape(chips, 2 * capacity, width), 'yx', split_...  28.3 us
    ppermute x12, waiting for transfers between devices, shift(): lax.ppermute(value, axis, [(i, (i + step) % count) for i in range(count)])  23.8 us
    dot_general x15, matrix products, dot(): lax.dot_general(left, right, (dims, ((), ())), preferred_element_type=F32)  18.7 us
    all_to_all x1, waiting for transfers between devices, body(): lax.all_to_all(expert_out.reshape(chips, 2 * capacity, width), 'yx', spli...  12.3 us
    all_to_all x1, starting transfers between devices, body(): lax.all_to_all(outbound, 'yx', split_axis=0, concat_axis=0, tiled=True)  10.3 us
    unnamed x48, local copies, waits for them, and re-layouts  9.77 us
  transfers between devices with their start and end apart: 16, of which 7 were waited for; matrix products, arithmetic and copies ran while one was open for 17% of the time, Pallas kernels for 0%

profile of v1, /device:TPU:2, one launch (start us, length us, event | category | flops | bytes accessed | tf_op | source)
XLA Modules:
  0.0 241.0 jit_solution(10602504171543977691)
XLA Ops:
  12.2 10.9 %collective-permute-start.3 = (bf16[384,512]{1,0:T(8,128)(2,1)S(1)}, bf16[384,512]{1,0:T(8,128)(2,1)}, u32[]{:S(2)}, u32[]{:S(2)}) collective-permute-start(bf16[384,512]{1,0:T(8,128)(2,1)S(1)} %bitcast_dynamic-update-slice_fusion.8), channel_id=1, source_target_pairs={{0,448},{64,0},{128,64},{192,128},{256,192},{320,256},{384,320},{4... | collective-permute-start | bytes 1179656 | tf_op jit(solution)/shard_map/ppermute | solution.py:37
  23.2 1.9 collective-permute-start.2
  28.4 2.4 collective-permute-start.1
  35.1 10.3 %all-to-all-start = ((bf16[32,32,512]{2,1,0:T(8,128)(2,1)}), bf16[32,32,512]{2,1,0:T(8,128)(2,1)}, u32[]{:S(2)}, u32[]{:S(2)}) async-start(bf16[32,32,512]{2,1,0:T(8,128)(2,1)} %pad_maximum_fusion), calls=%async_computation | async-start | bytes 2097152 | tf_op jit(solution)/shard_map/all_to_all | solution.py:123
  45.5 2.0 broadcast_in_dim.87
  48.3 5.1 %collective-permute-start.5 = (bf16[384,512]{1,0:T(8,128)(2,1)}, bf16[384,512]{1,0:T(8,128)(2,1)S(1)}, u32[]{:S(2)}, u32[]{:S(2)}) collective-permute-start(bf16[384,512]{1,0:T(8,128)(2,1)} %collective-permute-done.3), channel_id=1, source_target_pairs={{0,448},{64,0},{128,64},{192,128},{256,192},{320,256},{384,320},{4... | collective-permute-start | bytes 1179656 | tf_op jit(solution)/shard_map/ppermute | solution.py:37
  53.4 1.9 collective-permute-start.4
  58.0 3.7 %collective-permute-done.5 = bf16[384,512]{1,0:T(8,128)(2,1)S(1)} collective-permute-done((bf16[384,512]{1,0:T(8,128)(2,1)}, bf16[384,512]{1,0:T(8,128)(2,1)S(1)}, u32[]{:S(2)}, u32[]{:S(2)}) %collective-permute-start.5) | collective-permute-done | bytes 393248 | tf_op jit(solution)/shard_map/ppermute | solution.py:37
  61.7 5.5 %collective-permute-start.7 = (bf16[384,512]{1,0:T(8,128)(2,1)S(1)}, bf16[384,512]{1,0:T(8,128)(2,1)S(1)}, u32[]{:S(2)}, u32[]{:S(2)}) collective-permute-start(bf16[384,512]{1,0:T(8,128)(2,1)S(1)} %collective-permute-done.5), channel_id=1, source_target_pairs={{0,448},{64,0},{128,64},{192,128},{256,192},{320,256},{384,320},{4... | collective-permute-start | bytes 1179656 | tf_op jit(solution)/shard_map/ppermute | solution.py:37
  67.2 1.9 collective-permute-start.6
  70.7 9.0 %collective-permute-done.6 = bf16[384,512]{1,0:T(8,128)(2,1)S(1)} collective-permute-done((bf16[384,512]{1,0:T(8,128)(2,1)S(1)}, bf16[384,512]{1,0:T(8,128)(2,1)S(1)}, u32[]{:S(2)}, u32[]{:S(2)}) %collective-permute-start.6) | collective-permute-done | bytes 393248 | tf_op jit(solution)/shard_map/ppermute | solution.py:37
  83.3 8.2 %collective-permute-done.8 = bf16[384,512]{1,0:T(8,128)(2,1)S(1)} collective-permute-done((bf16[384,512]{1,0:T(8,128)(2,1)S(1)}, bf16[384,512]{1,0:T(8,128)(2,1)S(1)}, u32[]{:S(2)}, u32[]{:S(2)}) %collective-permute-start.8) | collective-permute-done | bytes 393248 | tf_op jit(solution)/shard_map/ppermute | solution.py:37
  92.3 2.3 slice.95
  94.5 2.8 %fusion.50 = (bf16[8,64,512]{2,1,0:T(8,128)(2,1)}, bf16[8,64,512]{2,1,0:T(8,128)(2,1)}, bf16[8,64,512]{2,1,0:T(8,128)(2,1)S(1)}, bf16[8,64,512]{2,1,0:T(8,128)(2,1)}) fusion(bf16[8,384,512]{2,1,0:T(8,128)(2,1)} %bitcast_dynamic-update-slice_fusion), kind=kLoop, calls=%fused_computation.119 | loop fusion | bytes 4194304 | tf_op jit(solution)/shard_map/slice | solution.py:136
  98.6 2.3 fusion.4
  101.0 2.9 %multiply_convert_fusion.2 = (bf16[768,1024]{1,0:T(8,128)(2,1)S(1)}, f32[768,1024]{1,0:T(8,128)}) fusion(f32[768,1024]{1,0:T(8,128)S(1)} %fusion.4, bf16[768,512]{1,0:T(8,128)(2,1)S(1)} %bitcast.123, bf16[512,512]{1,0:T(8,128)(2,1)S(1)} %bitcast.145, bf16[512,512]{1,0:T(8,128)(2,1)S(1)} %bitcast.144), kind=kOutput, calls=%fused_computation.4 | convolution fusion | flops 812122112 | bytes 9699328 | tf_op jit(solution)/shard_map/dot_general | solution.py:27
  105.7 9.7 %all-to-all-start.1 = ((bf16[32,24,512]{2,1,0:T(8,128)(2,1)}), bf16[32,24,512]{2,1,0:T(8,128)(2,1)S(1)}, u32[]{:S(2)}, u32[]{:S(2)}) async-start(bf16[32,24,512]{2,1,0:T(8,128)(2,1)} %bitcast.143), calls=%async_computation.1 | async-start | bytes 1572864 | tf_op jit(solution)/shard_map/all_to_all | solution.py:147
  117.2 1.9 collective-permute-start.10
  122.8 12.3 %all-to-all-done.1 = bf16[32,24,512]{2,1,0:T(8,128)(2,1)S(1)} async-done(((bf16[32,24,512]{2,1,0:T(8,128)(2,1)}), bf16[32,24,512]{2,1,0:T(8,128)(2,1)S(1)}, u32[]{:S(2)}, u32[]{:S(2)}) %all-to-all-start.1) | async-done | bytes 786464 | tf_op jit(solution)/shard_map/all_to_all | solution.py:147
  136.8 2.1 collective-permute-start.9
  138.9 4.2 %fusion.54 = f32[128,512]{1,0:T(8,128)S(1)} fusion(bf16[128,7168]{1,0:T(8,128)(2,1)S(1)} %copy-done, bf16[7168,512]{1,0:T(8,128)(2,1)} %all-gather.2.cloned.1.call-done), kind=kOutput, calls=%fused_computation.123 | convolution fusion | flops 939524096 | bytes 9437184 | tf_op jit(solution)/shard_map/dot_general | solution.py:27
  143.7 2.4 %collective-permute-start.11 = (bf16[128,512]{1,0:T(8,128)(2,1)S(1)}, bf16[128,512]{1,0:T(8,128)(2,1)S(1)}, u32[]{:S(2)}, u32[]{:S(2)}) collective-permute-start(bf16[128,512]{1,0:T(8,128)(2,1)S(1)} %fusion.18), channel_id=1, source_target_pairs={{0,1},{1,0},{2,3},{3,2},{4,5},{5,4},{6,7},{7,6},{8,9},{9,8},{10,11... | collective-permute-start | bytes 393224 | tf_op jit(solution)/shard_map/ppermute | solution.py:37
  148.5 28.3 %all_to_all.15 = bf16[32,24,512]{2,1,0:T(8,128)(2,1)S(1)} all-to-all(bf16[32,24,512]{2,1,0:T(8,128)(2,1)S(1)} %bitcast.130), channel_id=1, replica_groups=mesh['grp'=8,'yx'=32,'c'=2] {'yx'}, dimensions={0} | all-to-all | bytes 1572864 | tf_op jit(solution)/shard_map/all_to_all | solution.py:165
  188.5 42.1 %reduce-scatter.2.cloned.1.call-done = bf16[384,512]{1,0:T(8,128)(2,1)} async-done(((bf16[3072,512]{1,0:T(8,128)(2,1)}), bf16[384,512]{1,0:T(8,128)(2,1)}) %reduce-scatter.2.cloned.1.call-update) | async-done | bytes 393232 | tf_op jit(solution)/shard_map/reduce_scatter | solution.py:190
  (116 shorter events, 50.1 us)
Async XLA Ops:
  7.2 131.7 %copy-start = (bf16[128,7168]{1,0:T(8,128)(2,1)S(1)}, bf16[128,7168]{1,0:T(8,128)(2,1)}, u32[]{:S(2)}) copy-start(bf16[128,7168]{1,0:T(8,128)(2,1)} %param.11) | copy-start | bytes 5505028
  7.2 26.8 %copy-start.15 = (bf16[8,512]{1,0:T(8,128)(2,1)S(1)}, bf16[8,512]{1,0:T(8,128)(2,1)}, u32[]{:S(2)}) copy-start(bf16[8,512]{1,0:T(8,128)(2,1)} %param.18) | copy-start | bytes 24580
  7.2 131.7 %all-gather.2.cloned.1.call-start = ((), (), s32[]{:S(2)}) async-start(), calls=%async_computation.4 | async-start | bytes 7454720 | tf_op jit(solution)/shard_map/all_gather | solution.py:90
  12.2 36.0 %collective-permute-start.3 = (bf16[384,512]{1,0:T(8,128)(2,1)S(1)}, bf16[384,512]{1,0:T(8,128)(2,1)}, u32[]{:S(2)}, u32[]{:S(2)}) collective-permute-start(bf16[384,512]{1,0:T(8,128)(2,1)S(1)} %bitcast_dynamic-update-slice_fusion.8), channel_id=1, source_target_pairs={{0,448},{64,0},{128,64},{192,128},{256,192},{320,256},{384,320},{4... | collective-permute-start | bytes 1179656 | tf_op jit(solution)/shard_map/ppermute | solution.py:37
  23.2 30.2 %collective-permute-start.2 = (bf16[384,512]{1,0:T(8,128)(2,1)S(1)}, bf16[384,512]{1,0:T(8,128)(2,1)S(1)}, u32[]{:S(2)}, u32[]{:S(2)}) collective-permute-start(bf16[384,512]{1,0:T(8,128)(2,1)S(1)} %bitcast_dynamic-update-slice_fusion.8), channel_id=1, source_target_pairs={{0,64},{64,128},{128,192},{192,256},{256,320},{320,384},{384,448},... | collective-permute-start | bytes 1179656 | tf_op jit(solution)/shard_map/ppermute | solution.py:37
  26.5 4.4 %collective-permute-start = (f32[8,128]{1,0:T(8,128)S(1)}, f32[8,128]{1,0:T(8,128)S(1)}, u32[]{:S(2)}, u32[]{:S(2)}) collective-permute-start(f32[8,128]{1,0:T(8,128)S(1)} %pad_maximum_fusion.5), channel_id=1, source_target_pairs={{0,1},{1,0},{2,3},{3,2},{4,5},{5,4},{6,7},{7,6},{8,9},{9,8},{10,11... | collective-permute-start | bytes 12296 | tf_op jit(solution)/shard_map/ppermute | solution.py:37
  28.4 4.1 %collective-permute-start.1 = (bf16[128,512]{1,0:T(8,128)(2,1)}, bf16[128,512]{1,0:T(8,128)(2,1)S(1)}, u32[]{:S(2)}, u32[]{:S(2)}) collective-permute-start(bf16[128,512]{1,0:T(8,128)(2,1)} %param.10), channel_id=1, source_target_pairs={{0,1},{1,0},{2,3},{3,2},{4,5},{5,4},{6,7},{7,6},{8,9},{9,8},{10,11... | collective-permute-start | bytes 393224 | tf_op jit(solution)/shard_map/ppermute | solution.py:37
  35.1 62.3 %all-to-all-start = ((bf16[32,32,512]{2,1,0:T(8,128)(2,1)}), bf16[32,32,512]{2,1,0:T(8,128)(2,1)}, u32[]{:S(2)}, u32[]{:S(2)}) async-start(bf16[32,32,512]{2,1,0:T(8,128)(2,1)} %pad_maximum_fusion), calls=%async_computation | async-start | bytes 2097152 | tf_op jit(solution)/shard_map/all_to_all | solution.py:123
  48.3 13.4 %collective-permute-start.5 = (bf16[384,512]{1,0:T(8,128)(2,1)}, bf16[384,512]{1,0:T(8,128)(2,1)S(1)}, u32[]{:S(2)}, u32[]{:S(2)}) collective-permute-start(bf16[384,512]{1,0:T(8,128)(2,1)} %collective-permute-done.3), channel_id=1, source_target_pairs={{0,448},{64,0},{128,64},{192,128},{256,192},{320,256},{384,320},{4... | collective-permute-start | bytes 1179656 | tf_op jit(solution)/shard_map/ppermute | solution.py:37
  53.4 13.8 %collective-permute-start.4 = (bf16[384,512]{1,0:T(8,128)(2,1)S(1)}, bf16[384,512]{1,0:T(8,128)(2,1)S(1)}, u32[]{:S(2)}, u32[]{:S(2)}) collective-permute-start(bf16[384,512]{1,0:T(8,128)(2,1)S(1)} %collective-permute-done.2), channel_id=1, source_target_pairs={{0,64},{64,128},{128,192},{192,256},{256,320},{320,384},{384,448},... | collective-permute-start | bytes 1179656 | tf_op jit(solution)/shard_map/ppermute | solution.py:37
  61.7 20.8 %collective-permute-start.7 = (bf16[384,512]{1,0:T(8,128)(2,1)S(1)}, bf16[384,512]{1,0:T(8,128)(2,1)S(1)}, u32[]{:S(2)}, u32[]{:S(2)}) collective-permute-start(bf16[384,512]{1,0:T(8,128)(2,1)S(1)} %collective-permute-done.5), channel_id=1, source_target_pairs={{0,448},{64,0},{128,64},{192,128},{256,192},{320,256},{384,320},{4... | collective-permute-start | bytes 1179656 | tf_op jit(solution)/shard_map/ppermute | solution.py:37
  67.2 12.5 %collective-permute-start.6 = (bf16[384,512]{1,0:T(8,128)(2,1)S(1)}, bf16[384,512]{1,0:T(8,128)(2,1)S(1)}, u32[]{:S(2)}, u32[]{:S(2)}) collective-permute-start(bf16[384,512]{1,0:T(8,128)(2,1)S(1)} %collective-permute-done.4), channel_id=1, source_target_pairs={{0,64},{64,128},{128,192},{192,256},{256,320},{320,384},{384,448},... | collective-permute-start | bytes 1179656 | tf_op jit(solution)/shard_map/ppermute | solution.py:37
  79.7 11.8 %collective-permute-start.8 = (bf16[384,512]{1,0:T(8,128)(2,1)S(1)}, bf16[384,512]{1,0:T(8,128)(2,1)S(1)}, u32[]{:S(2)}, u32[]{:S(2)}) collective-permute-start(bf16[384,512]{1,0:T(8,128)(2,1)S(1)} %collective-permute-done.6), channel_id=1, source_target_pairs={{0,64},{64,128},{128,192},{192,256},{256,320},{320,384},{384,448},... | collective-permute-start | bytes 1179656 | tf_op jit(solution)/shard_map/ppermute | solution.py:37
  105.7 29.4 %all-to-all-start.1 = ((bf16[32,24,512]{2,1,0:T(8,128)(2,1)}), bf16[32,24,512]{2,1,0:T(8,128)(2,1)S(1)}, u32[]{:S(2)}, u32[]{:S(2)}) async-start(bf16[32,24,512]{2,1,0:T(8,128)(2,1)} %bitcast.143), calls=%async_computation.1 | async-start | bytes 1572864 | tf_op jit(solution)/shard_map/all_to_all | solution.py:147
  115.4 115.1 %reduce-scatter.2.cloned.1.call-start = ((), (), s32[]{:S(2)}) async-start(), calls=%async_computation.5 | async-start | bytes 3538944 | tf_op jit(solution)/shard_map/reduce_scatter | solution.py:190
  117.2 3.8 %collective-permute-start.10 = (bf16[32,8,512]{2,1,0:T(8,128)(2,1)}, bf16[32,8,512]{2,1,0:T(8,128)(2,1)}, u32[]{:S(2)}, u32[]{:S(2)}) collective-permute-start(bf16[32,8,512]{2,1,0:T(8,128)(2,1)} %slice.96), channel_id=1, source_target_pairs={{0,1},{1,0},{2,3},{3,2},{4,5},{5,4},{6,7},{7,6},{8,9},{9,8},{10,11... | collective-permute-start | bytes 786440 | tf_op jit(solution)/shard_map/ppermute | solution.py:37
  136.7 6.4 %copy-start.5 = (bf16[2,32,8,512]{3,2,0,1:T(8,128)(2,1)S(1)}, bf16[2,32,8,512]{3,2,0,1:T(8,128)(2,1)}, u32[]{:S(2)}) copy-start(bf16[2,32,8,512]{3,2,0,1:T(8,128)(2,1)} %pad_maximum_fusion.1) | copy-start | bytes 1572868
  136.7 6.4 %copy-start.11 = (f32[256,512]{1,0:T(8,128)S(1)}, f32[256,512]{1,0:T(8,128)}, u32[]{:S(2)}) copy-start(f32[256,512]{1,0:T(8,128)} %copy-done.10) | copy-start | bytes 1572868
  136.8 6.4 %copy-start.14 = (f32[512]{0:T(512)S(1)}, f32[512]{0:T(512)}, u32[]{:S(2)}) copy-start(f32[512]{0:T(512)} %param.19) | copy-start | bytes 6148
  136.8 6.3 %collective-permute-start.9 = (f32[128,512]{1,0:T(8,128)S(1)}, f32[128,512]{1,0:T(8,128)S(1)}, u32[]{:S(2)}, u32[]{:S(2)}) collective-permute-start(f32[128,512]{1,0:T(8,128)S(1)} %dynamic-slice_bitcast_fusion), channel_id=1, source_target_pairs={{0,1},{1,0},{2,3},{3,2},{4,5},{5,4},{6,7},{7,6},{8,9},{9,8},{10,11... | collective-permute-start | bytes 786440 | tf_op jit(solution)/shard_map/ppermute | solution.py:37
  143.1 4.6 %copy-start.2 = (bf16[768,256]{1,0:T(8,128)(2,1)S(1)}, bf16[768,256]{1,0:T(8,128)(2,1)}, u32[]{:S(2)}) copy-start(bf16[768,256]{1,0:T(8,128)(2,1)} %copy-done.1) | copy-start | bytes 1179652
  143.5 5.0 %copy-start.16 = (f32[128]{0:T(128)}, f32[128]{0:T(128)S(1)}, u32[]{:S(2)}) copy-start(f32[128]{0:T(128)S(1)} %get-tuple-element.31) | copy-start | bytes 1540
  143.7 3.4 %collective-permute-start.11 = (bf16[128,512]{1,0:T(8,128)(2,1)S(1)}, bf16[128,512]{1,0:T(8,128)(2,1)S(1)}, u32[]{:S(2)}, u32[]{:S(2)}) collective-permute-start(bf16[128,512]{1,0:T(8,128)(2,1)S(1)} %fusion.18), channel_id=1, source_target_pairs={{0,1},{1,0},{2,3},{3,2},{4,5},{5,4},{6,7},{7,6},{8,9},{9,8},{10,11... | collective-permute-start | bytes 393224 | tf_op jit(solution)/shard_map/ppermute | solution.py:37
  147.7 29.1 %copy-start.18 = (bf16[768,1024]{1,0:T(8,128)(2,1)S(1)}, bf16[768,1024]{1,0:T(8,128)(2,1)}, u32[]{:S(2)}) copy-start(bf16[768,1024]{1,0:T(8,128)(2,1)} %copy-done.17) | copy-start | bytes 4718596
  (12 other events, 23.8 us)
Sparse Core Ops, SparseCore 0:
  11.3 92.6 all-gather.1
  188.6 41.8 reduce-scatter.1

commit v2 on v1

--- a/solution.py
+++ b/solution.py
@@ -1,6 +1,10 @@
+import functools
+
 import jax
 import jax.numpy as jnp
 from jax import lax
+from jax.experimental import pallas as pl
+from jax.experimental.pallas import tpu as pltpu
 from jax.sharding import Mesh
 from jax.sharding import PartitionSpec as P
 
@@ -48,24 +52,219 @@
 
 def ring_gather(block):
     count = lax.axis_size("grp")
-    here = lax.axis_index("grp")
-    full = jnp.zeros((count,) + block.shape, block.dtype)
-
-    def put(full, piece, at):
-        return lax.dynamic_update_slice(full, piece[None], (at % count, 0, 0))
-
-    full = put(full, block, here)
+    pieces = [block] + [None] * (count - 1)
     up = down = block
     for step in range(1, count // 2 + 1):
         up = shift(up, "grp", 1)
-        full = put(full, up, here - step + count)
+        pieces[step] = up
         if 2 * step < count:
             down = shift(down, "grp", -1)
-            full = put(full, down, here + step)
-    return full
-
-
-def body(
+            pieces[count - step] = down
+    return pieces
+
+
+VMEM = pl.BlockSpec(memory_space=pltpu.VMEM)
+SMEM = pl.BlockSpec(memory_space=pltpu.SMEM)
+ANY = pl.BlockSpec(memory_space=pl.ANY)
+
+
+def pack_kernel(gate_ref, up_ref, down_ref, out_ref):
+    rows, hidden = gate_ref.shape
+    half = hidden // 2
+    out_ref[0:rows] = gate_ref[:, :half]
+    out_ref[rows : 2 * rows] = gate_ref[:, half:]
+    out_ref[2 * rows : 3 * rows] = up_ref[:, :half]
+    out_ref[3 * rows : 4 * rows] = up_ref[:, half:]
+    out_ref[4 * rows :] = down_ref[...]
+
+
+def pack_weights(gate, up, down):
+    rows = 4 * gate.shape[0] + down.shape[0]
+    return pl.pallas_call(
+        pack_kernel,
+        out_shape=jax.ShapeDtypeStruct((rows, down.shape[1]), BF),
+        in_specs=[VMEM] * 3,
+        out_specs=VMEM,
+        name="pack",
+    )(gate, up, down)
+
+
+def unpack_kernel(in_ref, gate_ref, up_ref, down_ref):
+    rows, hidden = gate_ref.shape
+    half = hidden // 2
+    gate_ref[:, :half] = in_ref[0:rows].astype(F32)
+    gate_ref[:, half:] = in_ref[rows : 2 * rows].astype(F32)
+    up_ref[:, :half] = in_ref[2 * rows : 3 * rows].astype(F32)
+    up_ref[:, half:] = in_ref[3 * rows : 4 * rows].astype(F32)
+    down_ref[...] = in_ref[4 * rows :].astype(F32)
+
+
+def unpack_grads(total, rows, half):
+    return pl.pallas_call(
+        unpack_kernel,
+        out_shape=[
+            jax.ShapeDtypeStruct((rows, 2 * half), F32),
+            jax.ShapeDtypeStruct((rows, 2 * half), F32),
+            jax.ShapeDtypeStruct((total.shape[0] - 4 * rows, total.shape[1]), F32),
+        ],
+        in_specs=[VMEM],
+        out_specs=[VMEM] * 3,
+        name="unpack",
+    )(total)
+
+
+def fetch(count, here_ref, pieces, target, sems, first):
+    copies = []
+    for k in range(count):
+        at = lax.rem(here_ref[0] - k + count, count)
+        piece = pieces[k].at[pl.ds(first, target.shape[1])]
+        copies.append(pltpu.make_async_copy(piece, target.at[at], sems.at[k]))
+    return copies
+
+
+def forward_kernel(count, rows, here_ref, routed_ref, *refs):
+    pieces = refs[:count]
+    hid_ref, coef_gate_ref, coef_up_ref, out_ref, full, sems = refs[count:]
+
+    @pl.when(pl.program_id(0) == 0)
+    def _():
+        copies = fetch(count, here_ref, pieces, full, sems, 0)
+        for copy in copies:
+            copy.start()
+        for copy in copies:
+            copy.wait()
+
+    width = routed_ref.shape[1]
+    half = full.shape[2]
+    routed = routed_ref[...]
+    out = jnp.zeros(out_ref.shape, F32)
+    for part in range(2):
+        gate_w = full[:, part * rows : (part + 1) * rows].reshape(width, half)
+        up_w = full[:, (2 + part) * rows : (3 + part) * rows].reshape(width, half)
+        gate = jnp.dot(routed, gate_w, preferred_element_type=F32)
+        up = jnp.dot(routed, up_w, preferred_element_type=F32)
+        sig = jax.nn.sigmoid(gate)
+        silu = gate * sig
+        hid = (silu * up).astype(BF)
+        span = slice(part * half, (part + 1) * half)
+        hid_ref[:, span] = hid
+        coef_up_ref[:, span] = silu.astype(BF)
+        coef_gate_ref[:, span] = (up * (sig + silu * (1.0 - sig))).astype(BF)
+        group = count // 2
+        down_w = full[part * group : (part + 1) * group, 4 * rows :].reshape(half, width)
+        out += jnp.dot(hid, down_w, preferred_element_type=F32)
+    out_ref[...] = out.astype(BF)
+
+
+def expert_forward(here, routed, pieces, rows, tile=384):
+    count = len(pieces)
+    slots, width = routed.shape
+    half = pieces[0].shape[1]
+    hidden = 2 * half
+    block = lambda cols: pl.BlockSpec((tile, cols), lambda i: (i, 0))
+    wide = jax.ShapeDtypeStruct((slots, hidden), BF)
+    return pl.pallas_call(
+        functools.partial(forward_kernel, count, rows),
+        grid=(slots // tile,),
+        out_shape=[wide, wide, wide, jax.ShapeDtypeStruct((slots, width), BF)],
+        in_specs=[SMEM, block(width)] + [ANY] * count,
+        out_specs=[block(hidden), block(hidden), block(hidden), block(width)],
+        scratch_shapes=[
+            pltpu.VMEM((count,) + pieces[0].shape, BF),
+            pltpu.SemaphoreType.DMA((count,)),
+        ],
+        cost_estimate=pl.CostEstimate(
+            flops=6 * slots * width * hidden,
+            transcendentals=slots * hidden,
+            bytes_accessed=6 * slots * hidden + 6 * width * hidden,
+        ),
+        name="expert_forward",
+    )(here, routed, *pieces)
+
+
+def backward_kernel(count, rows, here_ref, droute_ref, routed_ref, hid_ref, cg_ref, cu_ref, *refs):
+    pieces = refs[:count]
+    out_ref, down, parts, sems, out_sems = refs[count:]
+    step = pl.program_id(0)
+    width, half = routed_ref.shape[1], hid_ref.shape[1]
+    each = down.shape[1]
+    take = count // 2
+
+    @pl.when(step == 0)
+    def _():
+        copies = fetch(count, here_ref, pieces, down, sems, 4 * rows)
+        for copy in copies:
+            copy.start()
+        for copy in copies:
+            copy.wait()
+
+    droute = droute_ref[...]
+    routed = routed_ref[...]
+    down_w = down[pl.ds(step * take, take)].reshape(half, width)
+    dhid = lax.dot_general(droute, down_w, (((1,), (1,)), ((), ())), preferred_element_type=F32)
+    dgate = (dhid * cg_ref[...].astype(F32)).astype(BF)
+    dup = (dhid * cu_ref[...].astype(F32)).astype(BF)
+    rows_dot = functools.partial(
+        lax.dot_general, dimension_numbers=(((0,), (0,)), ((), ())), preferred_element_type=F32
+    )
+    part_down = rows_dot(hid_ref[...], droute).astype(BF).reshape(take, each, width)
+    part_gate = rows_dot(routed, dgate).astype(BF).reshape(count, rows, half)
+    part_up = rows_dot(routed, dup).astype(BF).reshape(count, rows, half)
+
+    def leaving(at):
+        places = [(pl.ds(at * take, take), pl.ds(4 * rows, each))]
+        places += [(slice(None), pl.ds(block * rows, rows)) for block in (at, 2 + at)]
+        return [
+            pltpu.make_async_copy(parts.at[place], out_ref.at[place], out_sems.at[3 * at + k])
+            for k, place in enumerate(places)
+        ]
+
+    for at in range(2):
+
+        @pl.when(step == at)
+        def _():
+            parts[at * take : (at + 1) * take, 4 * rows :] = part_down
+            parts[:, at * rows : (at + 1) * rows] = part_gate
+            parts[:, (2 + at) * rows : (3 + at) * rows] = part_up
+            for copy in leaving(at):
+                copy.start()
+
+    @pl.when(step == 1)
+    def _():
+        for at in range(2):
+            for copy in leaving(at):
+                copy.wait()
+
+
+def expert_backward(here, droute, routed, hid, coef_gate, coef_up, pieces, rows):
+    count = len(pieces)
+    slots, width = routed.shape
+    hidden = hid.shape[1]
+    whole = pl.BlockSpec((slots, width), lambda i: (0, 0))
+    block = pl.BlockSpec((slots, hidden // 2), lambda i: (0, i))
+    shape = (count,) + pieces[0].shape
+    return pl.pallas_call(
+        functools.partial(backward_kernel, count, rows),
+        grid=(2,),
+        out_shape=jax.ShapeDtypeStruct(shape, BF),
+        in_specs=[SMEM, whole, whole, block, block, block] + [ANY] * count,
+        out_specs=ANY,
+        scratch_shapes=[
+            pltpu.VMEM((count, shape[1] - 4 * rows, width), BF),
+            pltpu.VMEM(shape, BF),
+            pltpu.SemaphoreType.DMA((count,)),
+            pltpu.SemaphoreType.DMA((6,)),
+        ],
+        cost_estimate=pl.CostEstimate(
+            flops=8 * slots * width * hidden,
+            transcendentals=0,
+            bytes_accessed=6 * slots * hidden + 6 * width * hidden,
+        ),
+        name="expert_backward",
+    )(here, droute, routed, hid, coef_gate, coef_up, *pieces)
+
+
+def layer(
     tokens,
     teacher,
     expert_ids,
@@ -88,10 +287,8 @@
     rows_in = w_gate.shape[1]
 
     teacher_rows = lax.all_gather(critic_teacher, EP, axis=0, tiled=True)
-    pack = jnp.concatenate(
-        [w_gate[0, :, :half], w_gate[0, :, half:], w_up[0, :, :half], w_up[0, :, half:], w_down[0]]
-    )
-    full = ring_gather(pack)
+    here = lax.axis_index("grp").astype(jnp.int32).reshape(1)
+    pieces = ring_gather(pack_weights(w_gate[0], w_up[0], w_down[0]))
 
     meta = jnp.concatenate([expert_ids.T.astype(F32), route_weights.T])
     tok2 = both(core, tokens, swap(tokens)).reshape(2 * tok_dev, width)
@@ -127,25 +324,13 @@
         both(core, student_half, swap(student_half)).transpose(1, 0, 2, 3).reshape(width, -1)
     )
 
-    gate_w = jnp.concatenate(
-        [full[:, :rows_in].reshape(width, half), full[:, rows_in : 2 * rows_in].reshape(width, half)],
-        axis=1,
-    )
-    up_w = jnp.concatenate(
-        [
-            full[:, 2 * rows_in : 3 * rows_in].reshape(width, half),
-            full[:, 3 * rows_in : 4 * rows_in].reshape(width, half),
-        ],
-        axis=1,
-    )
-    down_w = full[:, 4 * rows_in :].reshape(hidden_all, width)
-    gate = dot(routed, gate_w)
-    up = dot(routed, up_w)
-    sig = jax.nn.sigmoid(gate)
-    hidden = (gate * sig * up).astype(BF)
-    expert_out = dot(hidden, down_w).astype(BF)
+    hidden, coef_gate, coef_up, expert_out = expert_forward(here, routed, pieces, rows_in)
     returned = lax.all_to_all(
-        expert_out.reshape(chips, 2 * capacity, width), "yx", split_axis=0, concat_axis=0, tiled=True
+        expert_out.reshape(chips, 2 * capacity, width),
+        "yx",
+        split_axis=0,
+        concat_axis=0,
+        tiled=True,
     ).reshape(slots, width)
 
     partial = dot(scaled_high, returned, ((0,), (0,))) + dot(scaled_low, returned, ((0,), (0,)))
@@ -153,7 +338,8 @@
     mine = lax.dynamic_index_in_dim(partial, core, 0, keepdims=False)
     theirs = lax.dynamic_index_in_dim(partial, 1 - core, 0, keepdims=False)
     student = (mine + swap(theirs)).astype(BF)
-    pre = dot(teacher, teacher_rows) + dot(student, student_rows)
+    pre_teacher = dot(teacher, teacher_rows)
+    pre = pre_teacher + dot(student, student_rows)
     score = jnp.sum(gelu_tanh(pre) * critic_head[None, :], axis=1)
     dscore = -jax.nn.sigmoid(-score)
     dpre = (dscore[:, None] * critic_head[None, :] * gelu_slope(pre)).astype(BF)
@@ -166,35 +352,12 @@
         grad_out.reshape(chips, 2 * capacity, width), "yx", split_axis=0, concat_axis=0, tiled=True
     ).reshape(slots, width)
 
-    dhidden = dot(droute, down_w, ((1,), (1,)))
-    part_down = dot(hidden, droute, ((0,), (0,))).astype(BF)
-    dgate = (dhidden * up * sig * (1.0 + gate * (1.0 - sig))).astype(BF)
-    dup = (dhidden * gate * sig).astype(BF)
-    part_gate = dot(routed, dgate, ((0,), (0,))).astype(BF)
-    part_up = dot(routed, dup, ((0,), (0,))).astype(BF)
-    groups = lax.axis_size("grp")
-
-    def by_group(value):
-        return value.reshape(groups, -1, width)
-
-    parts = jnp.concatenate(
-        [
-            by_group(part_gate[:, :half]),
-            by_group(part_gate[:, half:]),
-            by_group(part_up[:, :half]),
-            by_group(part_up[:, half:]),
-            by_group(part_down),
-        ],
-        axis=1,
-    )
+    parts = expert_backward(here, droute, routed, hidden, coef_gate, coef_up, pieces, rows_in)
     total = lax.psum_scatter(
         parts.reshape(-1, width), "grp", scatter_dimension=0, tiled=True
-    ).astype(F32)
-    grad_gate = jnp.concatenate([total[:rows_in], total[rows_in : 2 * rows_in]], axis=1)[None]
-    grad_up = jnp.concatenate(
-        [total[2 * rows_in : 3 * rows_in], total[3 * rows_in : 4 * rows_in]], axis=1
-    )[None]
-    return (grad_gate, grad_up, total[4 * rows_in :][None], score)
+    )
+    grad_gate, grad_up, grad_down = unpack_grads(total, rows_in, half)
+    return (grad_gate[None], grad_up[None], grad_down[None], score)
 
 
 def solution(mesh):
@@ -205,4 +368,4 @@
     critic = P(EP, None)
     in_specs = (rows, rows, rows, rows, weights, weights, weights, critic, critic, P())
     out_specs = (weights, weights, weights, P(("grp",) + EP))
-    return jax.shard_map(body, mesh=fine, in_specs=in_specs, out_specs=out_specs, check_vma=False)
+    return jax.shard_map(layer, mesh=fine, in_specs=in_specs, out_specs=out_specs, check_vma=False)

time: 242 us -> 229 us (0.946)
  the two profiles are of different devices: /device:TPU:2 before, /device:TPU:10 now
where the time goes in v2:
time: 229 us; the launch traced here: 228 us
  waiting for transfers between devices  86 us (38%)
  starting transfers between devices  59.6 us (26%)
  blocking collectives  28.2 us (12%)
  Pallas kernels  20.1 us (9%)
  between operations  14.5 us (6%)
  other arithmetic  7.53 us (3%)
  matrix products  6.96 us (3%)
  local copies, waits for them, and re-layouts  4.71 us (2%)
    reduce_scatter x1, waiting for transfers between devices, layer(): lax.psum_scatter(parts.reshape(-1, width), 'grp', scatter_dimension=0, ti...  45.5 us
    ppermute x12, starting transfers between devices, shift(): lax.ppermute(value, axis, [(i, (i + step) % count) for i in range(count)])  39.6 us
    ppermute x12, waiting for transfers between devices, shift(): lax.ppermute(value, axis, [(i, (i + step) % count) for i in range(count)])  28.7 us
    all_to_all x1, blocking collectives, layer(): lax.all_to_all(grad_out.reshape(chips, 2 * capacity, width), 'yx', split_...  28.2 us
    all_to_all x1, waiting for transfers between devices, layer(): lax.all_to_all(expert_out.reshape(chips, 2 * capacity, width), 'yx', spli...  11.1 us
    all_to_all x1, starting transfers between devices, layer(): lax.all_to_all(outbound, 'yx', split_axis=0, concat_axis=0, tiled=True)  10.2 us
    all_to_all x1, starting transfers between devices, layer(): lax.all_to_all(expert_out.reshape(chips, 2 * capacity, width), 'yx', spli...  9.76 us
    pallas_call x1, Pallas kernels, expert_backward(): pl.pallas_call(functools.partial(backward_kernel, count, rows), grid=(2,)...  9.06 us
  transfers between devices with their start and end apart: 16, of which 8 were waited for; matrix products, arithmetic and copies ran while one was open for 7% of the time, Pallas kernels for 4%

profile of v2, /device:TPU:10, one launch (start us, length us, event | category | flops | bytes accessed | tf_op | source)
XLA Modules:
  0.0 227.6 jit_solution(4364236987948313718)
XLA Ops:
  11.2 2.4 %collective-permute-start.1 = (bf16[128,512]{1,0:T(8,128)(2,1)}, bf16[128,512]{1,0:T(8,128)(2,1)S(1)}, u32[]{:S(2)}, u32[]{:S(2)}) collective-permute-start(bf16[128,512]{1,0:T(8,128)(2,1)} %param.10), channel_id=1, source_target_pairs={{0,1},{1,0},{2,3},{3,2},{4,5},{5,4},{6,7},{7,6},{8,9},{9,8},{10,11... | collective-permute-start | bytes 393224 | tf_op jit(solution)/shard_map/ppermute | solution.py:41
  18.0 10.2 %all-to-all-start = ((bf16[32,32,512]{2,1,0:T(8,128)(2,1)}), bf16[32,32,512]{2,1,0:T(8,128)(2,1)}, u32[]{:S(2)}, u32[]{:S(2)}) async-start(bf16[32,32,512]{2,1,0:T(8,128)(2,1)} %pad_maximum_fusion), calls=%async_computation | async-start | bytes 2097152 | tf_op jit(solution)/shard_map/all_to_all | solution.py:320
  30.0 4.3 %collective-permute-start.2 = (bf16[384,512]{1,0:T(8,128)(2,1)}, bf16[384,512]{1,0:T(8,128)(2,1)S(1)}, u32[]{:S(2)}, u32[]{:S(2)}) collective-permute-start(bf16[384,512]{1,0:T(8,128)(2,1)} %pack.1.refs_0_), channel_id=1, source_target_pairs={{0,64},{64,128},{128,192},{192,256},{256,320},{320,384},{384,448},... | collective-permute-start | bytes 1179656 | tf_op jit(solution)/shard_map/ppermute | solution.py:41
  34.3 8.6 %collective-permute-start.6 = (bf16[384,512]{1,0:T(8,128)(2,1)}, bf16[384,512]{1,0:T(8,128)(2,1)S(1)}, u32[]{:S(2)}, u32[]{:S(2)}) collective-permute-start(bf16[384,512]{1,0:T(8,128)(2,1)} %pack.1.refs_0_), channel_id=1, source_target_pairs={{0,448},{64,0},{128,64},{192,128},{256,192},{320,256},{384,320},{4... | collective-permute-start | bytes 1179656 | tf_op jit(solution)/shard_map/ppermute | solution.py:41
  42.9 7.0 %collective-permute-done.2.refs_1_ = bf16[384,512]{1,0:T(8,128)(2,1)S(1)} collective-permute-done((bf16[384,512]{1,0:T(8,128)(2,1)}, bf16[384,512]{1,0:T(8,128)(2,1)S(1)}, u32[]{:S(2)}, u32[]{:S(2)}) %collective-permute-start.2) | collective-permute-done | bytes 393248 | tf_op jit(solution)/shard_map/ppermute | solution.py:41
  49.9 1.9 collective-permute-start.3
  51.8 5.1 %collective-permute-start.7 = (bf16[384,512]{1,0:T(8,128)(2,1)S(1)}, bf16[384,512]{1,0:T(8,128)(2,1)}, u32[]{:S(2)}, u32[]{:S(2)}) collective-permute-start(bf16[384,512]{1,0:T(8,128)(2,1)S(1)} %collective-permute-done.6.refs_7_), channel_id=1, source_target_pairs={{0,448},{64,0},{128,64},{192,128},{256,192},{320,256},{384,320},{4... | collective-permute-start | bytes 1179656 | tf_op jit(solution)/shard_map/ppermute | solution.py:41
  57.0 6.0 %collective-permute-done.3.refs_2_ = bf16[384,512]{1,0:T(8,128)(2,1)S(1)} collective-permute-done((bf16[384,512]{1,0:T(8,128)(2,1)S(1)}, bf16[384,512]{1,0:T(8,128)(2,1)S(1)}, u32[]{:S(2)}, u32[]{:S(2)}) %collective-permute-start.3) | collective-permute-done | bytes 393248 | tf_op jit(solution)/shard_map/ppermute | solution.py:41
  63.0 1.9 collective-permute-start.4
  64.9 5.1 %collective-permute-start.8 = (bf16[384,512]{1,0:T(8,128)(2,1)}, bf16[384,512]{1,0:T(8,128)(2,1)}, u32[]{:S(2)}, u32[]{:S(2)}) collective-permute-start(bf16[384,512]{1,0:T(8,128)(2,1)} %collective-permute-done.7.refs_6_), channel_id=1, source_target_pairs={{0,448},{64,0},{128,64},{192,128},{256,192},{320,256},{384,320},{4... | collective-permute-start | bytes 1179656 | tf_op jit(solution)/shard_map/ppermute | solution.py:41
  70.1 5.3 %collective-permute-done.4.refs_3_ = bf16[384,512]{1,0:T(8,128)(2,1)} collective-permute-done((bf16[384,512]{1,0:T(8,128)(2,1)S(1)}, bf16[384,512]{1,0:T(8,128)(2,1)}, u32[]{:S(2)}, u32[]{:S(2)}) %collective-permute-start.4) | collective-permute-done | bytes 393248 | tf_op jit(solution)/shard_map/ppermute | solution.py:41
  75.3 1.9 collective-permute-start.5
  77.3 2.1 slice.18
  79.4 7.7 %collective-permute-done.5.refs_4_ = bf16[384,512]{1,0:T(8,128)(2,1)} collective-permute-done((bf16[384,512]{1,0:T(8,128)(2,1)}, bf16[384,512]{1,0:T(8,128)(2,1)}, u32[]{:S(2)}, u32[]{:S(2)}) %collective-permute-start.5) | collective-permute-done | bytes 393248 | tf_op jit(solution)/shard_map/ppermute | solution.py:41
  87.0 7.4 %expert_forward.1 = (bf16[768,1024]{1,0:T(8,128)(2,1)}, bf16[768,1024]{1,0:T(8,128)(2,1)}, bf16[768,1024]{1,0:T(8,128)(2,1)}, bf16[768,512]{1,0:T(8,128)(2,1)}) custom-call(s32[1]{0:T(128)} %bitcast.here_ref, bf16[768,512]{1,0:T(8,128)(2,1)} %bitcast.78, bf16[384,512]{1,0:T(8,128)(2,1)} %pack.1.refs_0_, bf16[384,512]{1,0:T(8,128)(2,1)} %copy-done.6, ...), custom_call_target="tpu_custom_call" | custom-call | flops 2415919104 | bytes 7864320 | tf_op jit(solution)/shard_map/expert_forward/pallas_call | solution.py:166
  94.4 9.8 %all-to-all-start.1 = ((bf16[32,24,512]{2,1,0:T(8,128)(2,1)}), bf16[32,24,512]{2,1,0:T(8,128)(2,1)S(1)}, u32[]{:S(2)}, u32[]{:S(2)}) async-start(bf16[32,24,512]{2,1,0:T(8,128)(2,1)} %bitcast.87), calls=%async_computation.1 | async-start | bytes 1572864 | tf_op jit(solution)/shard_map/all_to_all | solution.py:328
  105.9 1.9 collective-permute-start.10
  111.6 11.1 %all-to-all-done.1 = bf16[32,24,512]{2,1,0:T(8,128)(2,1)S(1)} async-done(((bf16[32,24,512]{2,1,0:T(8,128)(2,1)}), bf16[32,24,512]{2,1,0:T(8,128)(2,1)S(1)}, u32[]{:S(2)}, u32[]{:S(2)}) %all-to-all-start.1) | async-done | bytes 786464 | tf_op jit(solution)/shard_map/all_to_all | solution.py:328
  124.4 2.1 collective-permute-start.9
  126.5 4.2 %fusion.34 = f32[128,512]{1,0:T(8,128)S(1)} fusion(bf16[128,7168]{1,0:T(8,128)(2,1)S(1)} %copy-done, bf16[7168,512]{1,0:T(8,128)(2,1)} %all-gather.2.cloned.1.call-done), kind=kOutput, calls=%fused_computation.76 | convolution fusion | flops 939524096 | bytes 9437184 | tf_op jit(solution)/shard_map/dot_general | solution.py:31
  131.3 2.4 %collective-permute-start.11 = (bf16[128,512]{1,0:T(8,128)(2,1)S(1)}, bf16[128,512]{1,0:T(8,128)(2,1)S(1)}, u32[]{:S(2)}, u32[]{:S(2)}) collective-permute-start(bf16[128,512]{1,0:T(8,128)(2,1)S(1)} %fusion.6), channel_id=1, source_target_pairs={{0,1},{1,0},{2,3},{3,2},{4,5},{5,4},{6,7},{7,6},{8,9},{9,8},{10,11... | collective-permute-start | bytes 393224 | tf_op jit(solution)/shard_map/ppermute | solution.py:41
  136.1 28.2 %all_to_all.15 = bf16[32,24,512]{2,1,0:T(8,128)(2,1)} all-to-all(bf16[32,24,512]{2,1,0:T(8,128)(2,1)S(1)} %bitcast.81), channel_id=1, replica_groups=mesh['grp'=8,'yx'=32,'c'=2] {'yx'}, dimensions={0} | all-to-all | bytes 1572864 | tf_op jit(solution)/shard_map/all_to_all | solution.py:351
  164.3 9.1 %expert_backward.1 = bf16[8,384,512]{2,1,0:T(8,128)(2,1)} custom-call(s32[1]{0:T(128)} %bitcast.here_ref, bf16[768,512]{1,0:T(8,128)(2,1)} %bitcast.80, bf16[768,512]{1,0:T(8,128)(2,1)} %bitcast.79, bf16[768,1024]{1,0:T(8,128)(2,1)} %get-tuple-element.12.hid_ref, bf16[768,1024]{1,0:T(8,128)(2,1)} %get-tuple-element.13.cg_ref, ...), custom_call_target="tpu_custom_call" | custom-call | flops 3221225472 | bytes 7864320 | tf_op jit(solution)/shard_map/expert_backward/pallas_call | solution.py:246
  173.4 45.5 %reduce-scatter.2.cloned.1.call-done.in_ref = bf16[384,512]{1,0:T(8,128)(2,1)} async-done(((bf16[3072,512]{1,0:T(8,128)(2,1)}), bf16[384,512]{1,0:T(8,128)(2,1)}) %reduce-scatter.2.cloned.1.call-update) | async-done | bytes 393232 | tf_op jit(solution)/shard_map/reduce_scatter | solution.py:356
  (70 shorter events, 22.1 us)
Async XLA Ops:
  7.2 119.3 %copy-start = (bf16[128,7168]{1,0:T(8,128)(2,1)S(1)}, bf16[128,7168]{1,0:T(8,128)(2,1)}, u32[]{:S(2)}) copy-start(bf16[128,7168]{1,0:T(8,128)(2,1)} %param.11) | copy-start | bytes 5505028
  7.2 119.3 %all-gather.2.cloned.1.call-start = ((), (), s32[]{:S(2)}) async-start(), calls=%async_computation.4 | async-start | bytes 7454720 | tf_op jit(solution)/shard_map/all_gather | solution.py:289
  9.3 4.4 %collective-permute-start = (f32[8,128]{1,0:T(8,128)S(1)}, f32[8,128]{1,0:T(8,128)S(1)}, u32[]{:S(2)}, u32[]{:S(2)}) collective-permute-start(f32[8,128]{1,0:T(8,128)S(1)} %pad_maximum_fusion.5), channel_id=1, source_target_pairs={{0,1},{1,0},{2,3},{3,2},{4,5},{5,4},{6,7},{7,6},{8,9},{9,8},{10,11... | collective-permute-start | bytes 12296 | tf_op jit(solution)/shard_map/ppermute | solution.py:41
  11.2 4.1 %collective-permute-start.1 = (bf16[128,512]{1,0:T(8,128)(2,1)}, bf16[128,512]{1,0:T(8,128)(2,1)S(1)}, u32[]{:S(2)}, u32[]{:S(2)}) collective-permute-start(bf16[128,512]{1,0:T(8,128)(2,1)} %param.10), channel_id=1, source_target_pairs={{0,1},{1,0},{2,3},{3,2},{4,5},{5,4},{6,7},{7,6},{8,9},{9,8},{10,11... | collective-permute-start | bytes 393224 | tf_op jit(solution)/shard_map/ppermute | solution.py:41
  18.0 59.3 %all-to-all-start = ((bf16[32,32,512]{2,1,0:T(8,128)(2,1)}), bf16[32,32,512]{2,1,0:T(8,128)(2,1)}, u32[]{:S(2)}, u32[]{:S(2)}) async-start(bf16[32,32,512]{2,1,0:T(8,128)(2,1)} %pad_maximum_fusion), calls=%async_computation | async-start | bytes 2097152 | tf_op jit(solution)/shard_map/all_to_all | solution.py:320
  30.0 19.9 %collective-permute-start.2 = (bf16[384,512]{1,0:T(8,128)(2,1)}, bf16[384,512]{1,0:T(8,128)(2,1)S(1)}, u32[]{:S(2)}, u32[]{:S(2)}) collective-permute-start(bf16[384,512]{1,0:T(8,128)(2,1)} %pack.1.refs_0_), channel_id=1, source_target_pairs={{0,64},{64,128},{128,192},{192,256},{256,320},{320,384},{384,448},... | collective-permute-start | bytes 1179656 | tf_op jit(solution)/shard_map/ppermute | solution.py:41
  34.3 17.5 %collective-permute-start.6 = (bf16[384,512]{1,0:T(8,128)(2,1)}, bf16[384,512]{1,0:T(8,128)(2,1)S(1)}, u32[]{:S(2)}, u32[]{:S(2)}) collective-permute-start(bf16[384,512]{1,0:T(8,128)(2,1)} %pack.1.refs_0_), channel_id=1, source_target_pairs={{0,448},{64,0},{128,64},{192,128},{256,192},{320,256},{384,320},{4... | collective-permute-start | bytes 1179656 | tf_op jit(solution)/shard_map/ppermute | solution.py:41
  49.9 37.1 %copy-start.6 = (bf16[384,512]{1,0:T(8,128)(2,1)}, bf16[384,512]{1,0:T(8,128)(2,1)S(1)}, u32[]{:S(2)}) copy-start(bf16[384,512]{1,0:T(8,128)(2,1)S(1)} %collective-permute-done.2.refs_1_) | copy-start | bytes 1179652
  49.9 13.1 %collective-permute-start.3 = (bf16[384,512]{1,0:T(8,128)(2,1)S(1)}, bf16[384,512]{1,0:T(8,128)(2,1)S(1)}, u32[]{:S(2)}, u32[]{:S(2)}) collective-permute-start(bf16[384,512]{1,0:T(8,128)(2,1)S(1)} %collective-permute-done.2.refs_1_), channel_id=1, source_target_pairs={{0,64},{64,128},{128,192},{192,256},{256,320},{320,384},{384,448},... | collective-permute-start | bytes 1179656 | tf_op jit(solution)/shard_map/ppermute | solution.py:41
  51.8 35.2 %copy-start.7 = (bf16[384,512]{1,0:T(8,128)(2,1)}, bf16[384,512]{1,0:T(8,128)(2,1)S(1)}, u32[]{:S(2)}) copy-start(bf16[384,512]{1,0:T(8,128)(2,1)S(1)} %collective-permute-done.6.refs_7_) | copy-start | bytes 1179652
  51.8 13.1 %collective-permute-start.7 = (bf16[384,512]{1,0:T(8,128)(2,1)S(1)}, bf16[384,512]{1,0:T(8,128)(2,1)}, u32[]{:S(2)}, u32[]{:S(2)}) collective-permute-start(bf16[384,512]{1,0:T(8,128)(2,1)S(1)} %collective-permute-done.6.refs_7_), channel_id=1, source_target_pairs={{0,448},{64,0},{128,64},{192,128},{256,192},{320,256},{384,320},{4... | collective-permute-start | bytes 1179656 | tf_op jit(solution)/shard_map/ppermute | solution.py:41
  63.0 12.3 %collective-permute-start.4 = (bf16[384,512]{1,0:T(8,128)(2,1)S(1)}, bf16[384,512]{1,0:T(8,128)(2,1)}, u32[]{:S(2)}, u32[]{:S(2)}) collective-permute-start(bf16[384,512]{1,0:T(8,128)(2,1)S(1)} %collective-permute-done.3.refs_2_), channel_id=1, source_target_pairs={{0,64},{64,128},{128,192},{192,256},{256,320},{320,384},{384,448},... | collective-permute-start | bytes 1179656 | tf_op jit(solution)/shard_map/ppermute | solution.py:41
  64.9 14.5 %collective-permute-start.8 = (bf16[384,512]{1,0:T(8,128)(2,1)}, bf16[384,512]{1,0:T(8,128)(2,1)}, u32[]{:S(2)}, u32[]{:S(2)}) collective-permute-start(bf16[384,512]{1,0:T(8,128)(2,1)} %collective-permute-done.7.refs_6_), channel_id=1, source_target_pairs={{0,448},{64,0},{128,64},{192,128},{256,192},{320,256},{384,320},{4... | collective-permute-start | bytes 1179656 | tf_op jit(solution)/shard_map/ppermute | solution.py:41
  75.3 11.7 %collective-permute-start.5 = (bf16[384,512]{1,0:T(8,128)(2,1)}, bf16[384,512]{1,0:T(8,128)(2,1)}, u32[]{:S(2)}, u32[]{:S(2)}) collective-permute-start(bf16[384,512]{1,0:T(8,128)(2,1)} %collective-permute-done.4.refs_3_), channel_id=1, source_target_pairs={{0,64},{64,128},{128,192},{192,256},{256,320},{320,384},{384,448},... | collective-permute-start | bytes 1179656 | tf_op jit(solution)/shard_map/ppermute | solution.py:41
  94.4 28.2 %all-to-all-start.1 = ((bf16[32,24,512]{2,1,0:T(8,128)(2,1)}), bf16[32,24,512]{2,1,0:T(8,128)(2,1)S(1)}, u32[]{:S(2)}, u32[]{:S(2)}) async-start(bf16[32,24,512]{2,1,0:T(8,128)(2,1)} %bitcast.87), calls=%async_computation.1 | async-start | bytes 1572864 | tf_op jit(solution)/shard_map/all_to_all | solution.py:328
  104.2 114.7 %reduce-scatter.2.cloned.1.call-start = ((), (), s32[]{:S(2)}) async-start(), calls=%async_computation.5 | async-start | bytes 3538944 | tf_op jit(solution)/shard_map/reduce_scatter | solution.py:356
  105.9 3.8 %collective-permute-start.10 = (bf16[32,8,512]{2,1,0:T(8,128)(2,1)}, bf16[32,8,512]{2,1,0:T(8,128)(2,1)}, u32[]{:S(2)}, u32[]{:S(2)}) collective-permute-start(bf16[32,8,512]{2,1,0:T(8,128)(2,1)} %slice.19), channel_id=1, source_target_pairs={{0,1},{1,0},{2,3},{3,2},{4,5},{5,4},{6,7},{7,6},{8,9},{9,8},{10,11... | collective-permute-start | bytes 786440 | tf_op jit(solution)/shard_map/ppermute | solution.py:41
  124.4 6.3 %copy-start.3 = (bf16[2,32,8,512]{3,2,0,1:T(8,128)(2,1)S(1)}, bf16[2,32,8,512]{3,2,0,1:T(8,128)(2,1)}, u32[]{:S(2)}) copy-start(bf16[2,32,8,512]{3,2,0,1:T(8,128)(2,1)} %pad_maximum_fusion.1) | copy-start | bytes 1572868
  124.4 6.3 %copy-start.5 = (f32[256,512]{1,0:T(8,128)S(1)}, f32[256,512]{1,0:T(8,128)}, u32[]{:S(2)}) copy-start(f32[256,512]{1,0:T(8,128)} %copy-done.4) | copy-start | bytes 1572868
  124.4 6.3 %copy-start.9 = (f32[512]{0:T(512)S(1)}, f32[512]{0:T(512)}, u32[]{:S(2)}) copy-start(f32[512]{0:T(512)} %param.19) | copy-start | bytes 6148
  124.4 6.3 %collective-permute-start.9 = (f32[128,512]{1,0:T(8,128)S(1)}, f32[128,512]{1,0:T(8,128)S(1)}, u32[]{:S(2)}, u32[]{:S(2)}) collective-permute-start(f32[128,512]{1,0:T(8,128)S(1)} %dynamic-slice_bitcast_fusion), channel_id=1, source_target_pairs={{0,1},{1,0},{2,3},{3,2},{4,5},{5,4},{6,7},{7,6},{8,9},{9,8},{10,11... | collective-permute-start | bytes 786440 | tf_op jit(solution)/shard_map/ppermute | solution.py:41
  131.1 4.6 %copy-start.11 = (f32[128]{0:T(128)}, f32[128]{0:T(128)S(1)}, u32[]{:S(2)}) copy-start(f32[128]{0:T(128)S(1)} %get-tuple-element.31) | copy-start | bytes 1540
  131.1 4.2 %copy-start.2 = (bf16[768,256]{1,0:T(8,128)(2,1)S(1)}, bf16[768,256]{1,0:T(8,128)(2,1)}, u32[]{:S(2)}) copy-start(bf16[768,256]{1,0:T(8,128)(2,1)} %copy-done.1) | copy-start | bytes 1179652
  131.3 3.4 %collective-permute-start.11 = (bf16[128,512]{1,0:T(8,128)(2,1)S(1)}, bf16[128,512]{1,0:T(8,128)(2,1)S(1)}, u32[]{:S(2)}, u32[]{:S(2)}) collective-permute-start(bf16[128,512]{1,0:T(8,128)(2,1)S(1)} %fusion.6), channel_id=1, source_target_pairs={{0,1},{1,0},{2,3},{3,2},{4,5},{5,4},{6,7},{7,6},{8,9},{9,8},{10,11... | collective-permute-start | bytes 393224 | tf_op jit(solution)/shard_map/ppermute | solution.py:41
  (4 other events, 6.0 us)
Sparse Core Ops, SparseCore 0:
  11.3 93.6 all-gather.1
  173.5 45.3 reduce-scatter.1

commit v3 on v2

--- a/solution.py
+++ b/solution.py
@@ -1,4 +1,5 @@
 import functools
+import math
 
 import jax
 import jax.numpy as jnp
@@ -9,7 +10,9 @@
 from jax.sharding import PartitionSpec as P
 
 TOP = 4
-EP = ("yx", "c")
+CHIPS = ("y", "x")
+ROW = ("x", "c")
+EP = ("y", "x", "c")
 BF = jnp.bfloat16
 F32 = jnp.float32
 
@@ -48,19 +51,6 @@
 def both(core, own, other):
     first = core == 0
     return jnp.stack([jnp.where(first, own, other), jnp.where(first, other, own)])
-
-
-def ring_gather(block):
-    count = lax.axis_size("grp")
-    pieces = [block] + [None] * (count - 1)
-    up = down = block
-    for step in range(1, count // 2 + 1):
-        up = shift(up, "grp", 1)
-        pieces[step] = up
-        if 2 * step < count:
-            down = shift(down, "grp", -1)
-            pieces[count - step] = down
-    return pieces
 
 
 VMEM = pl.BlockSpec(memory_space=pltpu.VMEM)
@@ -113,27 +103,8 @@
     )(total)
 
 
-def fetch(count, here_ref, pieces, target, sems, first):
-    copies = []
-    for k in range(count):
-        at = lax.rem(here_ref[0] - k + count, count)
-        piece = pieces[k].at[pl.ds(first, target.shape[1])]
-        copies.append(pltpu.make_async_copy(piece, target.at[at], sems.at[k]))
-    return copies
-
-
-def forward_kernel(count, rows, here_ref, routed_ref, *refs):
-    pieces = refs[:count]
-    hid_ref, coef_gate_ref, coef_up_ref, out_ref, full, sems = refs[count:]
-
-    @pl.when(pl.program_id(0) == 0)
-    def _():
-        copies = fetch(count, here_ref, pieces, full, sems, 0)
-        for copy in copies:
-            copy.start()
-        for copy in copies:
-            copy.wait()
-
+def forward_kernel(rows, routed_ref, full, hid_ref, coef_gate_ref, coef_up_ref, out_ref):
+    count = full.shape[0]
     width = routed_ref.shape[1]
     half = full.shape[2]
     routed = routed_ref[...]
@@ -156,51 +127,39 @@
     out_ref[...] = out.astype(BF)
 
 
-def expert_forward(here, routed, pieces, rows, tile=384):
-    count = len(pieces)
+def expert_forward(routed, full, rows, tile=384):
     slots, width = routed.shape
-    half = pieces[0].shape[1]
+    half = full.shape[2]
     hidden = 2 * half
     block = lambda cols: pl.BlockSpec((tile, cols), lambda i: (i, 0))
     wide = jax.ShapeDtypeStruct((slots, hidden), BF)
     return pl.pallas_call(
-        functools.partial(forward_kernel, count, rows),
+        functools.partial(forward_kernel, rows),
         grid=(slots // tile,),
         out_shape=[wide, wide, wide, jax.ShapeDtypeStruct((slots, width), BF)],
-        in_specs=[SMEM, block(width)] + [ANY] * count,
+        in_specs=[block(width), pl.BlockSpec(full.shape, lambda i: (0, 0, 0))],
         out_specs=[block(hidden), block(hidden), block(hidden), block(width)],
-        scratch_shapes=[
-            pltpu.VMEM((count,) + pieces[0].shape, BF),
-            pltpu.SemaphoreType.DMA((count,)),
-        ],
         cost_estimate=pl.CostEstimate(
             flops=6 * slots * width * hidden,
             transcendentals=slots * hidden,
             bytes_accessed=6 * slots * hidden + 6 * width * hidden,
         ),
         name="expert_forward",
-    )(here, routed, *pieces)
-
-
-def backward_kernel(count, rows, here_ref, droute_ref, routed_ref, hid_ref, cg_ref, cu_ref, *refs):
-    pieces = refs[:count]
-    out_ref, down, parts, sems, out_sems = refs[count:]
+    )(routed, full)
+
+
+def backward_kernel(
+    rows, droute_ref, routed_ref, hid_ref, cg_ref, cu_ref, down, out_ref, parts, out_sems
+):
+    count = out_ref.shape[0]
     step = pl.program_id(0)
     width, half = routed_ref.shape[1], hid_ref.shape[1]
     each = down.shape[1]
     take = count // 2
 
-    @pl.when(step == 0)
-    def _():
-        copies = fetch(count, here_ref, pieces, down, sems, 4 * rows)
-        for copy in copies:
-            copy.start()
-        for copy in copies:
-            copy.wait()
-
     droute = droute_ref[...]
     routed = routed_ref[...]
-    down_w = down[pl.ds(step * take, take)].reshape(half, width)
+    down_w = down[...].reshape(half, width)
     dhid = lax.dot_general(droute, down_w, (((1,), (1,)), ((), ())), preferred_element_type=F32)
     dgate = (dhid * cg_ref[...].astype(F32)).astype(BF)
     dup = (dhid * cu_ref[...].astype(F32)).astype(BF)
@@ -236,23 +195,22 @@
                 copy.wait()
 
 
-def expert_backward(here, droute, routed, hid, coef_gate, coef_up, pieces, rows):
-    count = len(pieces)
+def expert_backward(droute, routed, hid, coef_gate, coef_up, full, rows):
     slots, width = routed.shape
     hidden = hid.shape[1]
     whole = pl.BlockSpec((slots, width), lambda i: (0, 0))
     block = pl.BlockSpec((slots, hidden // 2), lambda i: (0, i))
-    shape = (count,) + pieces[0].shape
-    return pl.pallas_call(
-        functools.partial(backward_kernel, count, rows),
+    shape = full.shape
+    each = shape[1] - 4 * rows
+    down = pl.BlockSpec((shape[0] // 2, each, width), lambda i: (i, 4 * rows // each, 0))
+    return pl.pallas_call(
+        functools.partial(backward_kernel, rows),
         grid=(2,),
         out_shape=jax.ShapeDtypeStruct(shape, BF),
-        in_specs=[SMEM, whole, whole, block, block, block] + [ANY] * count,
+        in_specs=[whole, whole, block, block, block, down],
         out_specs=ANY,
         scratch_shapes=[
-            pltpu.VMEM((count, shape[1] - 4 * rows, width), BF),
             pltpu.VMEM(shape, BF),
-            pltpu.SemaphoreType.DMA((count,)),
             pltpu.SemaphoreType.DMA((6,)),
         ],
         cost_estimate=pl.CostEstimate(
@@ -261,7 +219,35 @@
             bytes_accessed=6 * slots * hidden + 6 * width * hidden,
         ),
         name="expert_backward",
-    )(here, droute, routed, hid, coef_gate, coef_up, *pieces)
+    )(droute, routed, hid, coef_gate, coef_up, full)
+
+
+def slice_kernel(in_ref, out_ref):
+    out_ref[0] = in_ref[...]
+
+
+def slice_features(teacher, side):
+    tok_dev, depth = teacher.shape
+    each = depth // side
+    return pl.pallas_call(
+        slice_kernel,
+        grid=(side,),
+        out_shape=jax.ShapeDtypeStruct((side, tok_dev, each), BF),
+        in_specs=[pl.BlockSpec((tok_dev, each), lambda i: (0, i))],
+        out_specs=pl.BlockSpec((1, tok_dev, each), lambda i: (i, 0, 0)),
+        name="slice_features",
+    )(teacher)
+
+
+def share_teacher(slices):
+    return lax.all_to_all(slices, ROW, split_axis=0, concat_axis=0, tiled=True)
+
+
+def share_critic(critic_teacher):
+    side = lax.axis_size("y")
+    turn = [(i * side + j, j * side + i) for i in range(side) for j in range(side)]
+    turned = lax.ppermute(critic_teacher, EP, turn)
+    return lax.all_gather(turned, "y", axis=0, tiled=True)
 
 
 def layer(
@@ -277,7 +263,7 @@
     critic_head,
 ):
     core = lax.axis_index("c")
-    chips = lax.axis_size("yx")
+    chips = lax.axis_size("y") * lax.axis_size("x")
     experts = 2 * chips
     tok_dev, width = tokens.shape
     capacity = 3 * tok_dev * TOP // (2 * experts)
@@ -286,9 +272,16 @@
     half = hidden_all // 2
     rows_in = w_gate.shape[1]
 
-    teacher_rows = lax.all_gather(critic_teacher, EP, axis=0, tiled=True)
-    here = lax.axis_index("grp").astype(jnp.int32).reshape(1)
-    pieces = ring_gather(pack_weights(w_gate[0], w_up[0], w_down[0]))
+    packed = pack_weights(w_gate[0], w_up[0], w_down[0])
+    packed, teacher, tokens, expert_ids, critic_student = lax.optimization_barrier(
+        (packed, teacher, tokens, expert_ids, critic_student)
+    )
+    full = lax.all_gather(packed, "grp", axis=0)
+    theirs = share_teacher(slice_features(teacher, lax.axis_size("y")))
+    student_half = lax.all_gather(critic_student, CHIPS, axis=0)
+    student_rows = (
+        both(core, student_half, swap(student_half)).transpose(1, 0, 2, 3).reshape(width, -1)
+    )
 
     meta = jnp.concatenate([expert_ids.T.astype(F32), route_weights.T])
     tok2 = both(core, tokens, swap(tokens)).reshape(2 * tok_dev, width)
@@ -313,24 +306,18 @@
     scaled_high, scaled_low = split(scaled)
 
     outbound = dot(pick, tok2).astype(BF).reshape(chips, 2 * capacity, width)
-    rows_st = critic_student.shape[0]
-    outbound = jnp.concatenate(
-        [outbound, jnp.broadcast_to(critic_student[None], (chips, rows_st, width))], axis=1
-    )
-    inbound = lax.all_to_all(outbound, "yx", split_axis=0, concat_axis=0, tiled=True)
-    routed = inbound[:, : 2 * capacity].reshape(slots, width)
-    student_half = inbound[:, 2 * capacity :]
-    student_rows = (
-        both(core, student_half, swap(student_half)).transpose(1, 0, 2, 3).reshape(width, -1)
-    )
-
-    hidden, coef_gate, coef_up, expert_out = expert_forward(here, routed, pieces, rows_in)
+    outbound, theirs, student_rows = lax.optimization_barrier((outbound, theirs, student_rows))
+    inbound = lax.all_to_all(outbound, CHIPS, split_axis=0, concat_axis=0, tiled=True)
+    critic_rows = share_critic(critic_teacher)
+    product = dot(theirs.reshape(-1, theirs.shape[2]), critic_rows).astype(BF)
+    inbound, product = lax.optimization_barrier((inbound, product))
+    pre_teacher = lax.psum_scatter(product, ROW, scatter_dimension=0, tiled=True)
+    pre_teacher = pre_teacher.astype(F32)
+    routed = inbound.reshape(slots, width)
+
+    hidden, coef_gate, coef_up, expert_out = expert_forward(routed, full, rows_in)
     returned = lax.all_to_all(
-        expert_out.reshape(chips, 2 * capacity, width),
-        "yx",
-        split_axis=0,
-        concat_axis=0,
-        tiled=True,
+        expert_out.reshape(chips, 2 * capacity, width), CHIPS, split_axis=0, concat_axis=0, tiled=True
     ).reshape(slots, width)
 
     partial = dot(scaled_high, returned, ((0,), (0,))) + dot(scaled_low, returned, ((0,), (0,)))
@@ -338,7 +325,6 @@
     mine = lax.dynamic_index_in_dim(partial, core, 0, keepdims=False)
     theirs = lax.dynamic_index_in_dim(partial, 1 - core, 0, keepdims=False)
     student = (mine + swap(theirs)).astype(BF)
-    pre_teacher = dot(teacher, teacher_rows)
     pre = pre_teacher + dot(student, student_rows)
     score = jnp.sum(gelu_tanh(pre) * critic_head[None, :], axis=1)
     dscore = -jax.nn.sigmoid(-score)
@@ -349,10 +335,10 @@
     grad_rows = dot(pick, ds_high) + dot(pick, ds_low)
     grad_out = (grad_rows * row_weight[:, None]).astype(BF)
     droute = lax.all_to_all(
-        grad_out.reshape(chips, 2 * capacity, width), "yx", split_axis=0, concat_axis=0, tiled=True
+        grad_out.reshape(chips, 2 * capacity, width), CHIPS, split_axis=0, concat_axis=0, tiled=True
     ).reshape(slots, width)
 
-    parts = expert_backward(here, droute, routed, hidden, coef_gate, coef_up, pieces, rows_in)
+    parts = expert_backward(droute, routed, hidden, coef_gate, coef_up, full, rows_in)
     total = lax.psum_scatter(
         parts.reshape(-1, width), "grp", scatter_dimension=0, tiled=True
     )
@@ -362,7 +348,8 @@
 
 def solution(mesh):
     groups, members = mesh.devices.shape
-    fine = Mesh(mesh.devices.reshape(groups, members // 2, 2), ("grp",) + EP)
+    side = math.isqrt(members)
+    fine = Mesh(mesh.devices.reshape(groups, side, side // 2, 2), ("grp",) + EP)
     rows = P(("grp",) + EP, None)
     weights = P(EP, "grp", None)
     critic = P(EP, None)

time: 229 us -> 329 us (1.44)
  the two profiles are of different devices: /device:TPU:10 before, /device:TPU:6 now
where the time goes in v3:
time: 329 us; the launch traced here: 328 us
  waiting for transfers between devices  127 us (39%)
  blocking collectives  110 us (33%)
  starting transfers between devices  38.9 us (12%)
  Pallas kernels  23.2 us (7%)
  between operations  15.7 us (5%)
  matrix products  8.32 us (3%)
    all_gather x1, blocking collectives, layer(): student_half = lax.all_gather(critic_student, CHIPS, axis=0)  51.8 us
    reduce_scatter x1, waiting for transfers between devices, layer(): lax.psum_scatter(parts.reshape(-1, width), 'grp', scatter_dimension=0, ti...  47.7 us
    all_to_all x1, blocking collectives, layer(): lax.all_to_all(grad_out.reshape(chips, 2 * capacity, width), CHIPS, split...  31.5 us
    all_gather x1, blocking collectives, share_critic(): return lax.all_gather(turned, 'y', axis=0, tiled=True)  27 us
    reduce_scatter x1, waiting for transfers between devices, layer(): lax.psum_scatter(product, ROW, scatter_dimension=0, tiled=True)  22.7 us
    all_to_all x1, waiting for transfers between devices, share_teacher(): return lax.all_to_all(slices, ROW, split_axis=0, concat_axis=0, tiled=True)  20 us
    ppermute x1, waiting for transfers between devices, share_critic(): turned = lax.ppermute(critic_teacher, EP, turn)  19.8 us
    all_to_all x1, waiting for transfers between devices, layer(): lax.all_to_all(expert_out.reshape(chips, 2 * capacity, width), CHIPS, spl...  15.8 us
  transfers between devices with their start and end apart: 12, of which 6 were waited for; matrix products, arithmetic and copies ran while one was open for 3% of the time, Pallas kernels for 2%

profile of v3, /device:TPU:6, one launch (start us, length us, event | category | flops | bytes accessed | tf_op | source)
XLA Modules:
  0.0 327.6 jit_solution(1276918370144273643)
XLA Ops:
  8.0 1.8 pack.1
  11.3 1.9 collective-permute-start
  13.2 2.4 collective-permute-start.1
  15.6 51.8 %all-gather = bf16[256,512]{1,0:T(8,128)(2,1)S(1)} all-gather(bf16[8,512]{1,0:T(8,128)(2,1)} %param.18), channel_id=2, replica_groups=mesh['grp'=8,'y'=8,'x'=4,'c'=2] {'y','x'}, dimensions={0}, use_global_device_ids=true | all-gather | bytes 270336 | tf_op jit(solution)/shard_map/all_gather | solution.py:281
  67.4 1.9 collective-permute-start.2
  69.4 5.6 %slice_features.1 = bf16[8,128,896]{2,1,0:T(8,128)(2,1)} custom-call(bf16[128,7168]{1,0:T(8,128)(2,1)} %in_ref), custom_call_target="tpu_custom_call" | custom-call | tf_op jit(solution)/shard_map/slice_features/pallas_call | solution.py:232
  74.9 5.1 %all-to-all-start = ((bf16[8,128,896]{2,1,0:T(8,128)(2,1)}), bf16[8,128,896]{2,1,0:T(8,128)(2,1)}, u32[]{:S(2)}, u32[]{:S(2)}) async-start(bf16[8,128,896]{2,1,0:T(8,128)(2,1)} %slice_features.1), calls=%async_computation | async-start | bytes 3670016 | tf_op jit(solution)/shard_map/all_to_all | solution.py:243
  82.4 20.0 %all-to-all-done = bf16[8,128,896]{2,1,0:T(8,128)(2,1)} async-done(((bf16[8,128,896]{2,1,0:T(8,128)(2,1)}), bf16[8,128,896]{2,1,0:T(8,128)(2,1)}, u32[]{:S(2)}, u32[]{:S(2)}) %all-to-all-start) | async-done | bytes 1835040 | tf_op jit(solution)/shard_map/all_to_all | solution.py:243
  102.4 6.6 %all-to-all-start.1 = ((bf16[32,24,512]{2,1,0:T(8,128)(2,1)}), bf16[32,24,512]{2,1,0:T(8,128)(2,1)S(1)}, u32[]{:S(2)}, u32[]{:S(2)}) async-start(bf16[32,24,512]{2,1,0:T(8,128)(2,1)} %bitcast.13), calls=%async_computation.1 | async-start | bytes 1572864 | tf_op jit(solution)/shard_map/all_to_all | solution.py:310
  109.0 5.5 %collective-permute-start.3 = (bf16[112,512]{1,0:T(8,128)(2,1)S(1)}, bf16[112,512]{1,0:T(8,128)(2,1)S(1)}, u32[]{:S(2)}, u32[]{:S(2)}) collective-permute-start(bf16[112,512]{1,0:T(8,128)(2,1)S(1)} %copy-done.5), channel_id=1, source_target_pairs={{0,0},{1,8},{2,16},{3,24},{4,32},{5,40},{6,48},{7,56},{8,1},{9,9},... | collective-permute-start | bytes 344072 | tf_op jit(solution)/shard_map/ppermute | solution.py:249
  114.5 19.8 %collective-permute-done.3 = bf16[112,512]{1,0:T(8,128)(2,1)S(1)} collective-permute-done((bf16[112,512]{1,0:T(8,128)(2,1)S(1)}, bf16[112,512]{1,0:T(8,128)(2,1)S(1)}, u32[]{:S(2)}, u32[]{:S(2)}) %collective-permute-start.3) | collective-permute-done | bytes 114720 | tf_op jit(solution)/shard_map/ppermute | solution.py:249
  134.3 27.0 %all_gather.17 = bf16[896,512]{1,0:T(8,128)(2,1)S(1)} all-gather(bf16[112,512]{1,0:T(8,128)(2,1)S(1)} %collective-permute-done.3), channel_id=1, replica_groups=mesh['grp'=8,'y'=8,'x'=4,'c'=2] {'y'}, dimensions={0}, use_global_device_ids=true | all-gather | bytes 1032192 | tf_op jit(solution)/shard_map/all_gather | solution.py:250
  161.3 3.8 %convolution_convert_fusion = bf16[1024,512]{1,0:T(8,128)(2,1)} fusion(bf16[1024,896]{1,0:T(8,128)(2,1)} %bitcast.20, bf16[896,512]{1,0:T(8,128)(2,1)S(1)} %all_gather.17), kind=kOutput, calls=%fused_computation.5 | convolution fusion | flops 940048384 | bytes 3801088 | tf_op jit(solution)/shard_map/dot_general | solution.py:34
  165.9 6.3 %expert_forward.1 = (bf16[768,1024]{1,0:T(8,128)(2,1)}, bf16[768,1024]{1,0:T(8,128)(2,1)}, bf16[768,1024]{1,0:T(8,128)(2,1)}, bf16[768,512]{1,0:T(8,128)(2,1)}) custom-call(bf16[768,512]{1,0:T(8,128)(2,1)} %bitcast.82, bf16[8,384,512]{2,1,0:T(8,128)(2,1)} %bitcast.86), custom_call_target="tpu_custom_call" | custom-call | flops 2415919104 | bytes 7864320 | tf_op jit(solution)/shard_map/expert_forward/pallas_call | solution.py:136
  172.2 9.2 %all-to-all-start.2 = ((bf16[32,24,512]{2,1,0:T(8,128)(2,1)}), bf16[32,24,512]{2,1,0:T(8,128)(2,1)S(1)}, u32[]{:S(2)}, u32[]{:S(2)}) async-start(bf16[32,24,512]{2,1,0:T(8,128)(2,1)} %bitcast.93), calls=%async_computation.3 | async-start | bytes 1572864 | tf_op jit(solution)/shard_map/all_to_all | solution.py:319
  182.1 15.8 %all-to-all-done.2 = bf16[32,24,512]{2,1,0:T(8,128)(2,1)S(1)} async-done(((bf16[32,24,512]{2,1,0:T(8,128)(2,1)}), bf16[32,24,512]{2,1,0:T(8,128)(2,1)S(1)}, u32[]{:S(2)}, u32[]{:S(2)}) %all-to-all-start.2) | async-done | bytes 786464 | tf_op jit(solution)/shard_map/all_to_all | solution.py:319
  198.7 1.9 collective-permute-start.4
  200.7 22.7 %reduce-scatter.3.cloned.1.call-done = bf16[128,512]{1,0:T(8,128)(2,1)} async-done(((bf16[1024,512]{1,0:T(8,128)(2,1)}), bf16[128,512]{1,0:T(8,128)(2,1)}) %reduce-scatter.3.cloned.1.call-update) | async-done | bytes 131088 | tf_op jit(solution)/shard_map/reduce_scatter | solution.py:314
  223.4 1.3 multiply_reduce_fusion
  224.9 4.2 %collective-permute-start.5 = (bf16[128,512]{1,0:T(8,128)(2,1)S(1)}, bf16[128,512]{1,0:T(8,128)(2,1)S(1)}, u32[]{:S(2)}, u32[]{:S(2)}) collective-permute-start(bf16[128,512]{1,0:T(8,128)(2,1)S(1)} %fusion.6), channel_id=1, source_target_pairs={{0,1},{1,0},{2,3},{3,2},{4,5},{5,4},{6,7},{7,6},{8,9},{9,8},{10,11... | collective-permute-start | bytes 393224 | tf_op jit(solution)/shard_map/ppermute | solution.py:44
  231.4 31.5 %all_to_all.20 = bf16[32,24,512]{2,1,0:T(8,128)(2,1)} all-to-all(bf16[32,24,512]{2,1,0:T(8,128)(2,1)S(1)} %bitcast.85), channel_id=1, replica_groups=mesh['grp'=8,'y'=8,'x'=4,'c'=2] {'y','x'}, dimensions={0} | all-to-all | bytes 1572864 | tf_op jit(solution)/shard_map/all_to_all | solution.py:337
  262.9 7.7 %expert_backward.1 = bf16[8,384,512]{2,1,0:T(8,128)(2,1)} custom-call(bf16[768,512]{1,0:T(8,128)(2,1)} %bitcast.84, bf16[768,512]{1,0:T(8,128)(2,1)} %bitcast.83, bf16[768,1024]{1,0:T(8,128)(2,1)} %get-tuple-element.32.hid_ref, bf16[768,1024]{1,0:T(8,128)(2,1)} %get-tuple-element.33.cg_ref, bf16[768,1024]{1,0:T(8,128)(2,1)} %get-tuple-element.34.cu_ref, ...), custom_call_target="tpu_custom_call" | custom-call | flops 3221225472 | bytes 7864320 | tf_op jit(solution)/shard_map/expert_backward/pallas_call | solution.py:206
  270.6 47.7 %reduce-scatter.5.cloned.1.call-done.in_ref = bf16[384,512]{1,0:T(8,128)(2,1)} async-done(((bf16[3072,512]{1,0:T(8,128)(2,1)}), bf16[384,512]{1,0:T(8,128)(2,1)}) %reduce-scatter.5.cloned.1.call-update) | async-done | bytes 393232 | tf_op jit(solution)/shard_map/reduce_scatter | solution.py:342
  318.3 1.9 unpack.1
  (50 shorter events, 8.6 us)
Async XLA Ops:
  8.0 157.1 %all-gather.4.cloned.1.call-start = ((), (), s32[]{:S(2)}) async-start(), calls=%async_computation.8 | async-start | bytes 3538944 | tf_op jit(solution)/shard_map/all_gather | solution.py:279
  11.3 68.7 %collective-permute-start = (f32[8,128]{1,0:T(8,128)S(1)}, f32[8,128]{1,0:T(8,128)S(1)}, u32[]{:S(2)}, u32[]{:S(2)}) collective-permute-start(f32[8,128]{1,0:T(8,128)S(1)} %pad_maximum_fusion.4), channel_id=1, source_target_pairs={{0,1},{1,0},{2,3},{3,2},{4,5},{5,4},{6,7},{7,6},{8,9},{9,8},{10,11... | collective-permute-start | bytes 12296 | tf_op jit(solution)/shard_map/ppermute | solution.py:44
  13.2 67.8 %collective-permute-start.1 = (bf16[128,512]{1,0:T(8,128)(2,1)}, bf16[128,512]{1,0:T(8,128)(2,1)S(1)}, u32[]{:S(2)}, u32[]{:S(2)}) collective-permute-start(bf16[128,512]{1,0:T(8,128)(2,1)} %param.10), channel_id=1, source_target_pairs={{0,1},{1,0},{2,3},{3,2},{4,5},{5,4},{6,7},{7,6},{8,9},{9,8},{10,11... | collective-permute-start | bytes 393224 | tf_op jit(solution)/shard_map/ppermute | solution.py:44
  67.4 14.9 %collective-permute-start.2 = (bf16[32,8,512]{2,1,0:T(8,128)(2,1)S(1)}, bf16[32,8,512]{2,1,0:T(8,128)(2,1)S(1)}, u32[]{:S(2)}, u32[]{:S(2)}) collective-permute-start(bf16[32,8,512]{2,1,0:T(8,128)(2,1)S(1)} %bitcast.91), channel_id=1, source_target_pairs={{0,1},{1,0},{2,3},{3,2},{4,5},{5,4},{6,7},{7,6},{8,9},{9,8},{10,11... | collective-permute-start | bytes 786440 | tf_op jit(solution)/shard_map/ppermute | solution.py:44
  74.9 5.1 %copy-start.3 = (f32[128,4]{0,1:T(4,128)S(1)}, f32[128,4]{0,1:T(4,128)}, u32[]{:S(2)}) copy-start(f32[128,4]{0,1:T(4,128)} %param.13) | copy-start | bytes 6148
  74.9 6.1 %copy-start.1 = (bf16[128,512]{1,0:T(8,128)(2,1)S(1)}, bf16[128,512]{1,0:T(8,128)(2,1)}, u32[]{:S(2)}) copy-start(bf16[128,512]{1,0:T(8,128)(2,1)} %param.10) | copy-start | bytes 393220
  74.9 27.4 %all-to-all-start = ((bf16[8,128,896]{2,1,0:T(8,128)(2,1)}), bf16[8,128,896]{2,1,0:T(8,128)(2,1)}, u32[]{:S(2)}, u32[]{:S(2)}) async-start(bf16[8,128,896]{2,1,0:T(8,128)(2,1)} %slice_features.1), calls=%async_computation | async-start | bytes 3670016 | tf_op jit(solution)/shard_map/all_to_all | solution.py:243
  82.3 26.7 %copy-start.5 = (bf16[112,512]{1,0:T(8,128)(2,1)S(1)}, bf16[112,512]{1,0:T(8,128)(2,1)}, u32[]{:S(2)}) copy-start(bf16[112,512]{1,0:T(8,128)(2,1)} %param.17) | copy-start | bytes 344068
  102.4 62.7 %all-to-all-start.1 = ((bf16[32,24,512]{2,1,0:T(8,128)(2,1)}), bf16[32,24,512]{2,1,0:T(8,128)(2,1)S(1)}, u32[]{:S(2)}, u32[]{:S(2)}) async-start(bf16[32,24,512]{2,1,0:T(8,128)(2,1)} %bitcast.13), calls=%async_computation.1 | async-start | bytes 1572864 | tf_op jit(solution)/shard_map/all_to_all | solution.py:310
  109.0 25.3 %collective-permute-start.3 = (bf16[112,512]{1,0:T(8,128)(2,1)S(1)}, bf16[112,512]{1,0:T(8,128)(2,1)S(1)}, u32[]{:S(2)}, u32[]{:S(2)}) collective-permute-start(bf16[112,512]{1,0:T(8,128)(2,1)S(1)} %copy-done.5), channel_id=1, source_target_pairs={{0,0},{1,8},{2,16},{3,24},{4,32},{5,40},{6,48},{7,56},{8,1},{9,9},... | collective-permute-start | bytes 344072 | tf_op jit(solution)/shard_map/ppermute | solution.py:249
  165.1 0.9 copy-start
  172.2 25.7 %all-to-all-start.2 = ((bf16[32,24,512]{2,1,0:T(8,128)(2,1)}), bf16[32,24,512]{2,1,0:T(8,128)(2,1)S(1)}, u32[]{:S(2)}, u32[]{:S(2)}) async-start(bf16[32,24,512]{2,1,0:T(8,128)(2,1)} %bitcast.93), calls=%async_computation.3 | async-start | bytes 1572864 | tf_op jit(solution)/shard_map/all_to_all | solution.py:319
  181.5 41.9 %reduce-scatter.3.cloned.1.call-start = ((), (), s32[]{:S(2)}) async-start(), calls=%async_computation.6 | async-start | bytes 1179648 | tf_op jit(solution)/shard_map/reduce_scatter | solution.py:314
  182.0 136.3 %reduce-scatter.5.cloned.1.call-start = ((), (), s32[]{:S(2)}) async-start(), calls=%async_computation.7 | async-start | bytes 3538944 | tf_op jit(solution)/shard_map/reduce_scatter | solution.py:342
  198.3 25.1 %copy-start.2 = (f32[512]{0:T(512)S(1)}, f32[512]{0:T(512)}, u32[]{:S(2)}) copy-start(f32[512]{0:T(512)} %param.19) | copy-start | bytes 6148
  198.7 24.6 %collective-permute-start.4 = (f32[128,512]{1,0:T(8,128)S(1)}, f32[128,512]{1,0:T(8,128)S(1)}, u32[]{:S(2)}, u32[]{:S(2)}) collective-permute-start(f32[128,512]{1,0:T(8,128)S(1)} %dynamic-slice_bitcast_fusion), channel_id=1, source_target_pairs={{0,1},{1,0},{2,3},{3,2},{4,5},{5,4},{6,7},{7,6},{8,9},{9,8},{10,11... | collective-permute-start | bytes 786440 | tf_op jit(solution)/shard_map/ppermute | solution.py:44
  224.7 6.3 %copy-start.4 = (f32[128]{0:T(128)}, f32[128]{0:T(128)S(1)}, u32[]{:S(2)}) copy-start(f32[128]{0:T(128)S(1)} %get-tuple-element.51) | copy-start | bytes 1540
  224.9 5.2 %collective-permute-start.5 = (bf16[128,512]{1,0:T(8,128)(2,1)S(1)}, bf16[128,512]{1,0:T(8,128)(2,1)S(1)}, u32[]{:S(2)}, u32[]{:S(2)}) collective-permute-start(bf16[128,512]{1,0:T(8,128)(2,1)S(1)} %fusion.6), channel_id=1, source_target_pairs={{0,1},{1,0},{2,3},{3,2},{4,5},{5,4},{6,7},{7,6},{8,9},{9,8},{10,11... | collective-permute-start | bytes 393224 | tf_op jit(solution)/shard_map/ppermute | solution.py:44
Sparse Core Ops, SparseCore 0:
  10.9 52.9 all-gather.3
  270.7 47.5 reduce-scatter.4
Sparse Core Ops, SparseCore 1:
  184.8 38.6 reduce-scatter.2

commit v4 on v3

--- a/solution.py
+++ b/solution.py
@@ -1,5 +1,4 @@
 import functools
-import math
 
 import jax
 import jax.numpy as jnp
@@ -11,7 +10,6 @@
 
 TOP = 4
 CHIPS = ("y", "x")
-ROW = ("x", "c")
 EP = ("y", "x", "c")
 BF = jnp.bfloat16
 F32 = jnp.float32
@@ -222,32 +220,134 @@
     )(droute, routed, hid, coef_gate, coef_up, full)
 
 
-def slice_kernel(in_ref, out_ref):
-    out_ref[0] = in_ref[...]
-
-
-def slice_features(teacher, side):
-    tok_dev, depth = teacher.shape
-    each = depth // side
-    return pl.pallas_call(
-        slice_kernel,
-        grid=(side,),
-        out_shape=jax.ShapeDtypeStruct((side, tok_dev, each), BF),
-        in_specs=[pl.BlockSpec((tok_dev, each), lambda i: (0, i))],
-        out_specs=pl.BlockSpec((1, tok_dev, each), lambda i: (i, 0, 0)),
-        name="slice_features",
-    )(teacher)
-
-
-def share_teacher(slices):
-    return lax.all_to_all(slices, ROW, split_axis=0, concat_axis=0, tiled=True)
-
-
-def share_critic(critic_teacher):
-    side = lax.axis_size("y")
-    turn = [(i * side + j, j * side + i) for i in range(side) for j in range(side)]
-    turned = lax.ppermute(critic_teacher, EP, turn)
-    return lax.all_gather(turned, "y", axis=0, tiled=True)
+def ring(block, axis):
+    count = lax.axis_size(axis)
+    pieces = [block] + [None] * (count - 1)
+    up = down = block
+    for step in range(1, count // 2 + 1):
+        up = shift(up, axis, 1)
+        pieces[step] = up
+        if 2 * step < count:
+            down = shift(down, axis, -1)
+            pieces[count - step] = down
+    return pieces
+
+
+def order_kernel(here_ref, *refs):
+    count = len(refs) - 1
+    for k in range(count):
+        refs[count][lax.rem(here_ref[0] - k + count, count)] = refs[k][...]
+
+
+def in_order(here, pieces):
+    return pl.pallas_call(
+        order_kernel,
+        out_shape=jax.ShapeDtypeStruct((len(pieces),) + pieces[0].shape, BF),
+        in_specs=[SMEM] + [VMEM] * len(pieces),
+        out_specs=VMEM,
+        name="in_order",
+    )(here, *pieces)
+
+
+def critic_kernel(
+    tall, here_ref, own_ref, other_ref, block, behind, ahead, low, high,
+    out_ref, student_ref, tokens, rows, sems, row_sems,
+):
+    tok_dev = own_ref.shape[0]
+    columns, deep = rows.shape[:2]
+    half = deep // 2
+    at = lambda k: lax.rem(here_ref[0] + k, columns)
+    copies = [
+        pltpu.make_async_copy(own_ref, tokens.at[pl.ds(0, tok_dev)], sems.at[0]),
+        pltpu.make_async_copy(other_ref, tokens.at[pl.ds(tok_dev, tok_dev)], sems.at[1]),
+        pltpu.make_async_copy(block, rows.at[at(0)], row_sems.at[0]),
+        pltpu.make_async_copy(behind, rows.at[at(3)], row_sems.at[1]),
+        pltpu.make_async_copy(ahead, rows.at[at(1)], row_sems.at[2]),
+        pltpu.make_async_copy(low, rows.at[at(2), pl.ds(0, half)], row_sems.at[3]),
+        pltpu.make_async_copy(high, rows.at[at(2), pl.ds(half, half)], row_sems.at[4]),
+    ]
+    for copy in copies:
+        copy.start()
+    for copy in copies:
+        copy.wait()
+    span = columns * tall
+    cols = rows.shape[3]
+    small = columns * (rows.shape[2] - tall)
+    total = jnp.zeros((2 * tok_dev, cols), F32)
+    for y in range(deep):
+        weights = rows[:, y, :tall].reshape(span, cols)
+        total += jnp.dot(
+            tokens[:, y * span : (y + 1) * span], weights, preferred_element_type=F32
+        )
+        student_ref[y * small : (y + 1) * small] = rows[:, y, tall:].reshape(small, cols)
+    out_ref[0] = total[:tok_dev]
+    out_ref[1] = total[tok_dev:]
+
+
+def critic_product(here, own, other, pieces, tall):
+    block = pieces[0]
+    deep, high, cols = block.shape
+    tok_dev, depth = own.shape
+    columns = 4
+    return pl.pallas_call(
+        functools.partial(critic_kernel, tall),
+        out_shape=[
+            jax.ShapeDtypeStruct((2, tok_dev, cols), F32),
+            jax.ShapeDtypeStruct((columns * deep * (high - tall), cols), BF),
+        ],
+        in_specs=[SMEM] + [ANY] * 7,
+        out_specs=[VMEM] * 2,
+        scratch_shapes=[
+            pltpu.VMEM((2 * tok_dev, depth), BF),
+            pltpu.VMEM((columns,) + block.shape, BF),
+            pltpu.SemaphoreType.DMA((2,)),
+            pltpu.SemaphoreType.DMA((5,)),
+        ],
+        cost_estimate=pl.CostEstimate(
+            flops=4 * tok_dev * depth * cols,
+            transcendentals=0,
+            bytes_accessed=4 * tok_dev * depth + 2 * depth * cols,
+        ),
+        name="critic_product",
+    )(here, own, other, *pieces)
+
+
+def columns_of(core, value, which):
+    size = value.shape[1] // 2
+    at = core if which == 0 else 1 - core
+    return lax.dynamic_slice_in_dim(value, at * size, size, axis=1)
+
+
+def side_by_side(core, own, other):
+    first = core == 0
+    return jnp.concatenate(
+        [jnp.where(first, own, other), jnp.where(first, other, own)], axis=1
+    )
+
+
+def critic_on_teacher(core, teacher, critic_teacher, critic_student):
+    shard = jnp.concatenate([critic_teacher, critic_student])
+    mine = columns_of(core, shard, 0)
+    got = swap(columns_of(core, shard, 1))
+    pair = both(core, mine, got)
+    depth, cols = critic_teacher.shape[0], pair.shape[2]
+    block = jnp.concatenate(
+        [pair[:, :depth].reshape(-1, cols), pair[:, depth:].reshape(-1, cols)]
+    )
+    other = swap(teacher)
+    place = lambda axis: lax.axis_index(axis).astype(jnp.int32).reshape(1)
+    column = in_order(place("y"), ring(block, "y"))
+    cut = column.shape[0] // 2
+    behind = shift(column, "x", 1)
+    ahead = shift(column, "x", -1)
+    low = shift(behind[:cut], "x", 1)
+    high = shift(ahead[cut:], "x", -1)
+    product, student = critic_product(
+        place("x"), teacher, other, [column, behind, ahead, low, high], 2 * depth
+    )
+    pre = side_by_side(core, product[0], swap(product[1]))
+    student = side_by_side(core, student, swap(student))
+    return pre, student
 
 
 def layer(
@@ -273,15 +373,11 @@
     rows_in = w_gate.shape[1]
 
     packed = pack_weights(w_gate[0], w_up[0], w_down[0])
-    packed, teacher, tokens, expert_ids, critic_student = lax.optimization_barrier(
-        (packed, teacher, tokens, expert_ids, critic_student)
+    packed, teacher, tokens, expert_ids = lax.optimization_barrier(
+        (packed, teacher, tokens, expert_ids)
     )
     full = lax.all_gather(packed, "grp", axis=0)
-    theirs = share_teacher(slice_features(teacher, lax.axis_size("y")))
-    student_half = lax.all_gather(critic_student, CHIPS, axis=0)
-    student_rows = (
-        both(core, student_half, swap(student_half)).transpose(1, 0, 2, 3).reshape(width, -1)
-    )
+    pre_teacher, student_rows = critic_on_teacher(core, teacher, critic_teacher, critic_student)
 
     meta = jnp.concatenate([expert_ids.T.astype(F32), route_weights.T])
     tok2 = both(core, tokens, swap(tokens)).reshape(2 * tok_dev, width)
@@ -306,13 +402,7 @@
     scaled_high, scaled_low = split(scaled)
 
     outbound = dot(pick, tok2).astype(BF).reshape(chips, 2 * capacity, width)
-    outbound, theirs, student_rows = lax.optimization_barrier((outbound, theirs, student_rows))
     inbound = lax.all_to_all(outbound, CHIPS, split_axis=0, concat_axis=0, tiled=True)
-    critic_rows = share_critic(critic_teacher)
-    product = dot(theirs.reshape(-1, theirs.shape[2]), critic_rows).astype(BF)
-    inbound, product = lax.optimization_barrier((inbound, product))
-    pre_teacher = lax.psum_scatter(product, ROW, scatter_dimension=0, tiled=True)
-    pre_teacher = pre_teacher.astype(F32)
     routed = inbound.reshape(slots, width)
 
     hidden, coef_gate, coef_up, expert_out = expert_forward(routed, full, rows_in)
@@ -348,8 +438,7 @@
 
 def solution(mesh):
     groups, members = mesh.devices.shape
-    side = math.isqrt(members)
-    fine = Mesh(mesh.devices.reshape(groups, side, side // 2, 2), ("grp",) + EP)
+    fine = Mesh(mesh.devices.reshape(groups, members // 8, 4, 2), ("grp",) + EP)
     rows = P(("grp",) + EP, None)
     weights = P(EP, "grp", None)
     critic = P(EP, None)

time: 329 us -> 244 us (0.74)
  the two profiles are of different devices: /device:TPU:6 before, /device:TPU:14 now
where the time goes in v4:
time: 244 us; the launch traced here: 243 us
  waiting for transfers between devices  87.7 us (36%)
  starting transfers between devices  72.1 us (30%)
  blocking collectives  31.5 us (13%)
  Pallas kernels  25.1 us (10%)
  between operations  14.7 us (6%)
  local copies, waits for them, and re-layouts  4.62 us (2%)
  matrix products  3.67 us (2%)
  other arithmetic  3.47 us (1%)
    ppermute x19, starting transfers between devices, shift(): lax.ppermute(value, axis, [(i, (i + step) % count) for i in range(count)])  51.7 us
    reduce_scatter x1, waiting for transfers between devices, layer(): lax.psum_scatter(parts.reshape(-1, width), 'grp', scatter_dimension=0, ti...  51.6 us
    ppermute x19, waiting for transfers between devices, shift(): lax.ppermute(value, axis, [(i, (i + step) % count) for i in range(count)])  36.1 us
    all_to_all x1, blocking collectives, layer(): lax.all_to_all(grad_out.reshape(chips, 2 * capacity, width), CHIPS, split...  31.5 us
    all_to_all x1, starting transfers between devices, layer(): lax.all_to_all(expert_out.reshape(chips, 2 * capacity, width), CHIPS, spl...  10.2 us
    all_to_all x1, starting transfers between devices, layer(): lax.all_to_all(outbound, CHIPS, split_axis=0, concat_axis=0, tiled=True)  10.1 us
    pallas_call x1, Pallas kernels, expert_backward(): pl.pallas_call(functools.partial(backward_kernel, rows), grid=(2,), out_s...  7.58 us
    pallas_call x1, Pallas kernels, expert_forward(): pl.pallas_call(functools.partial(forward_kernel, rows), grid=(slots // ti...  6.28 us
  transfers between devices with their start and end apart: 23, of which 12 were waited for; matrix products, arithmetic and copies ran while one was open for 3% of the time, Pallas kernels for 6%

profile of v4, /device:TPU:14, one launch (start us, length us, event | category | flops | bytes accessed | tf_op | source)
XLA Modules:
  0.0 242.8 jit_solution(15021200110260106286)
XLA Ops:
  12.4 2.4 collective-permute-start.15
  17.8 10.1 %all-to-all-start = ((bf16[32,24,512]{2,1,0:T(8,128)(2,1)}), bf16[32,24,512]{2,1,0:T(8,128)(2,1)S(1)}, u32[]{:S(2)}, u32[]{:S(2)}) async-start(bf16[32,24,512]{2,1,0:T(8,128)(2,1)} %bitcast.23), calls=%async_computation | async-start | bytes 1572864 | tf_op jit(solution)/shard_map/all_to_all | solution.py:405
  31.2 3.4 %collective-permute-start.3 = (bf16[240,256]{1,0:T(8,128)(2,1)S(1)}, bf16[240,256]{1,0:T(8,128)(2,1)S(1)}, u32[]{:S(2)}, u32[]{:S(2)}) collective-permute-start(bf16[240,256]{1,0:T(8,128)(2,1)S(1)} %pad_maximum_fusion.7.refs_0_), channel_id=1, source_target_pairs={{0,8},{8,16},{16,24},{24,32},{32,40},{40,48},{48,56},{56,0},{1,9},... | collective-permute-start | bytes 368648 | tf_op jit(solution)/shard_map/ppermute | solution.py:42
  34.6 2.5 %collective-permute-start.7 = (bf16[240,256]{1,0:T(8,128)(2,1)S(1)}, bf16[240,256]{1,0:T(8,128)(2,1)S(1)}, u32[]{:S(2)}, u32[]{:S(2)}) collective-permute-start(bf16[240,256]{1,0:T(8,128)(2,1)S(1)} %pad_maximum_fusion.7.refs_0_), channel_id=1, source_target_pairs={{0,56},{8,0},{16,8},{24,16},{32,24},{40,32},{48,40},{56,48},{1,57}... | collective-permute-start | bytes 368648 | tf_op jit(solution)/shard_map/ppermute | solution.py:42
  37.1 11.0 %collective-permute-done.3.refs_1_ = bf16[240,256]{1,0:T(8,128)(2,1)S(1)} collective-permute-done((bf16[240,256]{1,0:T(8,128)(2,1)S(1)}, bf16[240,256]{1,0:T(8,128)(2,1)S(1)}, u32[]{:S(2)}, u32[]{:S(2)}) %collective-permute-start.3) | collective-permute-done | bytes 122912 | tf_op jit(solution)/shard_map/ppermute | solution.py:42
  48.1 3.4 %collective-permute-start.4 = (bf16[240,256]{1,0:T(8,128)(2,1)S(1)}, bf16[240,256]{1,0:T(8,128)(2,1)S(1)}, u32[]{:S(2)}, u32[]{:S(2)}) collective-permute-start(bf16[240,256]{1,0:T(8,128)(2,1)S(1)} %collective-permute-done.3.refs_1_), channel_id=1, source_target_pairs={{0,8},{8,16},{16,24},{24,32},{32,40},{40,48},{48,56},{56,0},{1,9},... | collective-permute-start | bytes 368648 | tf_op jit(solution)/shard_map/ppermute | solution.py:42
  53.4 3.2 %collective-permute-start.8 = (bf16[240,256]{1,0:T(8,128)(2,1)S(1)}, bf16[240,256]{1,0:T(8,128)(2,1)S(1)}, u32[]{:S(2)}, u32[]{:S(2)}) collective-permute-start(bf16[240,256]{1,0:T(8,128)(2,1)S(1)} %collective-permute-done.7.refs_7_), channel_id=1, source_target_pairs={{0,56},{8,0},{16,8},{24,16},{32,24},{40,32},{48,40},{56,48},{1,57}... | collective-permute-start | bytes 368648 | tf_op jit(solution)/shard_map/ppermute | solution.py:42
  56.7 2.6 %collective-permute-start.5 = (bf16[240,256]{1,0:T(8,128)(2,1)S(1)}, bf16[240,256]{1,0:T(8,128)(2,1)S(1)}, u32[]{:S(2)}, u32[]{:S(2)}) collective-permute-start(bf16[240,256]{1,0:T(8,128)(2,1)S(1)} %collective-permute-done.4.refs_2_), channel_id=1, source_target_pairs={{0,8},{8,16},{16,24},{24,32},{32,40},{40,48},{48,56},{56,0},{1,9},... | collective-permute-start | bytes 368648 | tf_op jit(solution)/shard_map/ppermute | solution.py:42
  61.0 4.0 %collective-permute-start.9 = (bf16[240,256]{1,0:T(8,128)(2,1)S(1)}, bf16[240,256]{1,0:T(8,128)(2,1)S(1)}, u32[]{:S(2)}, u32[]{:S(2)}) collective-permute-start(bf16[240,256]{1,0:T(8,128)(2,1)S(1)} %collective-permute-done.8.refs_6_), channel_id=1, source_target_pairs={{0,56},{8,0},{16,8},{24,16},{32,24},{40,32},{48,40},{56,48},{1,57}... | collective-permute-start | bytes 368648 | tf_op jit(solution)/shard_map/ppermute | solution.py:42
  65.5 2.1 collective-permute-start.6
  69.1 4.4 %collective-permute-done.6.refs_4_ = bf16[240,256]{1,0:T(8,128)(2,1)S(1)} collective-permute-done((bf16[240,256]{1,0:T(8,128)(2,1)S(1)}, bf16[240,256]{1,0:T(8,128)(2,1)S(1)}, u32[]{:S(2)}, u32[]{:S(2)}) %collective-permute-start.6) | collective-permute-done | bytes 122912 | tf_op jit(solution)/shard_map/ppermute | solution.py:42
  74.1 2.3 in_order.1.block
  76.4 2.7 %collective-permute-start.11 = (bf16[8,240,256]{2,1,0:T(8,128)(2,1)}, bf16[8,240,256]{2,1,0:T(8,128)(2,1)}, u32[]{:S(2)}, u32[]{:S(2)}) collective-permute-start(bf16[8,240,256]{2,1,0:T(8,128)(2,1)} %in_order.1.block), channel_id=1, source_target_pairs={{0,6},{2,0},{4,2},{6,4},{1,7},{3,1},{5,3},{7,5},{8,14},{10,8},{12,... | collective-permute-start | bytes 2949128 | tf_op jit(solution)/shard_map/ppermute | solution.py:42
  79.2 4.3 %collective-permute-start.10 = (bf16[8,240,256]{2,1,0:T(8,128)(2,1)}, bf16[8,240,256]{2,1,0:T(8,128)(2,1)}, u32[]{:S(2)}, u32[]{:S(2)}) collective-permute-start(bf16[8,240,256]{2,1,0:T(8,128)(2,1)} %in_order.1.block), channel_id=1, source_target_pairs={{0,2},{2,4},{4,6},{6,0},{1,3},{3,5},{5,7},{7,1},{8,10},{10,12},{12... | collective-permute-start | bytes 2949128 | tf_op jit(solution)/shard_map/ppermute | solution.py:42
  84.4 6.3 %expert_forward.1 = (bf16[768,1024]{1,0:T(8,128)(2,1)}, bf16[768,1024]{1,0:T(8,128)(2,1)}, bf16[768,1024]{1,0:T(8,128)(2,1)}, bf16[768,512]{1,0:T(8,128)(2,1)}) custom-call(bf16[768,512]{1,0:T(8,128)(2,1)} %bitcast.79, bf16[8,384,512]{2,1,0:T(8,128)(2,1)} %bitcast.83), custom_call_target="tpu_custom_call" | custom-call | flops 2415919104 | bytes 7864320 | tf_op jit(solution)/shard_map/expert_forward/pallas_call | solution.py:134
  90.7 10.2 %all-to-all-start.1 = ((bf16[32,24,512]{2,1,0:T(8,128)(2,1)}), bf16[32,24,512]{2,1,0:T(8,128)(2,1)S(1)}, u32[]{:S(2)}, u32[]{:S(2)}) async-start(bf16[32,24,512]{2,1,0:T(8,128)(2,1)} %bitcast.89), calls=%async_computation.1 | async-start | bytes 1572864 | tf_op jit(solution)/shard_map/all_to_all | solution.py:409
  100.9 2.7 %collective-permute-done.11.ahead = bf16[8,240,256]{2,1,0:T(8,128)(2,1)} collective-permute-done((bf16[8,240,256]{2,1,0:T(8,128)(2,1)}, bf16[8,240,256]{2,1,0:T(8,128)(2,1)}, u32[]{:S(2)}, u32[]{:S(2)}) %collective-permute-start.11) | collective-permute-done | bytes 983072 | tf_op jit(solution)/shard_map/ppermute | solution.py:42
  107.8 5.2 %collective-permute-start.12 = (bf16[4,240,256]{2,1,0:T(8,128)(2,1)S(1)}, bf16[4,240,256]{2,1,0:T(8,128)(2,1)}, u32[]{:S(2)}, u32[]{:S(2)}) collective-permute-start(bf16[4,240,256]{2,1,0:T(8,128)(2,1)S(1)} %slice.36), channel_id=1, source_target_pairs={{0,2},{2,4},{4,6},{6,0},{1,3},{3,5},{5,7},{7,1},{8,10},{10,12},{12... | collective-permute-start | bytes 1474568 | tf_op jit(solution)/shard_map/ppermute | solution.py:42
  113.0 8.9 %collective-permute-done.13.high = bf16[4,240,256]{2,1,0:T(8,128)(2,1)S(1)} collective-permute-done((bf16[4,240,256]{2,1,0:T(8,128)(2,1)S(1)}, bf16[4,240,256]{2,1,0:T(8,128)(2,1)S(1)}, u32[]{:S(2)}, u32[]{:S(2)}) %collective-permute-start.13) | collective-permute-done | bytes 491552 | tf_op jit(solution)/shard_map/ppermute | solution.py:42
  123.4 5.2 %critic_product.1 = (f32[2,128,256]{2,1,0:T(8,128)}, bf16[512,256]{1,0:T(8,128)(2,1)}) custom-call(s32[1]{0:T(128)} %bitcast.10.here_ref, bf16[128,7168]{1,0:T(8,128)(2,1)} %own_ref, bf16[128,7168]{1,0:T(8,128)(2,1)} %collective-permute-done.1.other_ref, bf16[8,240,256]{2,1,0:T(8,128)(2,1)} %in_order.1.block, ...), custom_call_target="tpu_custom_call" | custom-call | flops 939524096 | bytes 7340032 | tf_op jit(solution)/shard_map/critic_product/pallas_call | solution.py:292
  131.5 2.4 collective-permute-start.17
  143.4 31.5 %all_to_all.15 = bf16[32,24,512]{2,1,0:T(8,128)(2,1)} all-to-all(bf16[32,24,512]{2,1,0:T(8,128)(2,1)S(1)} %bitcast.82), channel_id=1, replica_groups=mesh['grp'=8,'y'=8,'x'=4,'c'=2] {'y','x'}, dimensions={0} | all-to-all | bytes 1572864 | tf_op jit(solution)/shard_map/all_to_all | solution.py:427
  174.9 7.6 %expert_backward.1 = bf16[8,384,512]{2,1,0:T(8,128)(2,1)} custom-call(bf16[768,512]{1,0:T(8,128)(2,1)} %bitcast.81, bf16[768,512]{1,0:T(8,128)(2,1)} %bitcast.80, bf16[768,1024]{1,0:T(8,128)(2,1)} %get-tuple-element.24.hid_ref, bf16[768,1024]{1,0:T(8,128)(2,1)} %get-tuple-element.25.cg_ref, bf16[768,1024]{1,0:T(8,128)(2,1)} %get-tuple-element.26.cu_ref, ...), custom_call_target="tpu_custom_call" | custom-call | flops 3221225472 | bytes 7864320 | tf_op jit(solution)/shard_map/expert_backward/pallas_call | solution.py:204
  182.5 51.6 %reduce-scatter.2.cloned.1.call-done.in_ref = bf16[384,512]{1,0:T(8,128)(2,1)} async-done(((bf16[3072,512]{1,0:T(8,128)(2,1)}), bf16[384,512]{1,0:T(8,128)(2,1)}) %reduce-scatter.2.cloned.1.call-update) | async-done | bytes 393232 | tf_op jit(solution)/shard_map/reduce_scatter | solution.py:432
  (101 shorter events, 38.2 us)
Async XLA Ops:
  7.2 76.4 %all-gather.3.cloned.1.call-start = ((), (), s32[]{:S(2)}) async-start(), calls=%async_computation.5 | async-start | bytes 3538944 | tf_op jit(solution)/shard_map/all_gather | solution.py:379
  10.5 4.4 %collective-permute-start = (f32[8,128]{1,0:T(8,128)S(1)}, f32[8,128]{1,0:T(8,128)S(1)}, u32[]{:S(2)}, u32[]{:S(2)}) collective-permute-start(f32[8,128]{1,0:T(8,128)S(1)} %pad_maximum_fusion.10), channel_id=1, source_target_pairs={{0,1},{1,0},{2,3},{3,2},{4,5},{5,4},{6,7},{7,6},{8,9},{9,8},{10,11... | collective-permute-start | bytes 12296 | tf_op jit(solution)/shard_map/ppermute | solution.py:42
  12.4 4.1 %collective-permute-start.15 = (bf16[128,512]{1,0:T(8,128)(2,1)}, bf16[128,512]{1,0:T(8,128)(2,1)S(1)}, u32[]{:S(2)}, u32[]{:S(2)}) collective-permute-start(bf16[128,512]{1,0:T(8,128)(2,1)} %param.10), channel_id=1, source_target_pairs={{0,1},{1,0},{2,3},{3,2},{4,5},{5,4},{6,7},{7,6},{8,9},{9,8},{10,11... | collective-permute-start | bytes 393224 | tf_op jit(solution)/shard_map/ppermute | solution.py:42
  17.8 65.7 %all-to-all-start = ((bf16[32,24,512]{2,1,0:T(8,128)(2,1)}), bf16[32,24,512]{2,1,0:T(8,128)(2,1)S(1)}, u32[]{:S(2)}, u32[]{:S(2)}) async-start(bf16[32,24,512]{2,1,0:T(8,128)(2,1)} %bitcast.23), calls=%async_computation | async-start | bytes 1572864 | tf_op jit(solution)/shard_map/all_to_all | solution.py:405
  28.0 3.1 %collective-permute-start.2 = (bf16[120,256]{1,0:T(8,128)(2,1)S(1)}, bf16[120,256]{1,0:T(8,128)(2,1)S(1)}, u32[]{:S(2)}, u32[]{:S(2)}) collective-permute-start(bf16[120,256]{1,0:T(8,128)(2,1)S(1)} %constant_dynamic-slice_fusion), channel_id=1, source_target_pairs={{0,1},{1,0},{2,3},{3,2},{4,5},{5,4},{6,7},{7,6},{8,9},{9,8},{10,11... | collective-permute-start | bytes 184328 | tf_op jit(solution)/shard_map/ppermute | solution.py:42
  31.2 42.3 %copy-start.1 = (bf16[240,256]{1,0:T(8,128)(2,1)}, bf16[240,256]{1,0:T(8,128)(2,1)S(1)}, u32[]{:S(2)}) copy-start(bf16[240,256]{1,0:T(8,128)(2,1)S(1)} %pad_maximum_fusion.7.refs_0_) | copy-start | bytes 368644
  31.2 16.9 %collective-permute-start.3 = (bf16[240,256]{1,0:T(8,128)(2,1)S(1)}, bf16[240,256]{1,0:T(8,128)(2,1)S(1)}, u32[]{:S(2)}, u32[]{:S(2)}) collective-permute-start(bf16[240,256]{1,0:T(8,128)(2,1)S(1)} %pad_maximum_fusion.7.refs_0_), channel_id=1, source_target_pairs={{0,8},{8,16},{16,24},{24,32},{32,40},{40,48},{48,56},{56,0},{1,9},... | collective-permute-start | bytes 368648 | tf_op jit(solution)/shard_map/ppermute | solution.py:42
  34.6 18.8 %collective-permute-start.7 = (bf16[240,256]{1,0:T(8,128)(2,1)S(1)}, bf16[240,256]{1,0:T(8,128)(2,1)S(1)}, u32[]{:S(2)}, u32[]{:S(2)}) collective-permute-start(bf16[240,256]{1,0:T(8,128)(2,1)S(1)} %pad_maximum_fusion.7.refs_0_), channel_id=1, source_target_pairs={{0,56},{8,0},{16,8},{24,16},{32,24},{40,32},{48,40},{56,48},{1,57}... | collective-permute-start | bytes 368648 | tf_op jit(solution)/shard_map/ppermute | solution.py:42
  48.1 8.6 %collective-permute-start.4 = (bf16[240,256]{1,0:T(8,128)(2,1)S(1)}, bf16[240,256]{1,0:T(8,128)(2,1)S(1)}, u32[]{:S(2)}, u32[]{:S(2)}) collective-permute-start(bf16[240,256]{1,0:T(8,128)(2,1)S(1)} %collective-permute-done.3.refs_1_), channel_id=1, source_target_pairs={{0,8},{8,16},{16,24},{24,32},{32,40},{40,48},{48,56},{56,0},{1,9},... | collective-permute-start | bytes 368648 | tf_op jit(solution)/shard_map/ppermute | solution.py:42
  51.5 61.5 %collective-permute-start.1 = (bf16[128,7168]{1,0:T(8,128)(2,1)}, bf16[128,7168]{1,0:T(8,128)(2,1)}, u32[]{:S(2)}, u32[]{:S(2)}) collective-permute-start(bf16[128,7168]{1,0:T(8,128)(2,1)} %own_ref), channel_id=1, source_target_pairs={{0,1},{1,0},{2,3},{3,2},{4,5},{5,4},{6,7},{7,6},{8,9},{9,8},{10,11... | collective-permute-start | bytes 5505032 | tf_op jit(solution)/shard_map/ppermute | solution.py:42
  53.4 7.6 %collective-permute-start.8 = (bf16[240,256]{1,0:T(8,128)(2,1)S(1)}, bf16[240,256]{1,0:T(8,128)(2,1)S(1)}, u32[]{:S(2)}, u32[]{:S(2)}) collective-permute-start(bf16[240,256]{1,0:T(8,128)(2,1)S(1)} %collective-permute-done.7.refs_7_), channel_id=1, source_target_pairs={{0,56},{8,0},{16,8},{24,16},{32,24},{40,32},{48,40},{56,48},{1,57}... | collective-permute-start | bytes 368648 | tf_op jit(solution)/shard_map/ppermute | solution.py:42
  56.7 8.8 %collective-permute-start.5 = (bf16[240,256]{1,0:T(8,128)(2,1)S(1)}, bf16[240,256]{1,0:T(8,128)(2,1)S(1)}, u32[]{:S(2)}, u32[]{:S(2)}) collective-permute-start(bf16[240,256]{1,0:T(8,128)(2,1)S(1)} %collective-permute-done.4.refs_2_), channel_id=1, source_target_pairs={{0,8},{8,16},{16,24},{24,32},{32,40},{40,48},{48,56},{56,0},{1,9},... | collective-permute-start | bytes 368648 | tf_op jit(solution)/shard_map/ppermute | solution.py:42
  61.0 8.1 %collective-permute-start.9 = (bf16[240,256]{1,0:T(8,128)(2,1)S(1)}, bf16[240,256]{1,0:T(8,128)(2,1)S(1)}, u32[]{:S(2)}, u32[]{:S(2)}) collective-permute-start(bf16[240,256]{1,0:T(8,128)(2,1)S(1)} %collective-permute-done.8.refs_6_), channel_id=1, source_target_pairs={{0,56},{8,0},{16,8},{24,16},{32,24},{40,32},{48,40},{56,48},{1,57}... | collective-permute-start | bytes 368648 | tf_op jit(solution)/shard_map/ppermute | solution.py:42
  65.5 8.0 %collective-permute-start.6 = (bf16[240,256]{1,0:T(8,128)(2,1)S(1)}, bf16[240,256]{1,0:T(8,128)(2,1)S(1)}, u32[]{:S(2)}, u32[]{:S(2)}) collective-permute-start(bf16[240,256]{1,0:T(8,128)(2,1)S(1)} %collective-permute-done.5.refs_3_), channel_id=1, source_target_pairs={{0,8},{8,16},{16,24},{24,32},{32,40},{40,48},{48,56},{56,0},{1,9},... | collective-permute-start | bytes 368648 | tf_op jit(solution)/shard_map/ppermute | solution.py:42
  76.4 27.3 %collective-permute-start.11 = (bf16[8,240,256]{2,1,0:T(8,128)(2,1)}, bf16[8,240,256]{2,1,0:T(8,128)(2,1)}, u32[]{:S(2)}, u32[]{:S(2)}) collective-permute-start(bf16[8,240,256]{2,1,0:T(8,128)(2,1)} %in_order.1.block), channel_id=1, source_target_pairs={{0,6},{2,0},{4,2},{6,4},{1,7},{3,1},{5,3},{7,5},{8,14},{10,8},{12,... | collective-permute-start | bytes 2949128 | tf_op jit(solution)/shard_map/ppermute | solution.py:42
  79.2 27.5 %collective-permute-start.10 = (bf16[8,240,256]{2,1,0:T(8,128)(2,1)}, bf16[8,240,256]{2,1,0:T(8,128)(2,1)}, u32[]{:S(2)}, u32[]{:S(2)}) collective-permute-start(bf16[8,240,256]{2,1,0:T(8,128)(2,1)} %in_order.1.block), channel_id=1, source_target_pairs={{0,2},{2,4},{4,6},{6,0},{1,3},{3,5},{5,7},{7,1},{8,10},{10,12},{12... | collective-permute-start | bytes 2949128 | tf_op jit(solution)/shard_map/ppermute | solution.py:42
  90.7 43.2 %all-to-all-start.1 = ((bf16[32,24,512]{2,1,0:T(8,128)(2,1)}), bf16[32,24,512]{2,1,0:T(8,128)(2,1)S(1)}, u32[]{:S(2)}, u32[]{:S(2)}) async-start(bf16[32,24,512]{2,1,0:T(8,128)(2,1)} %bitcast.89), calls=%async_computation.1 | async-start | bytes 1572864 | tf_op jit(solution)/shard_map/all_to_all | solution.py:409
  100.9 133.1 %reduce-scatter.2.cloned.1.call-start = ((), (), s32[]{:S(2)}) async-start(), calls=%async_computation.4 | async-start | bytes 3538944 | tf_op jit(solution)/shard_map/reduce_scatter | solution.py:432
  104.8 17.2 %collective-permute-start.13 = (bf16[4,240,256]{2,1,0:T(8,128)(2,1)S(1)}, bf16[4,240,256]{2,1,0:T(8,128)(2,1)S(1)}, u32[]{:S(2)}, u32[]{:S(2)}) collective-permute-start(bf16[4,240,256]{2,1,0:T(8,128)(2,1)S(1)} %slice.37), channel_id=1, source_target_pairs={{0,6},{2,0},{4,2},{6,4},{1,7},{3,1},{5,3},{7,5},{8,14},{10,8},{12,... | collective-permute-start | bytes 1474568 | tf_op jit(solution)/shard_map/ppermute | solution.py:42
  107.8 15.7 %collective-permute-start.12 = (bf16[4,240,256]{2,1,0:T(8,128)(2,1)S(1)}, bf16[4,240,256]{2,1,0:T(8,128)(2,1)}, u32[]{:S(2)}, u32[]{:S(2)}) collective-permute-start(bf16[4,240,256]{2,1,0:T(8,128)(2,1)S(1)} %slice.36), channel_id=1, source_target_pairs={{0,2},{2,4},{4,6},{6,0},{1,3},{3,5},{5,7},{7,1},{8,10},{10,12},{12... | collective-permute-start | bytes 1474568 | tf_op jit(solution)/shard_map/ppermute | solution.py:42
  129.5 7.2 %collective-permute-start.14 = (f32[128,256]{1,0:T(8,128)S(1)}, f32[128,256]{1,0:T(8,128)S(1)}, u32[]{:S(2)}, u32[]{:S(2)}) collective-permute-start(f32[128,256]{1,0:T(8,128)S(1)} %slice_bitcast_fusion), channel_id=1, source_target_pairs={{0,1},{1,0},{2,3},{3,2},{4,5},{5,4},{6,7},{7,6},{8,9},{9,8},{10,11... | collective-permute-start | bytes 393224 | tf_op jit(solution)/shard_map/ppermute | solution.py:42
  131.5 5.3 %collective-permute-start.17 = (bf16[512,256]{1,0:T(8,128)(2,1)}, bf16[512,256]{1,0:T(8,128)(2,1)S(1)}, u32[]{:S(2)}, u32[]{:S(2)}) collective-permute-start(bf16[512,256]{1,0:T(8,128)(2,1)} %get-tuple-element.23), channel_id=1, source_target_pairs={{0,1},{1,0},{2,3},{3,2},{4,5},{5,4},{6,7},{7,6},{8,9},{9,8},{10,11... | collective-permute-start | bytes 786440 | tf_op jit(solution)/shard_map/ppermute | solution.py:42
  134.8 3.4 %collective-permute-start.16 = (f32[128,512]{1,0:T(8,128)S(1)}, f32[128,512]{1,0:T(8,128)S(1)}, u32[]{:S(2)}, u32[]{:S(2)}) collective-permute-start(f32[128,512]{1,0:T(8,128)S(1)} %dynamic-slice_bitcast_fusion), channel_id=1, source_target_pairs={{0,1},{1,0},{2,3},{3,2},{4,5},{5,4},{6,7},{7,6},{8,9},{9,8},{10,11... | collective-permute-start | bytes 786440 | tf_op jit(solution)/shard_map/ppermute | solution.py:42
  138.8 3.2 %collective-permute-start.18 = (bf16[128,512]{1,0:T(8,128)(2,1)S(1)}, bf16[128,512]{1,0:T(8,128)(2,1)S(1)}, u32[]{:S(2)}, u32[]{:S(2)}) collective-permute-start(bf16[128,512]{1,0:T(8,128)(2,1)S(1)} %fusion.8), channel_id=1, source_target_pairs={{0,1},{1,0},{2,3},{3,2},{4,5},{5,4},{6,7},{7,6},{8,9},{9,8},{10,11... | collective-permute-start | bytes 393224 | tf_op jit(solution)/shard_map/ppermute | solution.py:42
  (16 other events, 135.1 us)
Sparse Core Ops, SparseCore 0:
  10.1 52.8 all-gather.2
  182.6 51.3 reduce-scatter.1

commit v5 on v2

--- a/solution.py
+++ b/solution.py
@@ -122,9 +122,9 @@
     return copies
 
 
-def forward_kernel(count, rows, here_ref, routed_ref, *refs):
+def forward_kernel(count, rows, chunk, here_ref, inbound_ref, *refs):
     pieces = refs[:count]
-    hid_ref, coef_gate_ref, coef_up_ref, out_ref, full, sems = refs[count:]
+    hid_ref, coef_gate_ref, coef_up_ref, out_ref, down_ref, full, sems = refs[count:]
 
     @pl.when(pl.program_id(0) == 0)
     def _():
@@ -133,10 +133,11 @@
             copy.start()
         for copy in copies:
             copy.wait()
-
-    width = routed_ref.shape[1]
+        down_ref[...] = full[:, 4 * rows :]
+
+    tile, width = out_ref.shape
     half = full.shape[2]
-    routed = routed_ref[...]
+    routed = inbound_ref[:, :chunk].reshape(tile, width)
     out = jnp.zeros(out_ref.shape, F32)
     for part in range(2):
         gate_w = full[:, part * rows : (part + 1) * rows].reshape(width, half)
@@ -156,19 +157,35 @@
     out_ref[...] = out.astype(BF)
 
 
-def expert_forward(here, routed, pieces, rows, tile=384):
+def expert_forward(here, inbound, pieces, rows, chunk, steps=2):
     count = len(pieces)
-    slots, width = routed.shape
-    half = pieces[0].shape[1]
+    chips, taken, width = inbound.shape
+    slots = chips * chunk
+    tile = slots // steps
+    high, half = pieces[0].shape
+    down = (count, high - 4 * rows, half)
     hidden = 2 * half
     block = lambda cols: pl.BlockSpec((tile, cols), lambda i: (i, 0))
     wide = jax.ShapeDtypeStruct((slots, hidden), BF)
     return pl.pallas_call(
-        functools.partial(forward_kernel, count, rows),
-        grid=(slots // tile,),
-        out_shape=[wide, wide, wide, jax.ShapeDtypeStruct((slots, width), BF)],
-        in_specs=[SMEM, block(width)] + [ANY] * count,
-        out_specs=[block(hidden), block(hidden), block(hidden), block(width)],
+        functools.partial(forward_kernel, count, rows, chunk),
+        grid=(steps,),
+        out_shape=[
+            wide,
+            wide,
+            wide,
+            jax.ShapeDtypeStruct((slots, width), BF),
+            jax.ShapeDtypeStruct(down, BF),
+        ],
+        in_specs=[SMEM, pl.BlockSpec((chips // steps, taken, width), lambda i: (i, 0, 0))]
+        + [ANY] * count,
+        out_specs=[
+            block(hidden),
+            block(hidden),
+            block(hidden),
+            block(width),
+            pl.BlockSpec(down, lambda i: (0, 0, 0)),
+        ],
         scratch_shapes=[
             pltpu.VMEM((count,) + pieces[0].shape, BF),
             pltpu.SemaphoreType.DMA((count,)),
@@ -179,28 +196,21 @@
             bytes_accessed=6 * slots * hidden + 6 * width * hidden,
         ),
         name="expert_forward",
-    )(here, routed, *pieces)
-
-
-def backward_kernel(count, rows, here_ref, droute_ref, routed_ref, hid_ref, cg_ref, cu_ref, *refs):
-    pieces = refs[:count]
-    out_ref, down, parts, sems, out_sems = refs[count:]
+    )(here, inbound, *pieces)
+
+
+def backward_kernel(
+    rows, chunk, droute_ref, inbound_ref, hid_ref, cg_ref, cu_ref, down, out_ref, parts, out_sems
+):
     step = pl.program_id(0)
-    width, half = routed_ref.shape[1], hid_ref.shape[1]
+    slots, width = droute_ref.shape
+    half = hid_ref.shape[1]
+    count = out_ref.shape[0]
     each = down.shape[1]
     take = count // 2
-
-    @pl.when(step == 0)
-    def _():
-        copies = fetch(count, here_ref, pieces, down, sems, 4 * rows)
-        for copy in copies:
-            copy.start()
-        for copy in copies:
-            copy.wait()
-
     droute = droute_ref[...]
-    routed = routed_ref[...]
-    down_w = down[pl.ds(step * take, take)].reshape(half, width)
+    routed = inbound_ref[:, :chunk].reshape(slots, width)
+    down_w = down[...].reshape(half, width)
     dhid = lax.dot_general(droute, down_w, (((1,), (1,)), ((), ())), preferred_element_type=F32)
     dgate = (dhid * cg_ref[...].astype(F32)).astype(BF)
     dup = (dhid * cu_ref[...].astype(F32)).astype(BF)
@@ -236,23 +246,27 @@
                 copy.wait()
 
 
-def expert_backward(here, droute, routed, hid, coef_gate, coef_up, pieces, rows):
-    count = len(pieces)
-    slots, width = routed.shape
+def expert_backward(droute, inbound, hid, coef_gate, coef_up, down, rows, chunk):
+    slots, width = droute.shape
     hidden = hid.shape[1]
-    whole = pl.BlockSpec((slots, width), lambda i: (0, 0))
     block = pl.BlockSpec((slots, hidden // 2), lambda i: (0, i))
-    shape = (count,) + pieces[0].shape
+    count, each = down.shape[:2]
+    shape = (count, 4 * rows + each, width)
     return pl.pallas_call(
-        functools.partial(backward_kernel, count, rows),
+        functools.partial(backward_kernel, rows, chunk),
         grid=(2,),
         out_shape=jax.ShapeDtypeStruct(shape, BF),
-        in_specs=[SMEM, whole, whole, block, block, block] + [ANY] * count,
+        in_specs=[
+            pl.BlockSpec((slots, width), lambda i: (0, 0)),
+            pl.BlockSpec(inbound.shape, lambda i: (0, 0, 0)),
+            block,
+            block,
+            block,
+            pl.BlockSpec((count // 2, each, width), lambda i: (i, 0, 0)),
+        ],
         out_specs=ANY,
         scratch_shapes=[
-            pltpu.VMEM((count, shape[1] - 4 * rows, width), BF),
             pltpu.VMEM(shape, BF),
-            pltpu.SemaphoreType.DMA((count,)),
             pltpu.SemaphoreType.DMA((6,)),
         ],
         cost_estimate=pl.CostEstimate(
@@ -261,7 +275,7 @@
             bytes_accessed=6 * slots * hidden + 6 * width * hidden,
         ),
         name="expert_backward",
-    )(here, droute, routed, hid, coef_gate, coef_up, *pieces)
+    )(droute, inbound, hid, coef_gate, coef_up, down)
 
 
 def layer(
@@ -318,13 +332,15 @@
         [outbound, jnp.broadcast_to(critic_student[None], (chips, rows_st, width))], axis=1
     )
     inbound = lax.all_to_all(outbound, "yx", split_axis=0, concat_axis=0, tiled=True)
-    routed = inbound[:, : 2 * capacity].reshape(slots, width)
     student_half = inbound[:, 2 * capacity :]
+    student_other = swap(student_half)
     student_rows = (
-        both(core, student_half, swap(student_half)).transpose(1, 0, 2, 3).reshape(width, -1)
-    )
-
-    hidden, coef_gate, coef_up, expert_out = expert_forward(here, routed, pieces, rows_in)
+        both(core, student_half, student_other).transpose(1, 0, 2, 3).reshape(width, -1)
+    )
+
+    hidden, coef_gate, coef_up, expert_out, down_w = expert_forward(
+        here, inbound, pieces, rows_in, 2 * capacity
+    )
     returned = lax.all_to_all(
         expert_out.reshape(chips, 2 * capacity, width),
         "yx",
@@ -352,7 +368,9 @@
         grad_out.reshape(chips, 2 * capacity, width), "yx", split_axis=0, concat_axis=0, tiled=True
     ).reshape(slots, width)
 
-    parts = expert_backward(here, droute, routed, hidden, coef_gate, coef_up, pieces, rows_in)
+    parts = expert_backward(
+        droute, inbound, hidden, coef_gate, coef_up, down_w, rows_in, 2 * capacity
+    )
     total = lax.psum_scatter(
         parts.reshape(-1, width), "grp", scatter_dimension=0, tiled=True
     )

time: 229 us -> 229 us (level)
  the two profiles are of different devices: /device:TPU:10 before, /device:TPU:4 now
where the time goes in v5:
time: 229 us; the launch traced here: 228 us
  waiting for transfers between devices  89.3 us (39%)
  starting transfers between devices  59.7 us (26%)
  blocking collectives  28.4 us (12%)
  Pallas kernels  19.3 us (8%)
  between operations  14.5 us (6%)
  matrix products  6.96 us (3%)
  other arithmetic  6.62 us (3%)
  local copies, waits for them, and re-layouts  3.4 us (1%)
    reduce_scatter x1, waiting for transfers between devices, layer(): lax.psum_scatter(parts.reshape(-1, width), 'grp', scatter_dimension=0, ti...  43.8 us
    ppermute x12, starting transfers between devices, shift(): lax.ppermute(value, axis, [(i, (i + step) % count) for i in range(count)])  39.5 us
    ppermute x12, waiting for transfers between devices, shift(): lax.ppermute(value, axis, [(i, (i + step) % count) for i in range(count)])  32.9 us
    all_to_all x1, blocking collectives, layer(): lax.all_to_all(grad_out.reshape(chips, 2 * capacity, width), 'yx', split_...  28.4 us
    all_to_all x1, waiting for transfers between devices, layer(): lax.all_to_all(expert_out.reshape(chips, 2 * capacity, width), 'yx', spli...  11.9 us
    all_to_all x1, starting transfers between devices, layer(): lax.all_to_all(outbound, 'yx', split_axis=0, concat_axis=0, tiled=True)  10.3 us
    all_to_all x1, starting transfers between devices, layer(): lax.all_to_all(expert_out.reshape(chips, 2 * capacity, width), 'yx', spli...  9.78 us
    pallas_call x1, Pallas kernels, expert_backward(): pl.pallas_call(functools.partial(backward_kernel, rows, chunk), grid=(2,)...  7.87 us
  transfers between devices with their start and end apart: 16, of which 9 were waited for; matrix products, arithmetic and copies ran while one was open for 6% of the time, Pallas kernels for 4%

profile of v5, /device:TPU:4, one launch (start us, length us, event | category | flops | bytes accessed | tf_op | source)
XLA Modules:
  0.0 228.2 jit_solution(17645341744056631951)
XLA Ops:
  7.9 1.9 collective-permute-start.1
  11.2 2.4 %collective-permute-start = (f32[8,128]{1,0:T(8,128)S(1)}, f32[8,128]{1,0:T(8,128)S(1)}, u32[]{:S(2)}, u32[]{:S(2)}) collective-permute-start(f32[8,128]{1,0:T(8,128)S(1)} %pad_maximum_fusion.4), channel_id=1, source_target_pairs={{0,1},{1,0},{2,3},{3,2},{4,5},{5,4},{6,7},{7,6},{8,9},{9,8},{10,11... | collective-permute-start | bytes 12296 | tf_op jit(solution)/shard_map/ppermute | solution.py:41
  18.7 10.3 %all-to-all-start = ((bf16[32,32,512]{2,1,0:T(8,128)(2,1)}), bf16[32,32,512]{2,1,0:T(8,128)(2,1)}, u32[]{:S(2)}, u32[]{:S(2)}) async-start(bf16[32,32,512]{2,1,0:T(8,128)(2,1)} %pad_maximum_fusion), calls=%async_computation | async-start | bytes 2097152 | tf_op jit(solution)/shard_map/all_to_all | solution.py:334
  30.8 4.3 %collective-permute-start.2 = (bf16[384,512]{1,0:T(8,128)(2,1)}, bf16[384,512]{1,0:T(8,128)(2,1)S(1)}, u32[]{:S(2)}, u32[]{:S(2)}) collective-permute-start(bf16[384,512]{1,0:T(8,128)(2,1)} %pack.1.refs_0_), channel_id=1, source_target_pairs={{0,64},{64,128},{128,192},{192,256},{256,320},{320,384},{384,448},... | collective-permute-start | bytes 1179656 | tf_op jit(solution)/shard_map/ppermute | solution.py:41
  35.1 8.6 %collective-permute-start.6 = (bf16[384,512]{1,0:T(8,128)(2,1)}, bf16[384,512]{1,0:T(8,128)(2,1)S(1)}, u32[]{:S(2)}, u32[]{:S(2)}) collective-permute-start(bf16[384,512]{1,0:T(8,128)(2,1)} %pack.1.refs_0_), channel_id=1, source_target_pairs={{0,448},{64,0},{128,64},{192,128},{256,192},{320,256},{384,320},{4... | collective-permute-start | bytes 1179656 | tf_op jit(solution)/shard_map/ppermute | solution.py:41
  43.7 7.3 %collective-permute-done.2.refs_1_ = bf16[384,512]{1,0:T(8,128)(2,1)S(1)} collective-permute-done((bf16[384,512]{1,0:T(8,128)(2,1)}, bf16[384,512]{1,0:T(8,128)(2,1)S(1)}, u32[]{:S(2)}, u32[]{:S(2)}) %collective-permute-start.2) | collective-permute-done | bytes 393248 | tf_op jit(solution)/shard_map/ppermute | solution.py:41
  51.0 1.9 collective-permute-start.3
  52.9 5.1 %collective-permute-start.7 = (bf16[384,512]{1,0:T(8,128)(2,1)S(1)}, bf16[384,512]{1,0:T(8,128)(2,1)}, u32[]{:S(2)}, u32[]{:S(2)}) collective-permute-start(bf16[384,512]{1,0:T(8,128)(2,1)S(1)} %collective-permute-done.6.refs_7_), channel_id=1, source_target_pairs={{0,448},{64,0},{128,64},{192,128},{256,192},{320,256},{384,320},{4... | collective-permute-start | bytes 1179656 | tf_op jit(solution)/shard_map/ppermute | solution.py:41
  58.1 6.3 %collective-permute-done.3.refs_2_ = bf16[384,512]{1,0:T(8,128)(2,1)S(1)} collective-permute-done((bf16[384,512]{1,0:T(8,128)(2,1)S(1)}, bf16[384,512]{1,0:T(8,128)(2,1)S(1)}, u32[]{:S(2)}, u32[]{:S(2)}) %collective-permute-start.3) | collective-permute-done | bytes 393248 | tf_op jit(solution)/shard_map/ppermute | solution.py:41
  64.4 1.9 collective-permute-start.4
  66.4 5.1 %collective-permute-start.8 = (bf16[384,512]{1,0:T(8,128)(2,1)}, bf16[384,512]{1,0:T(8,128)(2,1)}, u32[]{:S(2)}, u32[]{:S(2)}) collective-permute-start(bf16[384,512]{1,0:T(8,128)(2,1)} %collective-permute-done.7.refs_6_), channel_id=1, source_target_pairs={{0,448},{64,0},{128,64},{192,128},{256,192},{320,256},{384,320},{4... | collective-permute-start | bytes 1179656 | tf_op jit(solution)/shard_map/ppermute | solution.py:41
  71.5 5.6 %collective-permute-done.4.refs_3_ = bf16[384,512]{1,0:T(8,128)(2,1)} collective-permute-done((bf16[384,512]{1,0:T(8,128)(2,1)S(1)}, bf16[384,512]{1,0:T(8,128)(2,1)}, u32[]{:S(2)}, u32[]{:S(2)}) %collective-permute-start.4) | collective-permute-done | bytes 393248 | tf_op jit(solution)/shard_map/ppermute | solution.py:41
  77.1 1.9 collective-permute-start.5
  79.0 10.1 %collective-permute-done.5.refs_4_ = bf16[384,512]{1,0:T(8,128)(2,1)} collective-permute-done((bf16[384,512]{1,0:T(8,128)(2,1)}, bf16[384,512]{1,0:T(8,128)(2,1)}, u32[]{:S(2)}, u32[]{:S(2)}) %collective-permute-start.5) | collective-permute-done | bytes 393248 | tf_op jit(solution)/shard_map/ppermute | solution.py:41
  89.1 7.7 %expert_forward.1 = (bf16[768,1024]{1,0:T(8,128)(2,1)}, bf16[768,1024]{1,0:T(8,128)(2,1)}, bf16[768,1024]{1,0:T(8,128)(2,1)}, bf16[768,512]{1,0:T(8,128)(2,1)}, bf16[8,128,512]{2,1,0:T(8,128)(2,1)}) custom-call(s32[1]{0:T(128)} %bitcast.9.here_ref, bf16[32,32,512]{2,1,0:T(8,128)(2,1)} %all-to-all-done.inbound_ref, bf16[384,512]{1,0:T(8,128)(2,1)} %pack.1.refs_0_, ...), custom_call_target="tpu_custom_call" | custom-call | flops 2415919104 | bytes 7864320 | tf_op jit(solution)/shard_map/expert_forward/pallas_call | solution.py:170
  96.8 9.8 %all-to-all-start.1 = ((bf16[32,24,512]{2,1,0:T(8,128)(2,1)}), bf16[32,24,512]{2,1,0:T(8,128)(2,1)S(1)}, u32[]{:S(2)}, u32[]{:S(2)}) async-start(bf16[32,24,512]{2,1,0:T(8,128)(2,1)} %bitcast.81), calls=%async_computation.1 | async-start | bytes 1572864 | tf_op jit(solution)/shard_map/all_to_all | solution.py:344
  108.3 1.9 collective-permute-start.10
  114.1 11.9 %all-to-all-done.1 = bf16[32,24,512]{2,1,0:T(8,128)(2,1)S(1)} async-done(((bf16[32,24,512]{2,1,0:T(8,128)(2,1)}), bf16[32,24,512]{2,1,0:T(8,128)(2,1)S(1)}, u32[]{:S(2)}, u32[]{:S(2)}) %all-to-all-start.1) | async-done | bytes 786464 | tf_op jit(solution)/shard_map/all_to_all | solution.py:344
  127.6 2.1 collective-permute-start.9
  129.7 4.2 %fusion.34 = f32[128,512]{1,0:T(8,128)S(1)} fusion(bf16[128,7168]{1,0:T(8,128)(2,1)S(1)} %copy-done, bf16[7168,512]{1,0:T(8,128)(2,1)} %all-gather.2.cloned.1.call-done), kind=kOutput, calls=%fused_computation.76 | convolution fusion | flops 939524096 | bytes 9437184 | tf_op jit(solution)/shard_map/dot_general | solution.py:31
  134.6 2.4 %collective-permute-start.11 = (bf16[128,512]{1,0:T(8,128)(2,1)S(1)}, bf16[128,512]{1,0:T(8,128)(2,1)S(1)}, u32[]{:S(2)}, u32[]{:S(2)}) collective-permute-start(bf16[128,512]{1,0:T(8,128)(2,1)S(1)} %fusion.6), channel_id=1, source_target_pairs={{0,1},{1,0},{2,3},{3,2},{4,5},{5,4},{6,7},{7,6},{8,9},{9,8},{10,11... | collective-permute-start | bytes 393224 | tf_op jit(solution)/shard_map/ppermute | solution.py:41
  139.3 28.4 %all_to_all.15 = bf16[32,24,512]{2,1,0:T(8,128)(2,1)} all-to-all(bf16[32,24,512]{2,1,0:T(8,128)(2,1)S(1)} %bitcast.75), channel_id=1, replica_groups=mesh['grp'=8,'yx'=32,'c'=2] {'yx'}, dimensions={0} | all-to-all | bytes 1572864 | tf_op jit(solution)/shard_map/all_to_all | solution.py:367
  167.8 7.9 %expert_backward.1 = bf16[8,384,512]{2,1,0:T(8,128)(2,1)} custom-call(bf16[768,512]{1,0:T(8,128)(2,1)} %bitcast.82, bf16[32,32,512]{2,1,0:T(8,128)(2,1)} %all-to-all-done.inbound_ref, bf16[768,1024]{1,0:T(8,128)(2,1)} %get-tuple-element.13.hid_ref, bf16[768,1024]{1,0:T(8,128)(2,1)} %get-tuple-element.14.cg_ref, bf16[768,1024]{1,0:T(8,128)(2,1)} %get-tuple-element.15.cu_ref, ...), custom_call_target="tpu_custom_call" | custom-call | flops 3221225472 | bytes 7864320 | tf_op jit(solution)/shard_map/expert_backward/pallas_call | solution.py:255
  175.7 43.8 %reduce-scatter.2.cloned.1.call-done.in_ref = bf16[384,512]{1,0:T(8,128)(2,1)} async-done(((bf16[3072,512]{1,0:T(8,128)(2,1)}), bf16[384,512]{1,0:T(8,128)(2,1)}) %reduce-scatter.2.cloned.1.call-update) | async-done | bytes 393232 | tf_op jit(solution)/shard_map/reduce_scatter | solution.py:374
  (70 shorter events, 20.9 us)
Async XLA Ops:
  7.2 122.6 %copy-start = (bf16[128,7168]{1,0:T(8,128)(2,1)S(1)}, bf16[128,7168]{1,0:T(8,128)(2,1)}, u32[]{:S(2)}) copy-start(bf16[128,7168]{1,0:T(8,128)(2,1)} %param.11) | copy-start | bytes 5505028
  7.2 122.5 %all-gather.2.cloned.1.call-start = ((), (), s32[]{:S(2)}) async-start(), calls=%async_computation.4 | async-start | bytes 7454720 | tf_op jit(solution)/shard_map/all_gather | solution.py:303
  7.9 8.1 %collective-permute-start.1 = (bf16[128,512]{1,0:T(8,128)(2,1)}, bf16[128,512]{1,0:T(8,128)(2,1)S(1)}, u32[]{:S(2)}, u32[]{:S(2)}) collective-permute-start(bf16[128,512]{1,0:T(8,128)(2,1)} %param.10), channel_id=1, source_target_pairs={{0,1},{1,0},{2,3},{3,2},{4,5},{5,4},{6,7},{7,6},{8,9},{9,8},{10,11... | collective-permute-start | bytes 393224 | tf_op jit(solution)/shard_map/ppermute | solution.py:41
  11.2 3.2 %collective-permute-start = (f32[8,128]{1,0:T(8,128)S(1)}, f32[8,128]{1,0:T(8,128)S(1)}, u32[]{:S(2)}, u32[]{:S(2)}) collective-permute-start(f32[8,128]{1,0:T(8,128)S(1)} %pad_maximum_fusion.4), channel_id=1, source_target_pairs={{0,1},{1,0},{2,3},{3,2},{4,5},{5,4},{6,7},{7,6},{8,9},{9,8},{10,11... | collective-permute-start | bytes 12296 | tf_op jit(solution)/shard_map/ppermute | solution.py:41
  18.7 70.4 %all-to-all-start = ((bf16[32,32,512]{2,1,0:T(8,128)(2,1)}), bf16[32,32,512]{2,1,0:T(8,128)(2,1)}, u32[]{:S(2)}, u32[]{:S(2)}) async-start(bf16[32,32,512]{2,1,0:T(8,128)(2,1)} %pad_maximum_fusion), calls=%async_computation | async-start | bytes 2097152 | tf_op jit(solution)/shard_map/all_to_all | solution.py:334
  30.8 20.2 %collective-permute-start.2 = (bf16[384,512]{1,0:T(8,128)(2,1)}, bf16[384,512]{1,0:T(8,128)(2,1)S(1)}, u32[]{:S(2)}, u32[]{:S(2)}) collective-permute-start(bf16[384,512]{1,0:T(8,128)(2,1)} %pack.1.refs_0_), channel_id=1, source_target_pairs={{0,64},{64,128},{128,192},{192,256},{256,320},{320,384},{384,448},... | collective-permute-start | bytes 1179656 | tf_op jit(solution)/shard_map/ppermute | solution.py:41
  35.1 17.8 %collective-permute-start.6 = (bf16[384,512]{1,0:T(8,128)(2,1)}, bf16[384,512]{1,0:T(8,128)(2,1)S(1)}, u32[]{:S(2)}, u32[]{:S(2)}) collective-permute-start(bf16[384,512]{1,0:T(8,128)(2,1)} %pack.1.refs_0_), channel_id=1, source_target_pairs={{0,448},{64,0},{128,64},{192,128},{256,192},{320,256},{384,320},{4... | collective-permute-start | bytes 1179656 | tf_op jit(solution)/shard_map/ppermute | solution.py:41
  51.0 38.1 %copy-start.9 = (bf16[384,512]{1,0:T(8,128)(2,1)}, bf16[384,512]{1,0:T(8,128)(2,1)S(1)}, u32[]{:S(2)}) copy-start(bf16[384,512]{1,0:T(8,128)(2,1)S(1)} %collective-permute-done.2.refs_1_) | copy-start | bytes 1179652
  51.0 13.4 %collective-permute-start.3 = (bf16[384,512]{1,0:T(8,128)(2,1)S(1)}, bf16[384,512]{1,0:T(8,128)(2,1)S(1)}, u32[]{:S(2)}, u32[]{:S(2)}) collective-permute-start(bf16[384,512]{1,0:T(8,128)(2,1)S(1)} %collective-permute-done.2.refs_1_), channel_id=1, source_target_pairs={{0,64},{64,128},{128,192},{192,256},{256,320},{320,384},{384,448},... | collective-permute-start | bytes 1179656 | tf_op jit(solution)/shard_map/ppermute | solution.py:41
  52.9 36.2 %copy-start.10 = (bf16[384,512]{1,0:T(8,128)(2,1)}, bf16[384,512]{1,0:T(8,128)(2,1)S(1)}, u32[]{:S(2)}) copy-start(bf16[384,512]{1,0:T(8,128)(2,1)S(1)} %collective-permute-done.6.refs_7_) | copy-start | bytes 1179652
  52.9 13.4 %collective-permute-start.7 = (bf16[384,512]{1,0:T(8,128)(2,1)S(1)}, bf16[384,512]{1,0:T(8,128)(2,1)}, u32[]{:S(2)}, u32[]{:S(2)}) collective-permute-start(bf16[384,512]{1,0:T(8,128)(2,1)S(1)} %collective-permute-done.6.refs_7_), channel_id=1, source_target_pairs={{0,448},{64,0},{128,64},{192,128},{256,192},{320,256},{384,320},{4... | collective-permute-start | bytes 1179656 | tf_op jit(solution)/shard_map/ppermute | solution.py:41
  64.4 12.7 %collective-permute-start.4 = (bf16[384,512]{1,0:T(8,128)(2,1)S(1)}, bf16[384,512]{1,0:T(8,128)(2,1)}, u32[]{:S(2)}, u32[]{:S(2)}) collective-permute-start(bf16[384,512]{1,0:T(8,128)(2,1)S(1)} %collective-permute-done.3.refs_2_), channel_id=1, source_target_pairs={{0,64},{64,128},{128,192},{192,256},{256,320},{320,384},{384,448},... | collective-permute-start | bytes 1179656 | tf_op jit(solution)/shard_map/ppermute | solution.py:41
  66.4 12.6 %collective-permute-start.8 = (bf16[384,512]{1,0:T(8,128)(2,1)}, bf16[384,512]{1,0:T(8,128)(2,1)}, u32[]{:S(2)}, u32[]{:S(2)}) collective-permute-start(bf16[384,512]{1,0:T(8,128)(2,1)} %collective-permute-done.7.refs_6_), channel_id=1, source_target_pairs={{0,448},{64,0},{128,64},{192,128},{256,192},{320,256},{384,320},{4... | collective-permute-start | bytes 1179656 | tf_op jit(solution)/shard_map/ppermute | solution.py:41
  77.1 12.0 %collective-permute-start.5 = (bf16[384,512]{1,0:T(8,128)(2,1)}, bf16[384,512]{1,0:T(8,128)(2,1)}, u32[]{:S(2)}, u32[]{:S(2)}) collective-permute-start(bf16[384,512]{1,0:T(8,128)(2,1)} %collective-permute-done.4.refs_3_), channel_id=1, source_target_pairs={{0,64},{64,128},{128,192},{192,256},{256,320},{320,384},{384,448},... | collective-permute-start | bytes 1179656 | tf_op jit(solution)/shard_map/ppermute | solution.py:41
  96.8 29.1 %all-to-all-start.1 = ((bf16[32,24,512]{2,1,0:T(8,128)(2,1)}), bf16[32,24,512]{2,1,0:T(8,128)(2,1)S(1)}, u32[]{:S(2)}, u32[]{:S(2)}) async-start(bf16[32,24,512]{2,1,0:T(8,128)(2,1)} %bitcast.81), calls=%async_computation.1 | async-start | bytes 1572864 | tf_op jit(solution)/shard_map/all_to_all | solution.py:344
  106.6 112.9 %reduce-scatter.2.cloned.1.call-start = ((), (), s32[]{:S(2)}) async-start(), calls=%async_computation.5 | async-start | bytes 3538944 | tf_op jit(solution)/shard_map/reduce_scatter | solution.py:374
  108.3 3.8 %collective-permute-start.10 = (bf16[32,8,512]{2,1,0:T(8,128)(2,1)}, bf16[32,8,512]{2,1,0:T(8,128)(2,1)}, u32[]{:S(2)}, u32[]{:S(2)}) collective-permute-start(bf16[32,8,512]{2,1,0:T(8,128)(2,1)} %slice.14), channel_id=1, source_target_pairs={{0,1},{1,0},{2,3},{3,2},{4,5},{5,4},{6,7},{7,6},{8,9},{9,8},{10,11... | collective-permute-start | bytes 786440 | tf_op jit(solution)/shard_map/ppermute | solution.py:41
  127.6 6.3 %copy-start.3 = (bf16[32,2,8,512]{3,2,1,0:T(8,128)(2,1)S(1)}, bf16[32,2,8,512]{3,2,1,0:T(8,128)(2,1)}, u32[]{:S(2)}) copy-start(bf16[32,2,8,512]{3,2,1,0:T(8,128)(2,1)} %copy.15) | copy-start | bytes 1572868
  127.6 6.3 %copy-start.5 = (f32[256,512]{1,0:T(8,128)S(1)}, f32[256,512]{1,0:T(8,128)}, u32[]{:S(2)}) copy-start(f32[256,512]{1,0:T(8,128)} %copy-done.4) | copy-start | bytes 1572868
  127.6 6.3 %copy-start.6 = (f32[512]{0:T(512)S(1)}, f32[512]{0:T(512)}, u32[]{:S(2)}) copy-start(f32[512]{0:T(512)} %param.19) | copy-start | bytes 6148
  127.6 6.3 %collective-permute-start.9 = (f32[128,512]{1,0:T(8,128)S(1)}, f32[128,512]{1,0:T(8,128)S(1)}, u32[]{:S(2)}, u32[]{:S(2)}) collective-permute-start(f32[128,512]{1,0:T(8,128)S(1)} %dynamic-slice_bitcast_fusion), channel_id=1, source_target_pairs={{0,1},{1,0},{2,3},{3,2},{4,5},{5,4},{6,7},{7,6},{8,9},{9,8},{10,11... | collective-permute-start | bytes 786440 | tf_op jit(solution)/shard_map/ppermute | solution.py:41
  134.4 4.6 %copy-start.8 = (f32[128]{0:T(128)}, f32[128]{0:T(128)S(1)}, u32[]{:S(2)}) copy-start(f32[128]{0:T(128)S(1)} %get-tuple-element.33) | copy-start | bytes 1540
  134.4 4.2 %copy-start.2 = (bf16[768,256]{1,0:T(8,128)(2,1)S(1)}, bf16[768,256]{1,0:T(8,128)(2,1)}, u32[]{:S(2)}) copy-start(bf16[768,256]{1,0:T(8,128)(2,1)} %copy-done.1) | copy-start | bytes 1179652
  134.6 3.4 %collective-permute-start.11 = (bf16[128,512]{1,0:T(8,128)(2,1)S(1)}, bf16[128,512]{1,0:T(8,128)(2,1)S(1)}, u32[]{:S(2)}, u32[]{:S(2)}) collective-permute-start(bf16[128,512]{1,0:T(8,128)(2,1)S(1)} %fusion.6), channel_id=1, source_target_pairs={{0,1},{1,0},{2,3},{3,2},{4,5},{5,4},{6,7},{7,6},{8,9},{9,8},{10,11... | collective-permute-start | bytes 393224 | tf_op jit(solution)/shard_map/ppermute | solution.py:41
  (4 other events, 6.0 us)
Sparse Core Ops, SparseCore 0:
  11.3 93.9 all-gather.1
  175.8 43.6 reduce-scatter.1

commit v6 on v5

--- a/solution.py
+++ b/solution.py
@@ -61,6 +61,17 @@
             down = shift(down, "grp", -1)
             pieces[count - step] = down
     return pieces
+
+
+def pair_up(value):
+    count = lax.axis_size("grp")
+    return lax.ppermute(value, "grp", [(i, i ^ 1) for i in range(count)])
+
+
+def critic_half(side, shard):
+    cols = shard.shape[1] // 2
+    mine = lax.dynamic_slice_in_dim(shard, side * cols, cols, axis=1)
+    return lax.all_gather(mine, EP, axis=0, tiled=True)
 
 
 VMEM = pl.BlockSpec(memory_space=pltpu.VMEM)
@@ -300,9 +311,12 @@
     half = hidden_all // 2
     rows_in = w_gate.shape[1]
 
-    teacher_rows = lax.all_gather(critic_teacher, EP, axis=0, tiled=True)
+    side = lax.axis_index("grp") % 2
+    teacher_rows = critic_half(side, critic_teacher)
     here = lax.axis_index("grp").astype(jnp.int32).reshape(1)
     pieces = ring_gather(pack_weights(w_gate[0], w_up[0], w_down[0]))
+
+    other_teacher = pair_up(teacher)
 
     meta = jnp.concatenate([expert_ids.T.astype(F32), route_weights.T])
     tok2 = both(core, tokens, swap(tokens)).reshape(2 * tok_dev, width)
@@ -354,7 +368,14 @@
     mine = lax.dynamic_index_in_dim(partial, core, 0, keepdims=False)
     theirs = lax.dynamic_index_in_dim(partial, 1 - core, 0, keepdims=False)
     student = (mine + swap(theirs)).astype(BF)
-    pre_teacher = dot(teacher, teacher_rows)
+    own_pre = dot(teacher, teacher_rows)
+    other_pre = dot(other_teacher, teacher_rows)
+    own_pre, other_pre = lax.optimization_barrier((own_pre, other_pre))
+    got_pre = pair_up(other_pre)
+    even = side == 0
+    pre_teacher = jnp.concatenate(
+        [jnp.where(even, own_pre, got_pre), jnp.where(even, got_pre, own_pre)], axis=1
+    )
     pre = pre_teacher + dot(student, student_rows)
     score = jnp.sum(gelu_tanh(pre) * critic_head[None, :], axis=1)
     dscore = -jax.nn.sigmoid(-score)

time: 229 us -> 255 us (1.11)
  waiting for transfers between devices: 89.3 us -> 104 us
  blocking collectives: 28.4 us -> 32.4 us
  starting transfers between devices: 59.7 us -> 63.1 us
    ppermute x0 -> x2, waiting for transfers between devices: none -> 18.8 us  [pair_up(): return lax.ppermute(value, 'grp', [(i, i ^ 1) for i in range(count)])]
    ppermute x0 -> x2, starting transfers between devices: none -> 4.12 us  [pair_up(): return lax.ppermute(value, 'grp', [(i, i ^ 1) for i in range(count)])]
    all_to_all x1, blocking collectives: 28.4 us -> 32.4 us  [layer(): lax.all_to_all(grad_out.reshape(chips, 2 * capacity, width), 'yx', split_...]
    ppermute x12, waiting for transfers between devices: 32.9 us -> 29.4 us  [shift(): lax.ppermute(value, axis, [(i, (i + step) % count) for i in range(count)])]
    unnamed x24 -> x25, local copies, waits for them, and re-layouts: 0.84 us -> 3.6 us
    dot_general x8 -> x9, matrix products: 6.83 us -> 9.22 us  [dot(): lax.dot_general(left, right, (dims, ((), ())), preferred_element_type=F32)]
  transfers between devices with their start and end apart: 16 -> 18, of which waited for: 9 -> 10; matrix products, arithmetic and copies ran while one was open for 6% -> 5% of each run, Pallas kernels for 4% -> 4%
where the time goes in v6:
time: 255 us; the launch traced here: 253 us
  waiting for transfers between devices  104 us (41%)
  starting transfers between devices  63.1 us (25%)
  blocking collectives  32.4 us (13%)
  Pallas kernels  19.3 us (8%)
  between operations  14.6 us (6%)
  matrix products  9.35 us (4%)
  local copies, waits for them, and re-layouts  5.59 us (2%)
  other arithmetic  5.53 us (2%)
    reduce_scatter x1, waiting for transfers between devices, layer(): lax.psum_scatter(parts.reshape(-1, width), 'grp', scatter_dimension=0, ti...  43.7 us
    ppermute x12, starting transfers between devices, shift(): lax.ppermute(value, axis, [(i, (i + step) % count) for i in range(count)])  38.9 us
    all_to_all x1, blocking collectives, layer(): lax.all_to_all(grad_out.reshape(chips, 2 * capacity, width), 'yx', split_...  32.4 us
    ppermute x12, waiting for transfers between devices, shift(): lax.ppermute(value, axis, [(i, (i + step) % count) for i in range(count)])  29.4 us
    ppermute x2, waiting for transfers between devices, pair_up(): return lax.ppermute(value, 'grp', [(i, i ^ 1) for i in range(count)])  18.8 us
    all_to_all x1, waiting for transfers between devices, layer(): lax.all_to_all(expert_out.reshape(chips, 2 * capacity, width), 'yx', spli...  11.7 us
    all_to_all x1, starting transfers between devices, layer(): lax.all_to_all(outbound, 'yx', split_axis=0, concat_axis=0, tiled=True)  10.2 us
    all_to_all x1, starting transfers between devices, layer(): lax.all_to_all(expert_out.reshape(chips, 2 * capacity, width), 'yx', spli...  9.77 us
  transfers between devices with their start and end apart: 18, of which 10 were waited for; matrix products, arithmetic and copies ran while one was open for 5% of the time, Pallas kernels for 4%

profile of v6, /device:TPU:4, one launch (start us, length us, event | category | flops | bytes accessed | tf_op | source)
XLA Modules:
  0.0 253.5 jit_solution(12170059003281155603)
XLA Ops:
  13.0 2.4 collective-permute-start.3
  18.9 10.2 %all-to-all-start = ((bf16[32,32,512]{2,1,0:T(8,128)(2,1)}), bf16[32,32,512]{2,1,0:T(8,128)(2,1)S(1)}, u32[]{:S(2)}, u32[]{:S(2)}) async-start(bf16[32,32,512]{2,1,0:T(8,128)(2,1)} %pad_maximum_fusion), calls=%async_computation | async-start | bytes 2097152 | tf_op jit(solution)/shard_map/all_to_all | solution.py:348
  30.9 4.3 %collective-permute-start.4 = (bf16[384,512]{1,0:T(8,128)(2,1)}, bf16[384,512]{1,0:T(8,128)(2,1)S(1)}, u32[]{:S(2)}, u32[]{:S(2)}) collective-permute-start(bf16[384,512]{1,0:T(8,128)(2,1)} %pack.1.refs_0_), channel_id=1, source_target_pairs={{0,64},{64,128},{128,192},{192,256},{256,320},{320,384},{384,448},... | collective-permute-start | bytes 1179656 | tf_op jit(solution)/shard_map/ppermute | solution.py:41
  35.2 8.6 %collective-permute-start.8 = (bf16[384,512]{1,0:T(8,128)(2,1)}, bf16[384,512]{1,0:T(8,128)(2,1)S(1)}, u32[]{:S(2)}, u32[]{:S(2)}) collective-permute-start(bf16[384,512]{1,0:T(8,128)(2,1)} %pack.1.refs_0_), channel_id=1, source_target_pairs={{0,448},{64,0},{128,64},{192,128},{256,192},{320,256},{384,320},{4... | collective-permute-start | bytes 1179656 | tf_op jit(solution)/shard_map/ppermute | solution.py:41
  43.8 7.0 %collective-permute-done.4.refs_1_ = bf16[384,512]{1,0:T(8,128)(2,1)S(1)} collective-permute-done((bf16[384,512]{1,0:T(8,128)(2,1)}, bf16[384,512]{1,0:T(8,128)(2,1)S(1)}, u32[]{:S(2)}, u32[]{:S(2)}) %collective-permute-start.4) | collective-permute-done | bytes 393248 | tf_op jit(solution)/shard_map/ppermute | solution.py:41
  52.7 5.1 %collective-permute-start.9 = (bf16[384,512]{1,0:T(8,128)(2,1)S(1)}, bf16[384,512]{1,0:T(8,128)(2,1)S(1)}, u32[]{:S(2)}, u32[]{:S(2)}) collective-permute-start(bf16[384,512]{1,0:T(8,128)(2,1)S(1)} %collective-permute-done.8.refs_7_), channel_id=1, source_target_pairs={{0,448},{64,0},{128,64},{192,128},{256,192},{320,256},{384,320},{4... | collective-permute-start | bytes 1179656 | tf_op jit(solution)/shard_map/ppermute | solution.py:41
  57.8 5.9 %collective-permute-done.5.refs_2_ = bf16[384,512]{1,0:T(8,128)(2,1)S(1)} collective-permute-done((bf16[384,512]{1,0:T(8,128)(2,1)S(1)}, bf16[384,512]{1,0:T(8,128)(2,1)S(1)}, u32[]{:S(2)}, u32[]{:S(2)}) %collective-permute-start.5) | collective-permute-done | bytes 393248 | tf_op jit(solution)/shard_map/ppermute | solution.py:41
  65.7 5.1 %collective-permute-start.10 = (bf16[384,512]{1,0:T(8,128)(2,1)S(1)}, bf16[384,512]{1,0:T(8,128)(2,1)S(1)}, u32[]{:S(2)}, u32[]{:S(2)}) collective-permute-start(bf16[384,512]{1,0:T(8,128)(2,1)S(1)} %collective-permute-done.9.refs_6_), channel_id=1, source_target_pairs={{0,448},{64,0},{128,64},{192,128},{256,192},{320,256},{384,320},{4... | collective-permute-start | bytes 1179656 | tf_op jit(solution)/shard_map/ppermute | solution.py:41
  70.8 5.0 %collective-permute-done.6.refs_3_ = bf16[384,512]{1,0:T(8,128)(2,1)S(1)} collective-permute-done((bf16[384,512]{1,0:T(8,128)(2,1)S(1)}, bf16[384,512]{1,0:T(8,128)(2,1)S(1)}, u32[]{:S(2)}, u32[]{:S(2)}) %collective-permute-start.6) | collective-permute-done | bytes 393248 | tf_op jit(solution)/shard_map/ppermute | solution.py:41
  78.6 8.7 %collective-permute-done.7.refs_4_ = bf16[384,512]{1,0:T(8,128)(2,1)} collective-permute-done((bf16[384,512]{1,0:T(8,128)(2,1)S(1)}, bf16[384,512]{1,0:T(8,128)(2,1)}, u32[]{:S(2)}, u32[]{:S(2)}) %collective-permute-start.7) | collective-permute-done | bytes 393248 | tf_op jit(solution)/shard_map/ppermute | solution.py:41
  88.2 7.7 %expert_forward.1 = (bf16[768,1024]{1,0:T(8,128)(2,1)}, bf16[768,1024]{1,0:T(8,128)(2,1)}, bf16[768,1024]{1,0:T(8,128)(2,1)}, bf16[768,512]{1,0:T(8,128)(2,1)}, bf16[8,128,512]{2,1,0:T(8,128)(2,1)}) custom-call(s32[1]{0:T(128)} %bitcast.11.here_ref, bf16[32,32,512]{2,1,0:T(8,128)(2,1)} %copy-done.2, bf16[384,512]{1,0:T(8,128)(2,1)} %pack.1.refs_0_, ...), custom_call_target="tpu_custom_call" | custom-call | flops 2415919104 | bytes 7864320 | tf_op jit(solution)/shard_map/expert_forward/pallas_call | solution.py:181
  95.9 9.8 %all-to-all-start.1 = ((bf16[32,24,512]{2,1,0:T(8,128)(2,1)}), bf16[32,24,512]{2,1,0:T(8,128)(2,1)S(1)}, u32[]{:S(2)}, u32[]{:S(2)}) async-start(bf16[32,24,512]{2,1,0:T(8,128)(2,1)} %bitcast.89), calls=%async_computation.1 | async-start | bytes 1572864 | tf_op jit(solution)/shard_map/all_to_all | solution.py:358
  105.8 1.9 collective-permute-start.1
  108.7 1.9 collective-permute-start.12
  113.1 11.7 %all-to-all-done.1 = bf16[32,24,512]{2,1,0:T(8,128)(2,1)S(1)} async-done(((bf16[32,24,512]{2,1,0:T(8,128)(2,1)}), bf16[32,24,512]{2,1,0:T(8,128)(2,1)S(1)}, u32[]{:S(2)}, u32[]{:S(2)}) %all-to-all-start.1) | async-done | bytes 786464 | tf_op jit(solution)/shard_map/all_to_all | solution.py:358
  125.6 3.9 %convolution_bitcast_fusion.1 = f32[128,256]{0,1:T(8,128)S(1)} fusion(bf16[7168,256]{1,0:T(8,128)(2,1)} %all-gather.2.cloned.1.call-done, bf16[128,7168]{1,0:T(8,128)(2,1)} %param.11), kind=kOutput, calls=%fused_computation.8 | convolution fusion | flops 469762048 | bytes 5636096 | tf_op jit(solution)/shard_map/dot_general | solution.py:31
  129.5 16.2 %collective-permute-done.1 = bf16[128,7168]{1,0:T(8,128)(2,1)} collective-permute-done((bf16[128,7168]{1,0:T(8,128)(2,1)}, bf16[128,7168]{1,0:T(8,128)(2,1)}, u32[]{:S(2)}, u32[]{:S(2)}) %collective-permute-start.1) | collective-permute-done | bytes 1835040 | tf_op jit(solution)/shard_map/ppermute | solution.py:68
  145.8 2.7 %convolution_bitcast_fusion = f32[128,256]{0,1:T(8,128)S(1)} fusion(bf16[7168,256]{1,0:T(8,128)(2,1)S(1)} %copy-done.1, bf16[128,7168]{1,0:T(8,128)(2,1)} %collective-permute-done.1), kind=kOutput, calls=%fused_computation.7 | convolution fusion | flops 469762048 | bytes 5636096 | tf_op jit(solution)/shard_map/dot_general | solution.py:31
  148.5 2.2 collective-permute-start.2
  152.8 2.6 %collective-permute-done.2 = f32[128,256]{0,1:T(8,128)S(1)} collective-permute-done((f32[128,256]{0,1:T(8,128)S(1)}, f32[128,256]{0,1:T(8,128)S(1)}, u32[]{:S(2)}, u32[]{:S(2)}) %collective-permute-start.2) | collective-permute-done | bytes 131104 | tf_op jit(solution)/shard_map/ppermute | solution.py:68
  156.0 1.9 collective-permute-start.13
  160.7 32.4 %all_to_all.15 = bf16[32,24,512]{2,1,0:T(8,128)(2,1)} all-to-all(bf16[32,24,512]{2,1,0:T(8,128)(2,1)S(1)} %bitcast.83), channel_id=1, replica_groups=mesh['grp'=8,'yx'=32,'c'=2] {'yx'}, dimensions={0} | all-to-all | bytes 1572864 | tf_op jit(solution)/shard_map/all_to_all | solution.py:388
  193.2 7.9 %expert_backward.1 = bf16[8,384,512]{2,1,0:T(8,128)(2,1)} custom-call(bf16[768,512]{1,0:T(8,128)(2,1)} %bitcast.90, bf16[32,32,512]{2,1,0:T(8,128)(2,1)} %copy-done.2, bf16[768,1024]{1,0:T(8,128)(2,1)} %get-tuple-element.17.hid_ref, bf16[768,1024]{1,0:T(8,128)(2,1)} %get-tuple-element.18.cg_ref, bf16[768,1024]{1,0:T(8,128)(2,1)} %get-tuple-element.19.cu_ref, ...), custom_call_target="tpu_custom_call" | custom-call | flops 3221225472 | bytes 7864320 | tf_op jit(solution)/shard_map/expert_backward/pallas_call | solution.py:266
  201.1 43.7 %reduce-scatter.2.cloned.1.call-done.in_ref = bf16[384,512]{1,0:T(8,128)(2,1)} async-done(((bf16[3072,512]{1,0:T(8,128)(2,1)}), bf16[384,512]{1,0:T(8,128)(2,1)}) %reduce-scatter.2.cloned.1.call-update) | async-done | bytes 393232 | tf_op jit(solution)/shard_map/reduce_scatter | solution.py:395
  (80 shorter events, 30.1 us)
Async XLA Ops:
  7.2 118.4 %all-gather.2.cloned.1.call-start = ((), (), s32[]{:S(2)}) async-start(), calls=%async_computation.4 | async-start | bytes 3727360 | tf_op jit(solution)/shard_map/all_gather | solution.py:74
  10.1 5.4 %collective-permute-start = (f32[8,128]{1,0:T(8,128)S(1)}, f32[8,128]{1,0:T(8,128)S(1)}, u32[]{:S(2)}, u32[]{:S(2)}) collective-permute-start(f32[8,128]{1,0:T(8,128)S(1)} %pad_maximum_fusion.4), channel_id=1, source_target_pairs={{0,1},{1,0},{2,3},{3,2},{4,5},{5,4},{6,7},{7,6},{8,9},{9,8},{10,11... | collective-permute-start | bytes 12296 | tf_op jit(solution)/shard_map/ppermute | solution.py:41
  13.0 4.1 %collective-permute-start.3 = (bf16[128,512]{0,1:T(8,128)(2,1)S(1)}, bf16[128,512]{0,1:T(8,128)(2,1)S(1)}, u32[]{:S(2)}, u32[]{:S(2)}) collective-permute-start(bf16[128,512]{0,1:T(8,128)(2,1)S(1)} %copy.26), channel_id=1, source_target_pairs={{0,1},{1,0},{2,3},{3,2},{4,5},{5,4},{6,7},{7,6},{8,9},{9,8},{10,11... | collective-permute-start | bytes 393224 | tf_op jit(solution)/shard_map/ppermute | solution.py:41
  18.9 68.4 %all-to-all-start = ((bf16[32,32,512]{2,1,0:T(8,128)(2,1)}), bf16[32,32,512]{2,1,0:T(8,128)(2,1)S(1)}, u32[]{:S(2)}, u32[]{:S(2)}) async-start(bf16[32,32,512]{2,1,0:T(8,128)(2,1)} %pad_maximum_fusion), calls=%async_computation | async-start | bytes 2097152 | tf_op jit(solution)/shard_map/all_to_all | solution.py:348
  30.9 19.9 %collective-permute-start.4 = (bf16[384,512]{1,0:T(8,128)(2,1)}, bf16[384,512]{1,0:T(8,128)(2,1)S(1)}, u32[]{:S(2)}, u32[]{:S(2)}) collective-permute-start(bf16[384,512]{1,0:T(8,128)(2,1)} %pack.1.refs_0_), channel_id=1, source_target_pairs={{0,64},{64,128},{128,192},{192,256},{256,320},{320,384},{384,448},... | collective-permute-start | bytes 1179656 | tf_op jit(solution)/shard_map/ppermute | solution.py:41
  35.2 17.5 %collective-permute-start.8 = (bf16[384,512]{1,0:T(8,128)(2,1)}, bf16[384,512]{1,0:T(8,128)(2,1)S(1)}, u32[]{:S(2)}, u32[]{:S(2)}) collective-permute-start(bf16[384,512]{1,0:T(8,128)(2,1)} %pack.1.refs_0_), channel_id=1, source_target_pairs={{0,448},{64,0},{128,64},{192,128},{256,192},{320,256},{384,320},{4... | collective-permute-start | bytes 1179656 | tf_op jit(solution)/shard_map/ppermute | solution.py:41
  50.8 36.5 %copy-start.6 = (bf16[384,512]{1,0:T(8,128)(2,1)}, bf16[384,512]{1,0:T(8,128)(2,1)S(1)}, u32[]{:S(2)}) copy-start(bf16[384,512]{1,0:T(8,128)(2,1)S(1)} %collective-permute-done.4.refs_1_) | copy-start | bytes 1179652
  50.8 13.0 %collective-permute-start.5 = (bf16[384,512]{1,0:T(8,128)(2,1)S(1)}, bf16[384,512]{1,0:T(8,128)(2,1)S(1)}, u32[]{:S(2)}, u32[]{:S(2)}) collective-permute-start(bf16[384,512]{1,0:T(8,128)(2,1)S(1)} %collective-permute-done.4.refs_1_), channel_id=1, source_target_pairs={{0,64},{64,128},{128,192},{192,256},{256,320},{320,384},{384,448},... | collective-permute-start | bytes 1179656 | tf_op jit(solution)/shard_map/ppermute | solution.py:41
  52.7 34.6 %copy-start.7 = (bf16[384,512]{1,0:T(8,128)(2,1)}, bf16[384,512]{1,0:T(8,128)(2,1)S(1)}, u32[]{:S(2)}) copy-start(bf16[384,512]{1,0:T(8,128)(2,1)S(1)} %collective-permute-done.8.refs_7_) | copy-start | bytes 1179652
  52.7 13.0 %collective-permute-start.9 = (bf16[384,512]{1,0:T(8,128)(2,1)S(1)}, bf16[384,512]{1,0:T(8,128)(2,1)S(1)}, u32[]{:S(2)}, u32[]{:S(2)}) collective-permute-start(bf16[384,512]{1,0:T(8,128)(2,1)S(1)} %collective-permute-done.8.refs_7_), channel_id=1, source_target_pairs={{0,448},{64,0},{128,64},{192,128},{256,192},{320,256},{384,320},{4... | collective-permute-start | bytes 1179656 | tf_op jit(solution)/shard_map/ppermute | solution.py:41
  63.8 23.5 %copy-start.8 = (bf16[384,512]{1,0:T(8,128)(2,1)}, bf16[384,512]{1,0:T(8,128)(2,1)S(1)}, u32[]{:S(2)}) copy-start(bf16[384,512]{1,0:T(8,128)(2,1)S(1)} %collective-permute-done.5.refs_2_) | copy-start | bytes 1179652
  63.8 12.1 %collective-permute-start.6 = (bf16[384,512]{1,0:T(8,128)(2,1)S(1)}, bf16[384,512]{1,0:T(8,128)(2,1)S(1)}, u32[]{:S(2)}, u32[]{:S(2)}) collective-permute-start(bf16[384,512]{1,0:T(8,128)(2,1)S(1)} %collective-permute-done.5.refs_2_), channel_id=1, source_target_pairs={{0,64},{64,128},{128,192},{192,256},{256,320},{320,384},{384,448},... | collective-permute-start | bytes 1179656 | tf_op jit(solution)/shard_map/ppermute | solution.py:41
  65.7 12.1 %copy-start.9 = (bf16[384,512]{1,0:T(8,128)(2,1)}, bf16[384,512]{1,0:T(8,128)(2,1)S(1)}, u32[]{:S(2)}) copy-start(bf16[384,512]{1,0:T(8,128)(2,1)S(1)} %collective-permute-done.9.refs_6_) | copy-start | bytes 1179652
  65.7 12.1 %collective-permute-start.10 = (bf16[384,512]{1,0:T(8,128)(2,1)S(1)}, bf16[384,512]{1,0:T(8,128)(2,1)S(1)}, u32[]{:S(2)}, u32[]{:S(2)}) collective-permute-start(bf16[384,512]{1,0:T(8,128)(2,1)S(1)} %collective-permute-done.9.refs_6_), channel_id=1, source_target_pairs={{0,448},{64,0},{128,64},{192,128},{256,192},{320,256},{384,320},{4... | collective-permute-start | bytes 1179656 | tf_op jit(solution)/shard_map/ppermute | solution.py:41
  75.9 11.4 %collective-permute-start.7 = (bf16[384,512]{1,0:T(8,128)(2,1)S(1)}, bf16[384,512]{1,0:T(8,128)(2,1)}, u32[]{:S(2)}, u32[]{:S(2)}) collective-permute-start(bf16[384,512]{1,0:T(8,128)(2,1)S(1)} %collective-permute-done.6.refs_3_), channel_id=1, source_target_pairs={{0,64},{64,128},{128,192},{192,256},{256,320},{320,384},{384,448},... | collective-permute-start | bytes 1179656 | tf_op jit(solution)/shard_map/ppermute | solution.py:41
  95.9 28.8 %all-to-all-start.1 = ((bf16[32,24,512]{2,1,0:T(8,128)(2,1)}), bf16[32,24,512]{2,1,0:T(8,128)(2,1)S(1)}, u32[]{:S(2)}, u32[]{:S(2)}) async-start(bf16[32,24,512]{2,1,0:T(8,128)(2,1)} %bitcast.89), calls=%async_computation.1 | async-start | bytes 1572864 | tf_op jit(solution)/shard_map/all_to_all | solution.py:358
  105.7 139.0 %reduce-scatter.2.cloned.1.call-start = ((), (), s32[]{:S(2)}) async-start(), calls=%async_computation.5 | async-start | bytes 3538944 | tf_op jit(solution)/shard_map/reduce_scatter | solution.py:395
  105.8 40.0 %collective-permute-start.1 = (bf16[128,7168]{1,0:T(8,128)(2,1)}, bf16[128,7168]{1,0:T(8,128)(2,1)}, u32[]{:S(2)}, u32[]{:S(2)}) collective-permute-start(bf16[128,7168]{1,0:T(8,128)(2,1)} %param.11), channel_id=1, source_target_pairs={{0,64},{64,0},{128,192},{192,128},{256,320},{320,256},{384,448},{4... | collective-permute-start | bytes 5505032 | tf_op jit(solution)/shard_map/ppermute | solution.py:68
  108.7 3.4 %collective-permute-start.12 = (bf16[32,8,512]{2,1,0:T(8,128)(2,1)S(1)}, bf16[32,8,512]{2,1,0:T(8,128)(2,1)S(1)}, u32[]{:S(2)}, u32[]{:S(2)}) collective-permute-start(bf16[32,8,512]{2,1,0:T(8,128)(2,1)S(1)} %slice.14), channel_id=1, source_target_pairs={{0,1},{1,0},{2,3},{3,2},{4,5},{5,4},{6,7},{7,6},{8,9},{9,8},{10,11... | collective-permute-start | bytes 786440 | tf_op jit(solution)/shard_map/ppermute | solution.py:41
  125.6 20.2 %copy-start.1 = (bf16[7168,256]{1,0:T(8,128)(2,1)S(1)}, bf16[7168,256]{1,0:T(8,128)(2,1)}, u32[]{:S(2)}) copy-start(bf16[7168,256]{1,0:T(8,128)(2,1)} %all-gather.2.cloned.1.call-done) | copy-start | bytes 11010052
  148.4 6.9 %copy-start.3 = (f32[512]{0:T(512)S(1)}, f32[512]{0:T(512)}, u32[]{:S(2)}) copy-start(f32[512]{0:T(512)} %param.19) | copy-start | bytes 6148
  148.5 6.9 %collective-permute-start.2 = (f32[128,256]{0,1:T(8,128)S(1)}, f32[128,256]{0,1:T(8,128)S(1)}, u32[]{:S(2)}, u32[]{:S(2)}) collective-permute-start(f32[128,256]{0,1:T(8,128)S(1)} %convolution_bitcast_fusion), channel_id=1, source_target_pairs={{0,64},{64,0},{128,192},{192,128},{256,320},{320,256},{384,448},{4... | collective-permute-start | bytes 393224 | tf_op jit(solution)/shard_map/ppermute | solution.py:68
  150.7 4.6 %collective-permute-start.11 = (f32[128,512]{1,0:T(8,128)S(1)}, f32[128,512]{1,0:T(8,128)S(1)}, u32[]{:S(2)}, u32[]{:S(2)}) collective-permute-start(f32[128,512]{1,0:T(8,128)S(1)} %dynamic-slice_bitcast_fusion), channel_id=1, source_target_pairs={{0,1},{1,0},{2,3},{3,2},{4,5},{5,4},{6,7},{7,6},{8,9},{9,8},{10,11... | collective-permute-start | bytes 786440 | tf_op jit(solution)/shard_map/ppermute | solution.py:41
  156.0 3.2 %collective-permute-start.13 = (bf16[128,512]{0,1:T(8,128)(2,1)S(1)}, bf16[128,512]{0,1:T(8,128)(2,1)S(1)}, u32[]{:S(2)}, u32[]{:S(2)}) collective-permute-start(bf16[128,512]{0,1:T(8,128)(2,1)S(1)} %fusion.6), channel_id=1, source_target_pairs={{0,1},{1,0},{2,3},{3,2},{4,5},{5,4},{6,7},{7,6},{8,9},{9,8},{10,11... | collective-permute-start | bytes 393224 | tf_op jit(solution)/shard_map/ppermute | solution.py:41
  (6 other events, 10.4 us)
Sparse Core Ops, SparseCore 0:
  11.9 89.3 all-gather.1
  201.2 43.4 reduce-scatter.1
